TPU v7x, 256 devices: a whole 4x4x8 slice. The times are simulated.
256 devices in a mesh: seq: 16 (over z_lo, y), head: 16 (over x, z_hi, core).
Axes of the slice: x: 4, y: 4, z: 8 (z_hi: 2, z_lo: 4; z = z_hi * 4 + z_lo), core: 2. Of those that a mesh axis runs over, the one named last changes fastest.
Arguments:
- query: bfloat16 [16384, 2048], P(('seq', 'head')), may hold values from -6 to 6
- key: bfloat16 [16384, 2048], P(('seq', 'head')), may hold values from -6 to 6
- value: bfloat16 [16384, 2048], P(('seq', 'head')), may hold values from -6 to 6
- output: bfloat16 [16384, 2048], P(('seq', 'head')), may hold values from -6 to 6
- grad_out: bfloat16 [16384, 2048], P(('seq', 'head')), may hold values from -6 to 6
- logsumexp: float32 [16, 16384], P('head', 'seq'), may hold values from 3.5 to 8.5, as said below
- rand_blocks: int32 [256, 3], replicated, may hold values from 0 to 255, as said below
Outputs:
- grad_query: bfloat16 [16384, 2048], P(('seq', 'head'))
- grad_key: bfloat16 [16384, 2048], P(('seq', 'head'))
- grad_value: bfloat16 [16384, 2048], P(('seq', 'head'))
Inputs may be any that keep to these rules, and one draw needn't show every extreme that they name: `rand_blocks`: each row names 3 different blocks, none below 2 and none within one block of the row's own block. In aligned runs of 16 rows, exactly 3 of the run's entries fall in each aligned run of 16 key blocks. `logsumexp`: rows of the first 2 blocks lie between 7 and 8.5, all others between 3.5 and 5.
All inputs are finite; a program needn't handle non-finite values.
Results may differ from a plain program's by a relative error of at most 0.02.
Values may be sent and summed in bfloat16 or wider, within the bound.
No kernel may reach another device: no remote copies, remote signals or barrier semaphores. Data moves between devices by JAX's collectives and lax.ppermute only.
A program may use at most 64 MiB of HBM per device.

v0:
```python
import jax
import jax.numpy as jnp
from jax import lax
from jax.sharding import PartitionSpec as P

HEADS = 16
HD = 128
BLK = 64
GLOB = 2
RAND = 3


def spread(value, axis, source):
    kept = jnp.where(lax.axis_index(axis) == source, value, 0).astype(value.dtype)
    return lax.psum(kept, axis)


def passed_along(value, axis, steps):
    count = lax.axis_size(axis)
    initial, last = (max(0, -steps), min(count, count - steps))
    return lax.ppermute(value, axis, [(source, source + steps) for source in range(initial, last)])


def block_grads(queries, grad_rows, log_norm, deltas, keys, values, usable, factor):
    scores = (
        jnp.einsum("...md,...nd->...mn", queries, keys, preferred_element_type=jnp.float32) * factor
    )
    weights = jnp.where(usable, jnp.exp(scores - log_norm[..., None]), 0.0)
    weights_low = weights.astype(jnp.bfloat16)
    grad_values = jnp.einsum(
        "...mn,...md->...nd", weights_low, grad_rows, preferred_element_type=jnp.float32
    )
    grad_probs = jnp.einsum(
        "...md,...nd->...mn", grad_rows, values, preferred_element_type=jnp.float32
    )
    grad_scores = (weights * (grad_probs - deltas[..., None])).astype(jnp.bfloat16)
    grad_queries = (
        jnp.einsum("...mn,...nd->...md", grad_scores, keys, preferred_element_type=jnp.float32)
        * factor
    )
    grad_keys = (
        jnp.einsum("...mn,...md->...nd", grad_scores, queries, preferred_element_type=jnp.float32)
        * factor
    )
    return (grad_queries, grad_keys, grad_values)


def slide_blocks(stack, offset):
    if offset == 0:
        return stack
    blank = jnp.zeros_like(stack[:, :1])
    if offset > 0:
        return jnp.concatenate([stack[:, 1:], blank], axis=1)
    return jnp.concatenate([blank, stack[:, :-1]], axis=1)


def slot_order(rand_blocks, group_id, blocks_here):
    pattern_rows = lax.dynamic_slice_in_dim(rand_blocks, group_id * blocks_here, blocks_here, 0)
    entries = pattern_rows.reshape(-1)
    ranking = jnp.argsort(entries // blocks_here, stable=True)
    slot_query = ranking // rand_blocks.shape[1]
    slot_key = entries[ranking] % blocks_here
    return (slot_query, slot_key)


def per_device(query, key, value, output, grad_out, logsumexp, rand_blocks):
    tok_rows = query.shape[0]
    heads_here = logsumexp.shape[0]
    seq_rows = logsumexp.shape[1]
    blocks_here = seq_rows // BLK
    groups = lax.axis_size("seq")
    position = lax.axis_index("seq")
    per_group = RAND * blocks_here // groups
    glob_rows = GLOB * BLK
    factor = HD ** (-0.5)

    def to_heads(matrix):
        return matrix.reshape(tok_rows, HEADS, HD).transpose(1, 0, 2)

    query_rows, key_rows, value_rows, out_rows, grad_rows = (
        lax.all_to_all(to_heads(query), "head", split_axis=0, concat_axis=1, tiled=True),
        lax.all_to_all(to_heads(key), "head", split_axis=0, concat_axis=1, tiled=True),
        lax.all_to_all(to_heads(value), "head", split_axis=0, concat_axis=1, tiled=True),
        lax.all_to_all(to_heads(output), "head", split_axis=0, concat_axis=1, tiled=True),
        lax.all_to_all(to_heads(grad_out), "head", split_axis=0, concat_axis=1, tiled=True),
    )
    deltas = jnp.sum(grad_rows.astype(jnp.float32) * out_rows.astype(jnp.float32), axis=-1)

    def as_blocks(stack):
        return stack.reshape((heads_here, blocks_here, BLK) + stack.shape[2:])

    query_blk = as_blocks(query_rows)
    key_blk = as_blocks(key_rows)
    value_blk = as_blocks(value_rows)
    grad_blk = as_blocks(grad_rows)
    norm_blk = as_blocks(logsumexp)
    delta_blk = as_blocks(deltas)
    block_ids = jnp.arange(blocks_here, dtype=jnp.int32)
    first_id = position * blocks_here
    query_alive = first_id + block_ids >= GLOB
    grad_query = jnp.zeros((heads_here, blocks_here, BLK, HD), jnp.float32)
    grad_key_home = jnp.zeros_like(grad_query)
    grad_value_home = jnp.zeros_like(grad_query)
    for offset in (-1, 0, 1):
        target = block_ids + offset
        usable = query_alive & (target >= 0) & (target < blocks_here) & (first_id + target >= GLOB)
        part_q, part_k, part_v = block_grads(
            query_blk,
            grad_blk,
            norm_blk,
            delta_blk,
            slide_blocks(key_blk, offset),
            slide_blocks(value_blk, offset),
            usable[None, :, None, None],
            factor,
        )
        grad_query = grad_query + part_q
        grad_key_home = grad_key_home + slide_blocks(part_k, -offset)
        grad_value_home = grad_value_home + slide_blocks(part_v, -offset)
    row_alive = jnp.repeat(query_alive, BLK)
    at_home = (position == 0).astype(jnp.float32)
    glob_key, glob_value, glob_query, glob_grad = (
        spread(key_rows[:, :glob_rows], "seq", 0),
        spread(value_rows[:, :glob_rows], "seq", 0),
        spread(query_rows[:, :glob_rows], "seq", 0),
        spread(grad_rows[:, :glob_rows], "seq", 0),
    )
    glob_norm, glob_delta = (
        spread(logsumexp[:, :glob_rows], "seq", 0),
        spread(deltas[:, :glob_rows], "seq", 0),
    )
    key_part_q, key_part_k, key_part_v = block_grads(
        query_rows,
        grad_rows,
        logsumexp,
        deltas,
        glob_key,
        glob_value,
        row_alive[None, :, None],
        factor,
    )
    grad_query = grad_query + as_blocks(key_part_q)
    spread_q, spread_k, spread_v = block_grads(
        glob_query, glob_grad, glob_norm, glob_delta, key_rows, value_rows, True, factor
    )
    grad_key_home = grad_key_home + as_blocks(spread_k)
    grad_value_home = grad_value_home + as_blocks(spread_v)
    totals_k, totals_v, totals_q = (
        lax.psum(key_part_k.astype(jnp.bfloat16), "seq").astype(jnp.float32),
        lax.psum(key_part_v.astype(jnp.bfloat16), "seq").astype(jnp.float32),
        lax.psum(spread_q.astype(jnp.bfloat16), "seq").astype(jnp.float32),
    )
    grad_query = grad_query.at[:, :GLOB].add(at_home * totals_q.reshape(heads_here, GLOB, BLK, HD))
    grad_key_home = grad_key_home.at[:, :GLOB].add(
        at_home * totals_k.reshape(heads_here, GLOB, BLK, HD)
    )
    grad_value_home = grad_value_home.at[:, :GLOB].add(
        at_home * totals_v.reshape(heads_here, GLOB, BLK, HD)
    )
    slot_q = slot_order(rand_blocks, position, blocks_here)[0]

    def wanted(anchor):
        return slot_order(rand_blocks, anchor, blocks_here)[1]

    all_wanted = jax.vmap(wanted)(jnp.arange(groups, dtype=jnp.int32))
    send_ids = lax.dynamic_slice_in_dim(all_wanted, position * per_group, per_group, 1).reshape(-1)
    far_key, far_value = (
        lax.all_to_all(key_blk[:, send_ids], "seq", split_axis=1, concat_axis=1, tiled=True),
        lax.all_to_all(value_blk[:, send_ids], "seq", split_axis=1, concat_axis=1, tiled=True),
    )
    usable = first_id + slot_q >= GLOB
    part_q, part_k, part_v = block_grads(
        query_blk[:, slot_q],
        grad_blk[:, slot_q],
        norm_blk[:, slot_q],
        delta_blk[:, slot_q],
        far_key,
        far_value,
        usable[None, :, None, None],
        factor,
    )
    grad_query = grad_query.at[:, slot_q].add(part_q)
    back_key, back_value = (
        lax.all_to_all(part_k, "seq", split_axis=1, concat_axis=1, tiled=True),
        lax.all_to_all(part_v, "seq", split_axis=1, concat_axis=1, tiled=True),
    )
    grad_key_home = grad_key_home.at[:, send_ids].add(back_key)
    grad_value_home = grad_value_home.at[:, send_ids].add(back_value)
    left_key, left_value = passed_along((key_blk[:, -1:], value_blk[:, -1:]), "seq", 1)
    right_key, right_value = passed_along((key_blk[:, :1], value_blk[:, :1]), "seq", -1)
    left_ok = (position >= 1) & (first_id - 1 >= GLOB)
    right_ok = (position <= groups - 2) & (first_id + blocks_here - 1 >= GLOB)
    left_q, left_k, left_v = block_grads(
        query_blk[:, :1],
        grad_blk[:, :1],
        norm_blk[:, :1],
        delta_blk[:, :1],
        left_key,
        left_value,
        left_ok,
        factor,
    )
    right_q, right_k, right_v = block_grads(
        query_blk[:, -1:],
        grad_blk[:, -1:],
        norm_blk[:, -1:],
        delta_blk[:, -1:],
        right_key,
        right_value,
        right_ok,
        factor,
    )
    grad_query = grad_query.at[:, :1].add(left_q)
    grad_query = grad_query.at[:, -1:].add(right_q)
    from_right_k, from_right_v = (
        passed_along(left_k.astype(jnp.bfloat16), "seq", -1).astype(left_k.dtype),
        passed_along(left_v.astype(jnp.bfloat16), "seq", -1).astype(left_v.dtype),
    )
    from_left_k, from_left_v = (
        passed_along(right_k.astype(jnp.bfloat16), "seq", 1).astype(right_k.dtype),
        passed_along(right_v.astype(jnp.bfloat16), "seq", 1).astype(right_v.dtype),
    )
    grad_key_home = grad_key_home.at[:, -1:].add(from_right_k)
    grad_value_home = grad_value_home.at[:, -1:].add(from_right_v)
    grad_key_home = grad_key_home.at[:, :1].add(from_left_k)
    grad_value_home = grad_value_home.at[:, :1].add(from_left_v)

    def to_rows(stack):
        return stack.astype(jnp.bfloat16).reshape(heads_here, seq_rows, HD)

    back_q, back_k, back_v = (
        lax.all_to_all(to_rows(grad_query), "head", split_axis=1, concat_axis=0, tiled=True),
        lax.all_to_all(to_rows(grad_key_home), "head", split_axis=1, concat_axis=0, tiled=True),
        lax.all_to_all(to_rows(grad_value_home), "head", split_axis=1, concat_axis=0, tiled=True),
    )

    def to_tokens(stack):
        return stack.transpose(1, 0, 2).reshape(tok_rows, HEADS * HD)

    return (to_tokens(back_q), to_tokens(back_k), to_tokens(back_v))


def solution(mesh):
    in_specs = (
        P(("seq", "head"), None),
        P(("seq", "head"), None),
        P(("seq", "head"), None),
        P(("seq", "head"), None),
        P(("seq", "head"), None),
        P("head", "seq"),
        P(),
    )
    out_specs = (P(("seq", "head"), None), P(("seq", "head"), None), P(("seq", "head"), None))
    return jax.shard_map(
        per_device, mesh=mesh, in_specs=in_specs, out_specs=out_specs, check_vma=False
    )
```

profile of v0, /device:TPU:32, one launch (start us, length us, event | category | flops | bytes accessed | tf_op | source)
XLA Modules:
  0.0 657.0 jit_solution(3117383005306899725)
XLA Ops:
  8.9 10.1 %all-to-all-start = ((bf16[16,64,128]{2,1,0:T(8,128)(2,1)}), bf16[16,64,128]{2,1,0:T(8,128)(2,1)S(1)}, u32[]{:S(2)}, u32[]{:S(2)}) async-start(bf16[16,64,128]{2,1,0:T(8,128)(2,1)} %bitcast_bitcast_fusion.4), calls=%async_computation | async-start | bytes 524288 | tf_op jit(solution)/shard_map/all_to_all | solution.py:82
  19.1 32.0 %while.10 = (s32[]{:T(128)}, s32[256,3]{0,1:T(4,128)}, s32[16,2]{0,1:T(2,128)S(1)}, s32[16,16,3]{1,2,0:T(4,128)S(1)}, s32[]{:T(128)}) while((s32[]{:T(128)}, s32[256,3]{0,1:T(4,128)}, s32[16,2]{0,1:T(2,128)S(1)}, s32[16,16,3]{1,2,0:T(4,128)S(1)}, s32[]{:T(128)}) %tuple.65), condition=%wide.while_cond.9, body=%wide.while_body.9.sunk | while | flops 2 | bytes 2345 | solution.py:58
  52.4 5.3 gather_fusion.6
  58.3 2.0 sort.34
  62.5 9.6 %all-to-all-start.2 = ((bf16[16,64,128]{2,1,0:T(8,128)(2,1)}), bf16[16,64,128]{2,1,0:T(8,128)(2,1)S(1)}, u32[]{:S(2)}, u32[]{:S(2)}) async-start(bf16[16,64,128]{2,1,0:T(8,128)(2,1)} %bitcast_bitcast_fusion.2), calls=%async_computation.2 | async-start | bytes 524288 | tf_op jit(solution)/shard_map/all_to_all | solution.py:83
  73.0 13.9 %all-to-all-done.2 = bf16[16,64,128]{2,1,0:T(8,128)(2,1)S(1)} async-done(((bf16[16,64,128]{2,1,0:T(8,128)(2,1)}), bf16[16,64,128]{2,1,0:T(8,128)(2,1)S(1)}, u32[]{:S(2)}, u32[]{:S(2)}) %all-to-all-start.2) | async-done | bytes 262176 | tf_op jit(solution)/shard_map/all_to_all | solution.py:83
  86.9 3.5 all-to-all-start.4
  92.5 10.8 %all-to-all-done.4 = bf16[16,64,128]{2,1,0:T(8,128)(2,1)S(1)} async-done(((bf16[16,64,128]{2,1,0:T(8,128)(2,1)}), bf16[16,64,128]{2,1,0:T(8,128)(2,1)S(1)}, u32[]{:S(2)}, u32[]{:S(2)}) %all-to-all-start.4) | async-done | bytes 262176 | tf_op jit(solution)/shard_map/all_to_all | solution.py:84
  103.3 3.5 all-to-all-start.3
  110.1 8.8 %all-to-all-done.3 = bf16[16,64,128]{2,1,0:T(8,128)(2,1)S(1)} async-done(((bf16[16,64,128]{2,1,0:T(8,128)(2,1)}), bf16[16,64,128]{2,1,0:T(8,128)(2,1)S(1)}, u32[]{:S(2)}, u32[]{:S(2)}) %all-to-all-start.3) | async-done | bytes 262176 | tf_op jit(solution)/shard_map/all_to_all | solution.py:85
  118.9 3.5 all-to-all-start.1
  124.9 9.5 %all-to-all-done.1 = bf16[16,64,128]{2,1,0:T(8,128)(2,1)S(1)} async-done(((bf16[16,64,128]{2,1,0:T(8,128)(2,1)}), bf16[16,64,128]{2,1,0:T(8,128)(2,1)S(1)}, u32[]{:S(2)}, u32[]{:S(2)}) %all-to-all-start.1) | async-done | bytes 262176 | tf_op jit(solution)/shard_map/all_to_all | solution.py:81
  135.6 1.9 collective-permute-start.2
  137.5 3.9 collective-permute-start
  142.1 4.0 collective-permute-start.3
  146.1 1.9 collective-permute-start.1
  151.5 1.6 gather_fusion.1
  153.1 10.3 %all-to-all-start.5 = ((bf16[1,48,64,128]{3,2,0,1:T(8,128)(2,1)}), bf16[1,48,64,128]{3,2,0,1:T(8,128)(2,1)S(1)}, u32[]{:S(2)}, u32[]{:S(2)}) async-start(bf16[1,48,64,128]{3,2,0,1:T(8,128)(2,1)} %bitcast.32), calls=%async_computation.5 | async-start | bytes 1572864 | tf_op jit(solution)/shard_map/all_to_all | solution.py:168
  167.8 1.6 gather_fusion
  169.4 1.6 gather_fusion.4
  170.9 36.6 %all-reduce.9 = (f32[128]{0:T(128)}, f32[128]{0:T(128)S(1)}) all-reduce(f32[128]{0:T(128)S(1)} %copy-done.53, f32[128]{0:T(128)S(1)} %copy-done.54), channel_id=1, replica_groups=mesh['seq'=16,'head'=16] {'seq'}, use_global_device_ids=true, to_apply=%region_4.5 | all-reduce | flops 256 | bytes 2048 | tf_op jit(solution)/shard_map/psum | solution.py:15
  208.1 110.0 %all-reduce.17.cloned.1.call-done = (bf16[128,128]{1,0:T(8,128)(2,1)}, bf16[128,128]{1,0:T(8,128)(2,1)}, bf16[128,128]{1,0:T(8,128)(2,1)}, bf16[128,128]{1,0:T(8,128)(2,1)}) async-done(((bf16[128,128]{1,0:T(8,128)(2,1)}, bf16[128,128]{1,0:T(8,128)(2,1)}, bf16[128,128]{1,0:T(8,128)(2,1)}, bf16[128,128]{1,0:T(8,128)(2,1)}), (bf16[128,128]{1,0:T(8,128)(2,1)}, bf16[128,128]{1,0:T(8,128)(2,1)}, ...) | async-done | bytes 131088 | tf_op jit(solution)/shard_map/psum | solution.py:15
  323.1 12.9 %all-to-all-start.6 = ((bf16[1,48,64,128]{3,2,0,1:T(8,128)(2,1)}), bf16[1,48,64,128]{3,2,0,1:T(8,128)(2,1)}, u32[]{:S(2)}, u32[]{:S(2)}) async-start(bf16[1,48,64,128]{3,2,0,1:T(8,128)(2,1)} %bitcast.35), calls=%async_computation.6 | async-start | bytes 1572864 | tf_op jit(solution)/shard_map/all_to_all | solution.py:169
  340.6 148.5 %all-reduce.15.cloned.1.call-done = (bf16[1,128,128]{2,1,0:T(8,128)(2,1)}, bf16[1,128,128]{2,1,0:T(8,128)(2,1)}, bf16[1,128,128]{2,1,0:T(8,128)(2,1)}) async-done(((bf16[1,128,128]{2,1,0:T(8,128)(2,1)}, bf16[1,128,128]{2,1,0:T(8,128)(2,1)}, bf16[1,128,128]{2,1,0:T(8,128)(2,1)}), (bf16[1,128,128]{2,1,0:T(8,128)(2,1)}, bf16[1,128,128]{2,1,0:T(8,128)(2,1)}, ...) | async-done | bytes 98320 | tf_op jit(solution)/shard_map/psum | solution.py:151
  489.8 2.9 exponential_select_fusion
  492.8 2.3 multiply_convert_fusion
  495.0 1.5 convolution_multiply_fusion
  496.6 5.4 scatter_fusion
  503.2 2.1 reduce.25
  506.1 9.3 %all-to-all-start.7 = ((bf16[16,2,4096]{2,1,0:T(2,128)(2,1)}), bf16[16,2,4096]{2,1,0:T(2,128)(2,1)S(1)}, u32[]{:S(2)}, u32[]{:S(2)}) async-start(bf16[16,2,4096]{2,1,0:T(2,128)(2,1)} %reshape.1100), calls=%async_computation.7 | async-start | bytes 524288 | tf_op jit(solution)/shard_map/all_to_all | solution.py:232
  515.4 3.0 convolution_bitcast_fusion
  518.4 11.8 %all-to-all-done.7 = bf16[16,2,4096]{2,1,0:T(2,128)(2,1)S(1)} async-done(((bf16[16,2,4096]{2,1,0:T(2,128)(2,1)}), bf16[16,2,4096]{2,1,0:T(2,128)(2,1)S(1)}, u32[]{:S(2)}, u32[]{:S(2)}) %all-to-all-start.7) | async-done | bytes 262176 | tf_op jit(solution)/shard_map/all_to_all | solution.py:232
  530.2 4.3 all-to-all-start.10
  534.5 1.6 multiply_bitcast_fusion
  536.1 35.0 %all-to-all-done.10 = f32[1,48,64,128]{3,2,0,1:T(8,128)} async-done(((f32[1,48,64,128]{3,2,0,1:T(8,128)}), f32[1,48,64,128]{3,2,0,1:T(8,128)}, u32[]{:S(2)}, u32[]{:S(2)}) %all-to-all-start.10) | async-done | bytes 1572896 | tf_op jit(solution)/shard_map/all_to_all | solution.py:185
  571.1 5.4 all-to-all-start.8
  579.4 3.5 collective-permute-start.5
  583.0 4.6 collective-permute-start.4
  588.4 2.5 collective-permute-start.6
  591.7 3.4 collective-permute-start.7
  601.0 5.4 scatter_fusion.2
  608.3 2.1 reduce.27
  612.3 4.1 all-to-all-start.11
  617.3 2.9 scatter_fusion.1
  621.4 2.1 reduce.26
  624.3 6.9 %all-to-all-done.11 = bf16[16,2,4096]{2,1,0:T(2,128)(2,1)S(1)} async-done(((bf16[16,2,4096]{2,1,0:T(2,128)(2,1)}), bf16[16,2,4096]{2,1,0:T(2,128)(2,1)S(1)}, u32[]{:S(2)}, u32[]{:S(2)}) %all-to-all-start.11) | async-done | bytes 262176 | tf_op jit(solution)/shard_map/all_to_all | solution.py:234
  631.2 3.5 all-to-all-start.9
  636.9 12.2 %all-to-all-done.9 = bf16[16,2,4096]{2,1,0:T(2,128)(2,1)S(1)} async-done(((bf16[16,2,4096]{2,1,0:T(2,128)(2,1)}), bf16[16,2,4096]{2,1,0:T(2,128)(2,1)S(1)}, u32[]{:S(2)}, u32[]{:S(2)}) %all-to-all-start.9) | async-done | bytes 262176 | tf_op jit(solution)/shard_map/all_to_all | solution.py:233
  (309 shorter events, 88.4 us)
Async XLA Ops:
  8.9 53.6 %all-to-all-start = ((bf16[16,64,128]{2,1,0:T(8,128)(2,1)}), bf16[16,64,128]{2,1,0:T(8,128)(2,1)S(1)}, u32[]{:S(2)}, u32[]{:S(2)}) async-start(bf16[16,64,128]{2,1,0:T(8,128)(2,1)} %bitcast_bitcast_fusion.4), calls=%async_computation | async-start | bytes 524288 | tf_op jit(solution)/shard_map/all_to_all | solution.py:82
  52.4 8.8 %copy-start.39 = (f32[1,1024]{1,0:T(1,128)S(1)}, f32[1,1024]{1,0:T(1,128)}, u32[]{:S(2)}) copy-start(f32[1,1024]{1,0:T(1,128)} %param.30) | copy-start | bytes 12292
  52.4 9.3 %copy-start.27 = (bf16[64,2048]{1,0:T(8,128)(2,1)S(1)}, bf16[64,2048]{1,0:T(8,128)(2,1)}, u32[]{:S(2)}) copy-start(bf16[64,2048]{1,0:T(8,128)(2,1)} %param.27) | copy-start | bytes 786436
  52.4 19.8 %copy-start.28 = (bf16[64,2048]{1,0:T(8,128)(2,1)S(1)}, bf16[64,2048]{1,0:T(8,128)(2,1)}, u32[]{:S(2)}) copy-start(bf16[64,2048]{1,0:T(8,128)(2,1)} %param.28) | copy-start | bytes 786436
  57.7 33.2 %copy-start.29 = (bf16[64,2048]{1,0:T(8,128)(2,1)S(1)}, bf16[64,2048]{1,0:T(8,128)(2,1)}, u32[]{:S(2)}) copy-start(bf16[64,2048]{1,0:T(8,128)(2,1)} %param.25) | copy-start | bytes 786436
  57.8 34.0 %copy-start.30 = (bf16[64,2048]{1,0:T(8,128)(2,1)S(1)}, bf16[64,2048]{1,0:T(8,128)(2,1)}, u32[]{:S(2)}) copy-start(bf16[64,2048]{1,0:T(8,128)(2,1)} %param.29) | copy-start | bytes 786436
  60.9 31.6 %copy-start.49 = (s32[48]{0:T(128)}, s32[48]{0:T(128)S(1)}, u32[]{:S(2)}) copy-start(s32[48]{0:T(128)S(1)} %compare_select_fusion.3) | copy-start | bytes 580
  61.1 11.0 %copy-start.46 = (s32[48]{0:T(128)}, s32[48]{0:T(128)S(1)}, u32[]{:S(2)}) copy-start(s32[48]{0:T(128)S(1)} %fusion.115) | copy-start | bytes 580
  62.5 24.4 %all-to-all-start.2 = ((bf16[16,64,128]{2,1,0:T(8,128)(2,1)}), bf16[16,64,128]{2,1,0:T(8,128)(2,1)S(1)}, u32[]{:S(2)}, u32[]{:S(2)}) async-start(bf16[16,64,128]{2,1,0:T(8,128)(2,1)} %bitcast_bitcast_fusion.2), calls=%async_computation.2 | async-start | bytes 524288 | tf_op jit(solution)/shard_map/all_to_all | solution.py:83
  86.9 16.5 %all-to-all-start.4 = ((bf16[16,64,128]{2,1,0:T(8,128)(2,1)}), bf16[16,64,128]{2,1,0:T(8,128)(2,1)S(1)}, u32[]{:S(2)}, u32[]{:S(2)}) async-start(bf16[16,64,128]{2,1,0:T(8,128)(2,1)} %bitcast_bitcast_fusion), calls=%async_computation.4 | async-start | bytes 524288 | tf_op jit(solution)/shard_map/all_to_all | solution.py:84
  103.3 15.6 %all-to-all-start.3 = ((bf16[16,64,128]{2,1,0:T(8,128)(2,1)}), bf16[16,64,128]{2,1,0:T(8,128)(2,1)S(1)}, u32[]{:S(2)}, u32[]{:S(2)}) async-start(bf16[16,64,128]{2,1,0:T(8,128)(2,1)} %bitcast_bitcast_fusion.1), calls=%async_computation.3 | async-start | bytes 524288 | tf_op jit(solution)/shard_map/all_to_all | solution.py:85
  118.9 15.5 %all-to-all-start.1 = ((bf16[16,64,128]{2,1,0:T(8,128)(2,1)}), bf16[16,64,128]{2,1,0:T(8,128)(2,1)S(1)}, u32[]{:S(2)}, u32[]{:S(2)}) async-start(bf16[16,64,128]{2,1,0:T(8,128)(2,1)} %bitcast_bitcast_fusion.3), calls=%async_computation.1 | async-start | bytes 524288 | tf_op jit(solution)/shard_map/all_to_all | solution.py:81
  135.6 71.9 %collective-permute-start.2 = (bf16[1,1,64,128]{3,2,1,0:T(8,128)(2,1)S(1)}, bf16[1,1,64,128]{3,2,1,0:T(8,128)(2,1)S(1)}, u32[]{:S(2)}, u32[]{:S(2)}) collective-permute-start(bf16[1,1,64,128]{3,2,1,0:T(8,128)(2,1)S(1)} %get-tuple-element.144), channel_id=1, source_target_pairs={{16,0},{32,16},{48,32},{64,48},{80,64},{96,80},{112,96},{128,112},... | collective-permute-start | bytes 49160 | tf_op jit(solution)/shard_map/ppermute | solution.py:21
  137.5 70.2 %collective-permute-start = (bf16[1,1,64,128]{3,2,1,0:T(8,128)(2,1)S(1)}, bf16[1,1,64,128]{3,2,1,0:T(8,128)(2,1)S(1)}, u32[]{:S(2)}, u32[]{:S(2)}) collective-permute-start(bf16[1,1,64,128]{3,2,1,0:T(8,128)(2,1)S(1)} %get-tuple-element.145), channel_id=1, source_target_pairs={{0,16},{16,32},{32,48},{48,64},{64,80},{80,96},{96,112},{112,128},... | collective-permute-start | bytes 49160 | tf_op jit(solution)/shard_map/ppermute | solution.py:21
  142.1 65.6 %collective-permute-start.3 = (bf16[1,1,64,128]{3,2,1,0:T(8,128)(2,1)S(1)}, bf16[1,1,64,128]{3,2,1,0:T(8,128)(2,1)S(1)}, u32[]{:S(2)}, u32[]{:S(2)}) collective-permute-start(bf16[1,1,64,128]{3,2,1,0:T(8,128)(2,1)S(1)} %get-tuple-element.142), channel_id=1, source_target_pairs={{16,0},{32,16},{48,32},{64,48},{80,64},{96,80},{112,96},{128,112},... | collective-permute-start | bytes 49160 | tf_op jit(solution)/shard_map/ppermute | solution.py:21
  146.1 61.9 %collective-permute-start.1 = (bf16[1,1,64,128]{3,2,1,0:T(8,128)(2,1)S(1)}, bf16[1,1,64,128]{3,2,1,0:T(8,128)(2,1)S(1)}, u32[]{:S(2)}, u32[]{:S(2)}) collective-permute-start(bf16[1,1,64,128]{3,2,1,0:T(8,128)(2,1)S(1)} %get-tuple-element.143), channel_id=1, source_target_pairs={{0,16},{16,32},{32,48},{48,64},{64,80},{80,96},{96,112},{112,128},... | collective-permute-start | bytes 49160 | tf_op jit(solution)/shard_map/ppermute | solution.py:21
  151.5 12.7 %copy-start.55 = (pred[16]{0:T(512)(128)(4,1)S(1)}, pred[16]{0:T(512)(128)(4,1)}, u32[]{:S(2)}) copy-start(pred[16]{0:T(512)(128)(4,1)} %and_and_fusion) | copy-start | bytes 52
  153.1 170.0 %all-to-all-start.5 = ((bf16[1,48,64,128]{3,2,0,1:T(8,128)(2,1)}), bf16[1,48,64,128]{3,2,0,1:T(8,128)(2,1)S(1)}, u32[]{:S(2)}, u32[]{:S(2)}) async-start(bf16[1,48,64,128]{3,2,0,1:T(8,128)(2,1)} %bitcast.32), calls=%async_computation.5 | async-start | bytes 1572864 | tf_op jit(solution)/shard_map/all_to_all | solution.py:168
  163.4 154.7 %all-reduce.17.cloned.1.call-start = ((), (), s32[]{:S(2)}) async-start(), calls=%async_computation.13 | async-start | bytes 262144 | tf_op jit(solution)/shard_map/psum | solution.py:15
  169.4 148.7 %copy-start.48 = (pred[1024]{0:T(1024)(128)(4,1)S(1)}, pred[1024]{0:T(1024)(128)(4,1)}, u32[]{:S(2)}) copy-start(pred[1024]{0:T(1024)(128)(4,1)} %broadcast_in_dim.110) | copy-start | bytes 3076
  207.7 110.4 %copy-start.34 = (f32[64,64]{1,0:T(8,128)}, f32[64,64]{1,0:T(8,128)S(1)}, u32[]{:S(2)}) copy-start(f32[64,64]{1,0:T(8,128)S(1)} %fusion.41) | copy-start | bytes 49156
  207.8 113.5 %copy-start.44 = (bf16[1,1,64,128]{3,2,1,0:T(8,128)(2,1)}, bf16[1,1,64,128]{3,2,1,0:T(8,128)(2,1)S(1)}, u32[]{:S(2)}) copy-start(bf16[1,1,64,128]{3,2,1,0:T(8,128)(2,1)S(1)} %collective-permute-done) | copy-start | bytes 49156
  208.0 110.1 %copy-start.36 = (f32[64,64]{1,0:T(8,128)}, f32[64,64]{1,0:T(8,128)S(1)}, u32[]{:S(2)}) copy-start(f32[64,64]{1,0:T(8,128)S(1)} %fusion.46) | copy-start | bytes 49156
  323.1 13.1 %copy-start.10 = (bf16[128,1024]{1,0:T(8,128)(2,1)S(1)}, bf16[128,1024]{1,0:T(8,128)(2,1)}, u32[]{:S(2)}) copy-start(bf16[128,1024]{1,0:T(8,128)(2,1)} %fusion.30) | copy-start | bytes 786436
  323.1 14.8 %copy-start.33 = (bf16[128,128]{1,0:T(8,128)(2,1)S(1)}, bf16[128,128]{1,0:T(8,128)(2,1)}, u32[]{:S(2)}) copy-start(bf16[128,128]{1,0:T(8,128)(2,1)} %get-tuple-element.136) | copy-start | bytes 98308
  323.1 14.8 %copy-start.5 = (bf16[1,48,64,128]{3,2,0,1:T(8,128)(2,1)}, bf16[1,48,64,128]{3,2,0,1:T(8,128)(2,1)S(1)}, u32[]{:S(2)}) copy-start(bf16[1,48,64,128]{3,2,0,1:T(8,128)(2,1)S(1)} %all-to-all-done.5) | copy-start | bytes 2359300
  323.1 169.7 %all-to-all-start.6 = ((bf16[1,48,64,128]{3,2,0,1:T(8,128)(2,1)}), bf16[1,48,64,128]{3,2,0,1:T(8,128)(2,1)}, u32[]{:S(2)}, u32[]{:S(2)}) async-start(bf16[1,48,64,128]{3,2,0,1:T(8,128)(2,1)} %bitcast.35), calls=%async_computation.6 | async-start | bytes 1572864 | tf_op jit(solution)/shard_map/all_to_all | solution.py:169
  336.0 153.1 %all-reduce.15.cloned.1.call-start = ((), (), s32[]{:S(2)}) async-start(), calls=%async_computation.12 | async-start | bytes 196608 | tf_op jit(solution)/shard_map/psum | solution.py:151
  337.9 151.9 %copy-start.3 = (bf16[48,64,128]{2,1,0:T(8,128)(2,1)S(1)}, bf16[48,64,128]{2,1,0:T(8,128)(2,1)}, u32[]{:S(2)}) copy-start(bf16[48,64,128]{2,1,0:T(8,128)(2,1)} %gather_fusion) | copy-start | bytes 2359300
  337.9 151.9 %copy-start.51 = (pred[48]{0:T(512)(128)(4,1)S(1)}, pred[48]{0:T(512)(128)(4,1)}, u32[]{:S(2)}) copy-start(pred[48]{0:T(512)(128)(4,1)} %get-tuple-element.140) | copy-start | bytes 148
  339.2 150.6 %copy-start.43 = (f32[48,64]{1,0:T(8,128)S(1)}, f32[48,64]{1,0:T(8,128)}, u32[]{:S(2)}) copy-start(f32[48,64]{1,0:T(8,128)} %gather_fusion.2) | copy-start | bytes 36868
  506.1 24.0 %all-to-all-start.7 = ((bf16[16,2,4096]{2,1,0:T(2,128)(2,1)}), bf16[16,2,4096]{2,1,0:T(2,128)(2,1)S(1)}, u32[]{:S(2)}, u32[]{:S(2)}) async-start(bf16[16,2,4096]{2,1,0:T(2,128)(2,1)} %reshape.1100), calls=%async_computation.7 | async-start | bytes 524288 | tf_op jit(solution)/shard_map/all_to_all | solution.py:232
  518.4 16.1 %copy-start.4 = (bf16[48,64,128]{2,1,0:T(8,128)(2,1)S(1)}, bf16[48,64,128]{2,1,0:T(8,128)(2,1)}, u32[]{:S(2)}) copy-start(bf16[48,64,128]{2,1,0:T(8,128)(2,1)} %gather_fusion) | copy-start | bytes 2359300
  530.2 40.9 %all-to-all-start.10 = ((f32[1,48,64,128]{3,2,0,1:T(8,128)}), f32[1,48,64,128]{3,2,0,1:T(8,128)}, u32[]{:S(2)}, u32[]{:S(2)}) async-start(f32[1,48,64,128]{3,2,0,1:T(8,128)} %convolution_bitcast_fusion), calls=%async_computation.10 | async-start | bytes 3145728 | tf_op jit(solution)/shard_map/all_to_all | solution.py:185
  536.1 40.4 %copy-start.20 = (f32[16,64,64]{2,1,0:T(8,128)S(1)}, f32[16,64,64]{2,1,0:T(8,128)}, u32[]{:S(2)}) copy-start(f32[16,64,64]{2,1,0:T(8,128)} %copy-done.19) | copy-start | bytes 786436
  571.1 41.2 %all-to-all-start.8 = ((f32[1,48,64,128]{3,2,0,1:T(8,128)}), f32[1,48,64,128]{3,2,0,1:T(8,128)S(1)}, u32[]{:S(2)}, u32[]{:S(2)}) async-start(f32[1,48,64,128]{3,2,0,1:T(8,128)} %multiply_bitcast_fusion), calls=%async_computation.8 | async-start | bytes 3145728 | tf_op jit(solution)/shard_map/all_to_all | solution.py:184
  578.9 9.5 %copy-start.23 = (f32[1,16,64,128]{3,2,1,0:T(8,128)}, f32[1,16,64,128]{3,2,1,0:T(8,128)S(1)}, u32[]{:S(2)}) copy-start(f32[1,16,64,128]{3,2,1,0:T(8,128)S(1)} %fusion.2) | copy-start | bytes 1572868
  578.9 8.7 %copy-start.37 = (f32[64,64]{1,0:T(8,128)S(1)}, f32[64,64]{1,0:T(8,128)}, u32[]{:S(2)}) copy-start(f32[64,64]{1,0:T(8,128)} %copy-done.36) | copy-start | bytes 49156
  578.9 12.0 %copy-start.35 = (f32[64,64]{1,0:T(8,128)S(1)}, f32[64,64]{1,0:T(8,128)}, u32[]{:S(2)}) copy-start(f32[64,64]{1,0:T(8,128)} %copy-done.34) | copy-start | bytes 49156
  578.9 16.1 %copy-start.2 = (f32[128,1024]{1,0:T(8,128)S(1)}, f32[128,1024]{1,0:T(8,128)}, u32[]{:S(2)}) copy-start(f32[128,1024]{1,0:T(8,128)} %copy-done.1) | copy-start | bytes 1572868
  579.2 11.7 %copy-start.24 = (f32[1,16,64,128]{3,2,1,0:T(8,128)}, f32[1,16,64,128]{3,2,1,0:T(8,128)S(1)}, u32[]{:S(2)}) copy-start(f32[1,16,64,128]{3,2,1,0:T(8,128)S(1)} %fusion) | copy-start | bytes 1572868
  579.2 18.0 %copy-start.22 = (f32[16,64,64]{2,1,0:T(8,128)S(1)}, f32[16,64,64]{2,1,0:T(8,128)}, u32[]{:S(2)}) copy-start(f32[16,64,64]{2,1,0:T(8,128)} %copy-done.21) | copy-start | bytes 786436
  579.4 41.6 %collective-permute-start.5 = (bf16[1,1,64,128]{3,2,1,0:T(8,128)(2,1)S(1)}, bf16[1,1,64,128]{3,2,1,0:T(8,128)(2,1)S(1)}, u32[]{:S(2)}, u32[]{:S(2)}) collective-permute-start(bf16[1,1,64,128]{3,2,1,0:T(8,128)(2,1)S(1)} %fusion.58), channel_id=1, source_target_pairs={{0,16},{16,32},{32,48},{48,64},{64,80},{80,96},{96,112},{112,128},... | collective-permute-start | bytes 49160 | tf_op jit(solution)/shard_map/ppermute | solution.py:21
  583.0 37.2 %collective-permute-start.4 = (bf16[1,1,64,128]{3,2,1,0:T(8,128)(2,1)S(1)}, bf16[1,1,64,128]{3,2,1,0:T(8,128)(2,1)}, u32[]{:S(2)}, u32[]{:S(2)}) collective-permute-start(bf16[1,1,64,128]{3,2,1,0:T(8,128)(2,1)S(1)} %fusion.59), channel_id=1, source_target_pairs={{16,0},{32,16},{48,32},{64,48},{80,64},{96,80},{112,96},{128,112},... | collective-permute-start | bytes 49160 | tf_op jit(solution)/shard_map/ppermute | solution.py:21
  588.4 18.0 %collective-permute-start.6 = (bf16[1,1,64,128]{3,2,1,0:T(8,128)(2,1)}, bf16[1,1,64,128]{3,2,1,0:T(8,128)(2,1)}, u32[]{:S(2)}, u32[]{:S(2)}) collective-permute-start(bf16[1,1,64,128]{3,2,1,0:T(8,128)(2,1)} %fusion.56), channel_id=1, source_target_pairs={{16,0},{32,16},{48,32},{64,48},{80,64},{96,80},{112,96},{128,112},... | collective-permute-start | bytes 49160 | tf_op jit(solution)/shard_map/ppermute | solution.py:21
  591.7 15.5 %collective-permute-start.7 = (bf16[1,1,64,128]{3,2,1,0:T(8,128)(2,1)}, bf16[1,1,64,128]{3,2,1,0:T(8,128)(2,1)}, u32[]{:S(2)}, u32[]{:S(2)}) collective-permute-start(bf16[1,1,64,128]{3,2,1,0:T(8,128)(2,1)} %fusion.57), channel_id=1, source_target_pairs={{0,16},{16,32},{32,48},{48,64},{64,80},{80,96},{96,112},{112,128},... | collective-permute-start | bytes 49160 | tf_op jit(solution)/shard_map/ppermute | solution.py:21
  612.3 18.9 %all-to-all-start.11 = ((bf16[16,2,4096]{2,1,0:T(2,128)(2,1)}), bf16[16,2,4096]{2,1,0:T(2,128)(2,1)S(1)}, u32[]{:S(2)}, u32[]{:S(2)}) async-start(bf16[16,2,4096]{2,1,0:T(2,128)(2,1)} %reshape.1104), calls=%async_computation.11 | async-start | bytes 524288 | tf_op jit(solution)/shard_map/all_to_all | solution.py:234
  631.2 17.9 %all-to-all-start.9 = ((bf16[16,2,4096]{2,1,0:T(2,128)(2,1)}), bf16[16,2,4096]{2,1,0:T(2,128)(2,1)S(1)}, u32[]{:S(2)}, u32[]{:S(2)}) async-start(bf16[16,2,4096]{2,1,0:T(2,128)(2,1)} %reshape.1102), calls=%async_computation.9 | async-start | bytes 524288 | tf_op jit(solution)/shard_map/all_to_all | solution.py:233
  (32 other events, 62.1 us)
Sparse Core Ops, SparseCore 0:
  167.7 150.3 all-reduce.16
  339.8 149.1 all-reduce.14
where the time goes:
time: 661 us; the launch traced here: 657 us
  waiting for transfers between devices  369 us (56%)
  starting transfers between devices  106 us (16%)
  local copies, waits for them, and re-layouts  67.5 us (10%)
  blocking collectives  36.6 us (6%)
  other arithmetic  33.5 us (5%)
  matrix products  28.9 us (4%)
  between operations  15.3 us (2%)
    psum x1, waiting for transfers between devices, per_device(): lax.psum(spread_q.astype(jnp.bfloat16), 'seq').astype(jnp.float32)  148 us
    psum x1, waiting for transfers between devices, spread(): return lax.psum(kept, axis)  110 us
    psum x1, blocking collectives, spread(): return lax.psum(kept, axis)  36.6 us
    all_to_all x1, waiting for transfers between devices, per_device(): lax.all_to_all(part_v, 'seq', split_axis=1, concat_axis=1, tiled=True)  35 us
    gather x48, local copies, waits for them, and re-layouts  32 us
    ppermute x8, starting transfers between devices, passed_along(): lax.ppermute(value, axis, [(source, source + steps) for source in range(i...  25.7 us
    all_to_all x1, waiting for transfers between devices, per_device(): lax.all_to_all(to_heads(value), 'head', split_axis=0, concat_axis=1, tile...  13.9 us
  transfers between devices with their start and end apart: 22, of which 11 were waited for; matrix products, arithmetic and copies ran while one was open for 16% of the time, Pallas kernels for 0%

commit v1 on v0

v1 whole, which is shorter than its diff:
```python
import jax
import jax.numpy as jnp
from jax import lax
from jax.experimental import pallas as pl
from jax.experimental.pallas import tpu as pltpu
from jax.sharding import PartitionSpec as P

HEADS = 16
HD = 128
BLK = 64
GLOB = 2
RAND = 3
NB = 16
FACTOR = HD ** (-0.5)
OFF = 1e30
SLAB = 4 * BLK + 16
PAIR = RAND * 2 * BLK + 16
F32 = jnp.float32
BF16 = jnp.bfloat16

VM = pl.BlockSpec(memory_space=pltpu.VMEM)
SM = pl.BlockSpec(memory_space=pltpu.SMEM)


def call(body, outs, in_specs, flops=0, nbytes=0, scratch=(), aliases={}):
    return pl.pallas_call(
        body,
        out_shape=outs,
        in_specs=in_specs,
        out_specs=jax.tree.map(lambda _: VM, outs),
        scratch_shapes=list(scratch),
        input_output_aliases=aliases,
        compiler_params=pltpu.CompilerParams(vmem_limit_bytes=32 << 20),
        cost_estimate=pl.CostEstimate(flops=flops, bytes_accessed=nbytes, transcendentals=0),
    )


def nt(a, b):
    return lax.dot_general(a, b, (((1,), (1,)), ((), ())), preferred_element_type=F32)


def nn(a, b):
    return lax.dot_general(a, b, (((1,), (0,)), ((), ())), preferred_element_type=F32)


def tn(a, b):
    return lax.dot_general(a, b, (((0,), (0,)), ((), ())), preferred_element_type=F32)


def pieces(x):
    high = x.astype(BF16).astype(F32)
    return high, (x - high).astype(BF16).astype(F32)


def pack_body(q, k, v, o, g, out):
    lane = lax.broadcasted_iota(jnp.int32, (BLK, HD), 1)
    row = lax.broadcasted_iota(jnp.int32, (16, HD), 0)
    deltas = jnp.zeros((BLK, HD), F32)
    for h in range(HEADS):
        cols = pl.ds(h * HD, HD)
        gh = g[:, cols]
        out[h, 0:64] = q[:, cols]
        out[h, 64:128] = k[:, cols]
        out[h, 128:192] = v[:, cols]
        out[h, 192:256] = gh
        part = jnp.sum(gh.astype(F32) * o[:, cols].astype(F32), axis=1, keepdims=True)
        deltas = jnp.where(lane == h, part, deltas)
    turned = jnp.transpose(jnp.concatenate([deltas, jnp.zeros((BLK, HD), F32)], axis=0))
    high, low = pieces(turned)
    for h in range(HEADS):
        tile = jnp.where(row == 0, high[h : h + 1], jnp.where(row == 1, low[h : h + 1], 0.0))
        out[h, 256:272] = tile.astype(BF16)


def table_body(pos, entries, out):
    here = pos[0]
    e = entries[...]
    width = e.shape[1]
    lane = lax.broadcasted_iota(jnp.int32, (NB, width), 1)
    row = lax.broadcasted_iota(jnp.int32, (NB, width), 0)
    mine = jnp.sum(jnp.where(row == here, e, 0), axis=0, keepdims=True)
    to_group = jnp.broadcast_to(mine, (NB, width)) >> 4
    hit = jnp.concatenate(
        [jnp.where(to_group == row, 1.0, 0.0), jnp.where((e >> 4) == here, 1.0, 0.0)], axis=0
    )
    value = jnp.concatenate([(lane * 171) >> 9, e & 15], axis=0)
    ii = lax.broadcasted_iota(jnp.int32, (width, width), 0)
    jj = lax.broadcasted_iota(jnp.int32, (width, width), 1)
    before = jnp.where(ii < jj, 1.0, 0.0).astype(BF16)
    rank = nn(hit.astype(BF16), before)
    out_lane = lax.broadcasted_iota(jnp.int32, (2 * NB, HD), 1)
    result = jnp.zeros((2 * NB, HD), jnp.int32)
    for r in range(RAND):
        chosen = jnp.where((hit > 0.5) & (jnp.abs(rank - r) < 0.5), value, 0)
        total = jnp.sum(chosen, axis=1, keepdims=True)
        result = jnp.where(out_lane == r, total, result)
    out[...] = result


def norm_rows(lse, b):
    pair = lse[:, (b // 2) * HD : (b // 2 + 1) * HD]
    return pair[:, 64:128] if b % 2 else pair[:, 0:64]


def select_body(pos, table, x, lse, out, halo, glob, ext):
    row = lax.broadcasted_iota(jnp.int32, (16, BLK), 0)
    lse_all = lse[...]

    def ext_of(b, norm):
        high, low = pieces(norm)
        tile = jnp.where(row == 2, high, jnp.where(row == 3, low, 0.0))
        return x[b, 256:272, 0:64].astype(F32) + tile

    for b in range(NB):
        norm = norm_rows(lse_all, b)
        if b < GLOB:
            plain = ext_of(b, norm)
            glob[b, 0:256] = x[b, 0:256]
            glob[b, 256:272] = jnp.concatenate([plain, plain], axis=1).astype(BF16)
            norm = jnp.where(pos[0] == 0, OFF, norm)
        ext[b] = ext_of(b, norm)
        if b == NB - 1:
            halo[0:256] = x[b, 0:256]
            halo[256:272] = jnp.concatenate([ext[b], ext[b]], axis=1).astype(BF16)

    rows16 = lax.broadcasted_iota(jnp.int32, (16, BLK), 0)

    def step(t, carry):
        tile = jnp.zeros((16, BLK), F32)
        for r in range(RAND):
            b = table[t, r]
            out[t, r * 128 : r * 128 + 64] = x[b, 0:64]
            out[t, r * 128 + 64 : r * 128 + 128] = x[b, 192:256]
            part = ext[b]
            if r:
                part = pltpu.roll(part, 4 * r, 0)
            tile = tile + part
        out[t, 384:400] = jnp.concatenate([tile, tile], axis=1).astype(BF16)
        return carry

    lax.fori_loop(0, NB, step, 0)


def grads(q, g, norm, delta, k, v, keep=None):
    st = nt(k, q) * FACTOR
    pt = jnp.exp(st - norm)
    if keep is not None:
        pt = jnp.where(keep, pt, 0.0)
    dst = (pt * (nt(v, g) - delta)).astype(BF16)
    return tn(dst, k), nn(dst, q), nn(pt.astype(BF16), g)


def home_body(pos, x, lse, glob, halo, dq, dk, dv, gpart, hback):
    here = pos[0]
    lse_all = lse[...]
    lanes = lax.broadcasted_iota(jnp.int32, lse_all.shape, 1)
    lse_all = jnp.where((here == 0) & (lanes < GLOB * BLK), OFF, lse_all)

    def two(ext, a):
        return ext[a : a + 1].astype(F32) + ext[a + 1 : a + 2].astype(F32)

    def part(b, a):
        return x[b, a * 64 : (a + 1) * 64]

    def rows(b, a):
        return jnp.concatenate([part(b, a), part(b + 1, a)], axis=0)

    gq = jnp.concatenate([glob[0, 0:64], glob[1, 0:64]], axis=0)
    gk = jnp.concatenate([glob[0, 64:128], glob[1, 64:128]], axis=0)
    gv = jnp.concatenate([glob[0, 128:192], glob[1, 128:192]], axis=0)
    gg = jnp.concatenate([glob[0, 192:256], glob[1, 192:256]], axis=0)
    ext0 = glob[0, 256:272].astype(F32)
    ext1 = glob[1, 256:272].astype(F32)
    gdelta = jnp.concatenate([two(ext0, 0)[:, 0:64], two(ext1, 0)[:, 0:64]], axis=1)
    gnorm = jnp.concatenate([two(ext0, 2)[:, 0:64], two(ext1, 2)[:, 0:64]], axis=1)

    gq_sum = jnp.zeros((HD, HD), F32)
    gk_sum = jnp.zeros((HD, HD), F32)
    gv_sum = jnp.zeros((HD, HD), F32)
    for i in range(NB // 2):
        b = 2 * i
        fq, fk, fv = grads(gq, gg, gnorm, gdelta, rows(b, 1), rows(b, 2))
        gq_sum = gq_sum + fq
        dk[b * 64 : b * 64 + 128] = fk
        dv[b * 64 : b * 64 + 128] = fv
    for i in range(NB // 2):
        b = 2 * i
        q2, g2 = rows(b, 0), rows(b, 3)
        norm = lse_all[:, i * HD : (i + 1) * HD]
        e0 = x[b, 256:272].astype(F32)
        e1 = x[b + 1, 256:272].astype(F32)
        delta = jnp.concatenate([two(e0, 0)[:, 0:64], two(e1, 0)[:, 0:64]], axis=1)
        low, high = max(b - 1, 0), min(b + 3, NB)
        count = high - low
        keys = jnp.concatenate([gk] + [part(n, 1) for n in range(low, high)], axis=0)
        vals = jnp.concatenate([gv] + [part(n, 2) for n in range(low, high)], axis=0)
        shape = (HD + count * BLK, HD)
        sub = lax.broadcasted_iota(jnp.int32, shape, 0)
        lane = lax.broadcasted_iota(jnp.int32, shape, 1)
        kb = (sub >> 6) - 2 + low
        qb = (lane >> 6) + b
        keep = (sub < HD) | (jnp.abs(kb - qb) <= 1)
        if i <= 1:
            keep = keep & ((sub < HD) | (here > 0) | (kb >= GLOB))
        wq, wk, wv = grads(q2, g2, norm, delta, keys, vals, keep)
        dq[b * 64 : b * 64 + 128] = wq
        gk_sum = gk_sum + wk[0:HD]
        gv_sum = gv_sum + wv[0:HD]
        span = slice(low * 64, high * 64)
        dk[span] = dk[span] + wk[HD:]
        dv[span] = dv[span] + wv[HD:]
    hext = halo[256:272].astype(F32)
    hdelta = two(hext, 0)[:, 0:64]
    hnorm = jnp.where(here == 0, OFF, two(hext, 2)[:, 0:64])
    hq, hk, hv, hg = halo[0:64], halo[64:128], halo[128:192], halo[192:256]
    e0 = x[0, 256:272].astype(F32)
    aq, ak, av = grads(
        part(0, 0), part(0, 3), lse_all[:, 0:64], two(e0, 0)[:, 0:64], hk, hv
    )
    bq, bk, bv = grads(hq, hg, hnorm, hdelta, part(0, 1), part(0, 2))
    dq[0:64] = dq[0:64] + aq
    dk[0:64] = dk[0:64] + bk
    dv[0:64] = dv[0:64] + bv
    hback[0:64] = (bq * FACTOR).astype(BF16)
    hback[64:128] = (ak * FACTOR).astype(BF16)
    hback[128:192] = av.astype(BF16)
    gpart[0] = gq_sum * FACTOR
    gpart[1] = gk_sum * FACTOR
    gpart[2] = gv_sum


def rand_body(table, x, y, dk_in, dv_in, dk, dv, z):
    dk[...] = dk_in[...]
    dv[...] = dv_in[...]

    def step(t, carry):
        ext = y[t, 384:400].astype(F32)
        for r in range(RAND):
            j = table[NB + t, r]
            k = x[j, 64:128]
            v = x[j, 128:192]
            q = y[t, r * 128 : r * 128 + 64]
            g = y[t, r * 128 + 64 : r * 128 + 128]
            delta = (ext[4 * r : 4 * r + 1] + ext[4 * r + 1 : 4 * r + 2])[:, 0:64]
            norm = (ext[4 * r + 2 : 4 * r + 3] + ext[4 * r + 3 : 4 * r + 4])[:, 0:64]
            pq, pk, pv = grads(q, g, norm, delta, k, v)
            z[t, r * 64 : r * 64 + 64] = (pq * FACTOR).astype(BF16)
            span = pl.ds(pl.multiple_of(j * 64, 64), 64)
            dk[span] = dk[span] + pk
            dv[span] = dv[span] + pv
        return carry

    lax.fori_loop(0, NB, step, 0)


def merge_body(pos, table, dq, dk, dv, z, hback, gtot, out, acc):
    acc[...] = dq[...] * FACTOR

    def step(t, carry):
        for r in range(RAND):
            b = table[t, r]
            span = pl.ds(pl.multiple_of(b * 64, 64), 64)
            acc[span] = acc[span] + z[t, r * 64 : r * 64 + 64].astype(F32)
        return carry

    lax.fori_loop(0, NB, step, 0)
    home = jnp.where(pos[0] == 0, 1.0, 0.0)
    for b in range(NB):
        span = slice(b * 64, b * 64 + 64)
        rq, rk, rv = acc[span], dk[span] * FACTOR, dv[span]
        if b < GLOB:
            rq = rq + home * gtot[0, span]
            rk = rk + home * gtot[1, span]
            rv = rv + home * gtot[2, span]
        if b == NB - 1:
            rq = rq + hback[0:64].astype(F32)
            rk = rk + hback[64:128].astype(F32)
            rv = rv + hback[128:192].astype(F32)
        out[b, 0:64] = rq.astype(BF16)
        out[b, 64:128] = rk.astype(BF16)
        out[b, 128:192] = rv.astype(BF16)


def unpack_body(w, q, k, v):
    for h in range(HEADS):
        cols = pl.ds(h * HD, HD)
        q[:, cols] = w[h, 0:64]
        k[:, cols] = w[h, 64:128]
        v[:, cols] = w[h, 128:192]


def struct(shape, dtype=BF16):
    return jax.ShapeDtypeStruct(shape, dtype)


def exchange(x, axis):
    return lax.all_to_all(x, axis, split_axis=0, concat_axis=0, tiled=True)


def per_device(query, key, value, output, grad_out, logsumexp, rand_blocks):
    position = lax.axis_index("seq")
    pos = position.astype(jnp.int32).reshape(1)
    rows = NB * BLK
    packed = call(
        pack_body, struct((HEADS, SLAB, HD)), [VM] * 5, nbytes=5 << 18
    )(query, key, value, output, grad_out)
    x = exchange(packed, "head")
    table = call(table_body, struct((2 * NB, HD), jnp.int32), [SM, VM], nbytes=1 << 14)(
        pos, rand_blocks.reshape(NB, NB * RAND)
    )
    y, halo, glob = call(
        select_body,
        (struct((NB, PAIR, HD)), struct((SLAB, HD)), struct((GLOB, SLAB, HD))),
        [SM, SM, VM, VM],
        nbytes=3 << 20,
        scratch=[pltpu.VMEM((NB, 16, BLK), F32)],
    )(pos, table, x, logsumexp)
    groups = NB
    halo = lax.ppermute(halo, "seq", [(s, s + 1) for s in range(groups - 1)])
    glob = jnp.where(position == 0, glob, 0).astype(BF16)
    for reach in (8, 4, 2, 1):
        moved = lax.ppermute(
            glob, "seq", [(s, s + reach) for s in range(0, groups, 2 * reach)]
        )
        glob = jnp.where(position % (2 * reach) == reach, moved, glob)
    y = exchange(y, "seq")
    dq, dk, dv, gpart, hback = call(
        home_body,
        (
            struct((rows, HD), F32),
            struct((rows, HD), F32),
            struct((rows, HD), F32),
            struct((3, HD, HD), F32),
            struct((3 * BLK, HD)),
        ),
        [SM, VM, VM, VM, VM],
        flops=1 << 30,
        nbytes=4 << 20,
    )(pos, x, logsumexp, glob, halo)
    hback = lax.ppermute(hback, "seq", [(s, s - 1) for s in range(1, groups)])
    dk, dv, z = call(
        rand_body,
        (struct((rows, HD), F32), struct((rows, HD), F32), struct((NB, RAND * BLK, HD))),
        [SM, VM, VM, VM, VM],
        flops=1 << 28,
        nbytes=6 << 20,
        aliases={3: 0, 4: 1},
    )(table, x, y, dk, dv)
    z = exchange(z, "seq")
    for reach in (1, 2, 4, 8):
        moved = lax.ppermute(
            gpart.astype(BF16),
            "seq",
            [(s + reach, s) for s in range(0, groups, 2 * reach)],
        )
        gpart = gpart + moved.astype(F32)
    w = call(
        merge_body,
        struct((NB, 3 * BLK, HD)),
        [SM, SM, VM, VM, VM, VM, VM, VM],
        nbytes=4 << 20,
        scratch=[pltpu.VMEM((rows, HD), F32)],
    )(pos, table, dq, dk, dv, z, hback, gpart)
    w = exchange(w, "head")
    shape = struct((BLK, HEADS * HD))
    return call(unpack_body, (shape, shape, shape), [VM], nbytes=3 << 19)(w)


def solution(mesh):
    in_specs = (
        P(("seq", "head"), None),
        P(("seq", "head"), None),
        P(("seq", "head"), None),
        P(("seq", "head"), None),
        P(("seq", "head"), None),
        P("head", "seq"),
        P(),
    )
    out_specs = (P(("seq", "head"), None), P(("seq", "head"), None), P(("seq", "head"), None))
    return jax.shard_map(
        per_device, mesh=mesh, in_specs=in_specs, out_specs=out_specs, check_vma=False
    )
```

time: 661 us -> 202 us (0.31)
  waiting for transfers between devices: 369 us -> 92.6 us
  starting transfers between devices: 106 us -> 41.2 us
  local copies, waits for them, and re-layouts: 67.5 us -> 11.6 us
  other arithmetic: 33.5 us -> 0.28 us
  matrix products: 28.9 us -> 0 us
  Pallas kernels: 0 us -> 23.3 us
  between operations: 15.3 us -> 0.93 us
  blocking collectives: 36.6 us -> 28.8 us
    psum x2 -> x0, waiting for transfers between devices: 258 us -> none  [the longest x1 148 us: per_device(): lax.psum(spread_q.astype(jnp.bfloat16), 'seq').astype(jnp.float32)]
    all_to_all x12 -> x3, waiting for transfers between devices: 110 us -> 32.5 us  [exchange(): return lax.all_to_all(x, axis, split_axis=0, concat_axis=0, tiled=True)]
    ppermute x8 -> x10, waiting for transfers between devices: 0.03 us -> 60.1 us  [the longest x4 35.7 us: per_device(): lax.ppermute(glob, 'seq', [(s, s + reach) for s in range(0, groups, 2 * r...]
    all_to_all x12 -> x3, starting transfers between devices: 80.2 us -> 25.3 us  [exchange(): return lax.all_to_all(x, axis, split_axis=0, concat_axis=0, tiled=True)]
    gather x60 -> x0, local copies, waits for them, and re-layouts: 45.4 us -> none
    psum x1 -> x0, blocking collectives: 36.6 us -> none  [spread(): return lax.psum(kept, axis)]
    dot_general x40 -> x0, matrix products: 28.9 us -> none  [the longest x8 7.53 us: block_grads(): jnp.einsum('...mn,...md->...nd', weights_low, grad_rows, preferred_elemen...]
    all_to_all x0 -> x1, blocking collectives: none -> 28.8 us  [exchange(): return lax.all_to_all(x, axis, split_axis=0, concat_axis=0, tiled=True)]
  transfers between devices with their start and end apart: 22 -> 13, of which waited for: 11 -> 9; matrix products, arithmetic and copies ran while one was open for 16% -> 0% of each run, Pallas kernels for 0% -> 2%
where the time goes in v1:
time: 202 us; the launch traced here: 199 us
  waiting for transfers between devices  92.6 us (46%)
  starting transfers between devices  41.2 us (20%)
  blocking collectives  28.8 us (14%)
  Pallas kernels  23.3 us (12%)
  local copies, waits for them, and re-layouts  11.6 us (6%)
    ppermute x4, waiting for transfers between devices, per_device(): lax.ppermute(glob, 'seq', [(s, s + reach) for s in range(0, groups, 2 * r...  35.7 us
    all_to_all x3, waiting for transfers between devices, exchange(): return lax.all_to_all(x, axis, split_axis=0, concat_axis=0, tiled=True)  32.5 us
    all_to_all x1, blocking collectives, exchange(): return lax.all_to_all(x, axis, split_axis=0, concat_axis=0, tiled=True)  28.8 us
    all_to_all x3, starting transfers between devices, exchange(): return lax.all_to_all(x, axis, split_axis=0, concat_axis=0, tiled=True)  25.3 us
    ppermute x4, waiting for transfers between devices, per_device(): lax.ppermute(gpart.astype(BF16), 'seq', [(s + reach, s) for s in range(0,...  14.6 us
    pallas_call x1, Pallas kernels, per_device(): call(rand_body, (struct((rows, HD), F32), struct((rows, HD), F32), struct...  12.6 us
    unnamed x31, local copies, waits for them, and re-layouts  11.5 us
    ppermute x4, starting transfers between devices, per_device(): lax.ppermute(gpart.astype(BF16), 'seq', [(s + reach, s) for s in range(0,...  7.48 us
  transfers between devices with their start and end apart: 13, of which 9 were waited for; matrix products, arithmetic and copies ran while one was open for 0% of the time, Pallas kernels for 2%

profile of v1, /device:TPU:32, one launch (start us, length us, event | category | flops | bytes accessed | tf_op | source)
XLA Modules:
  0.0 198.7 jit_solution(8042374879755707434)
XLA Ops:
  0.6 0.9 copy-done.8
  1.6 0.9 copy-done.9
  2.5 0.9 copy-done.10
  3.5 0.9 copy-done.11
  4.4 0.9 copy-done.12
  5.4 1.3 shard_map.95
  6.7 10.3 %all-to-all-start = ((bf16[16,272,128]{2,1,0:T(8,128)(2,1)}), bf16[16,272,128]{2,1,0:T(8,128)(2,1)S(1)}, u32[]{:S(2)}, u32[]{:S(2)}) async-start(bf16[16,272,128]{2,1,0:T(8,128)(2,1)} %shard_map.95), calls=%async_computation | async-start | bytes 2228224 | tf_op jit(solution)/shard_map/all_to_all | solution.py:297
  17.0 0.1 copy.13
  17.1 0.1 reshape.13.entries
  17.3 0.2 shard_map.94.table
  17.5 32.5 %all-to-all-done.x = bf16[16,272,128]{2,1,0:T(8,128)(2,1)S(1)} async-done(((bf16[16,272,128]{2,1,0:T(8,128)(2,1)}), bf16[16,272,128]{2,1,0:T(8,128)(2,1)S(1)}, u32[]{:S(2)}, u32[]{:S(2)}) %all-to-all-start) | async-done | bytes 1114144 | tf_op jit(solution)/shard_map/all_to_all | solution.py:297
  50.0 2.2 %shard_map.96 = (bf16[16,400,128]{2,1,0:T(8,128)(2,1)S(1)}, bf16[272,128]{1,0:T(8,128)(2,1)S(1)}, bf16[2,272,128]{2,1,0:T(8,128)(2,1)S(1)}) custom-call(s32[1]{0:T(128)} %bitcast.pos, s32[32,128]{1,0:T(8,128)S(1)} %shard_map.94.table, bf16[16,272,128]{2,1,0:T(8,128)(2,1)S(1)} %all-to-all-done.x, f32[1,1024]{1,0:T(1,128)S(1)} %copy-done.13), custom_call_target="tpu_custom_call" | custom-call | bytes 3145728 | tf_op jit(solution)/shard_map/pallas_call | solution.py:311
  52.2 1.2 copy-done.4
  53.4 6.4 %all-to-all-start.1 = ((bf16[16,400,128]{2,1,0:T(8,128)(2,1)}), bf16[16,400,128]{2,1,0:T(8,128)(2,1)S(1)}, u32[]{:S(2)}, u32[]{:S(2)}) async-start(bf16[16,400,128]{2,1,0:T(8,128)(2,1)} %copy-done.4), calls=%async_computation.1 | async-start | bytes 3276800 | tf_op jit(solution)/shard_map/all_to_all | solution.py:297
  59.8 0.7 collective-permute-start
  60.5 0.0 collective-permute-done
  60.6 1.3 collective-permute-start.1
  61.9 31.6 %collective-permute-done.1 = bf16[2,272,128]{2,1,0:T(8,128)(2,1)S(1)} collective-permute-done((bf16[2,272,128]{2,1,0:T(8,128)(2,1)S(1)}, bf16[2,272,128]{2,1,0:T(8,128)(2,1)S(1)}, u32[]{:S(2)}, u32[]{:S(2)}) %collective-permute-start.1) | collective-permute-done | bytes 139296 | tf_op jit(solution)/shard_map/ppermute | solution.py:322
  93.5 1.3 collective-permute-start.2
  94.8 3.5 %collective-permute-done.2 = bf16[2,272,128]{2,1,0:T(8,128)(2,1)S(1)} collective-permute-done((bf16[2,272,128]{2,1,0:T(8,128)(2,1)S(1)}, bf16[2,272,128]{2,1,0:T(8,128)(2,1)S(1)}, u32[]{:S(2)}, u32[]{:S(2)}) %collective-permute-start.2) | collective-permute-done | bytes 139296 | tf_op jit(solution)/shard_map/ppermute | solution.py:322
  98.3 1.3 collective-permute-start.3
  99.7 1.9 collective-permute-start.4
  101.6 0.6 collective-permute-done.3
  102.2 5.7 %collective-permute-done.4.halo = bf16[272,128]{1,0:T(8,128)(2,1)S(1)} collective-permute-done((bf16[272,128]{1,0:T(8,128)(2,1)S(1)}, bf16[272,128]{1,0:T(8,128)(2,1)S(1)}, u32[]{:S(2)}, u32[]{:S(2)}) %collective-permute-start.4) | collective-permute-done | bytes 69664 | tf_op jit(solution)/shard_map/ppermute | solution.py:319
  108.0 4.6 %shard_map.97 = (f32[1024,128]{1,0:T(8,128)S(1)}, f32[1024,128]{1,0:T(8,128)S(1)}, f32[1024,128]{1,0:T(8,128)S(1)}, f32[3,128,128]{2,1,0:T(8,128)S(1)}, bf16[192,128]{1,0:T(8,128)(2,1)S(1)}) custom-call(s32[1]{0:T(128)} %bitcast.pos, bf16[16,272,128]{2,1,0:T(8,128)(2,1)S(1)} %all-to-all-done.x, f32[1,1024]{1,0:T(1,128)S(1)} %copy-done.13, ...), custom_call_target="tpu_custom_call" | custom-call | flops 1073741824 | bytes 4194304 | tf_op jit(solution)/shard_map/pallas_call | solution.py:327
  112.6 0.8 copy-done
  113.4 0.8 copy-done.6
  114.2 1.0 copy-done.1
  115.3 12.6 %shard_map.98 = (f32[1024,128]{1,0:T(8,128)S(1)}, f32[1024,128]{1,0:T(8,128)S(1)}, bf16[16,192,128]{2,1,0:T(8,128)(2,1)S(1)}) custom-call(s32[32,128]{1,0:T(8,128)S(1)} %shard_map.94.table, bf16[16,272,128]{2,1,0:T(8,128)(2,1)S(1)} %all-to-all-done.x, bf16[16,400,128]{2,1,0:T(8,128)(2,1)S(1)} %all-to-all-done.1.y, ...), custom_call_target="tpu_custom_call", output_to_operand_aliasing={{0}: (3, {}), {1}: (4, {})} | custom-call | flops 268435456 | bytes 6291456 | tf_op jit(solution)/shard_map/pallas_call | solution.py:341
  127.9 0.8 copy-done.2
  128.7 0.9 copy-done.5
  129.6 8.7 %all-to-all-start.2 = ((bf16[16,192,128]{2,1,0:T(8,128)(2,1)}), bf16[16,192,128]{2,1,0:T(8,128)(2,1)S(1)}, u32[]{:S(2)}, u32[]{:S(2)}) async-start(bf16[16,192,128]{2,1,0:T(8,128)(2,1)} %copy-done.5), calls=%async_computation.2 | async-start | bytes 1572864 | tf_op jit(solution)/shard_map/all_to_all | solution.py:297
  138.3 1.4 collective-permute-start.6
  139.8 5.2 %collective-permute-done.6 = bf16[3,128,128]{2,1,0:T(8,128)(2,1)S(1)} collective-permute-done((bf16[3,128,128]{2,1,0:T(8,128)(2,1)S(1)}, bf16[3,128,128]{2,1,0:T(8,128)(2,1)S(1)}, u32[]{:S(2)}, u32[]{:S(2)}) %collective-permute-start.6) | collective-permute-done | bytes 98336 | tf_op jit(solution)/shard_map/ppermute | solution.py:351
  145.0 1.3 collective-permute-start.7
  146.3 7.2 %collective-permute-done.7 = bf16[3,128,128]{2,1,0:T(8,128)(2,1)S(1)} collective-permute-done((bf16[3,128,128]{2,1,0:T(8,128)(2,1)S(1)}, bf16[3,128,128]{2,1,0:T(8,128)(2,1)S(1)}, u32[]{:S(2)}, u32[]{:S(2)}) %collective-permute-start.7) | collective-permute-done | bytes 98336 | tf_op jit(solution)/shard_map/ppermute | solution.py:351
  153.5 4.1 %collective-permute-start.8 = (bf16[3,128,128]{2,1,0:T(8,128)(2,1)S(1)}, bf16[3,128,128]{2,1,0:T(8,128)(2,1)S(1)}, u32[]{:S(2)}, u32[]{:S(2)}) collective-permute-start(bf16[3,128,128]{2,1,0:T(8,128)(2,1)S(1)} %fusion.2), channel_id=1, source_target_pairs={{64,0},{192,128},{65,1},{193,129},{66,2},{194,130},{67,3},{195,131... | collective-permute-start | bytes 294920 | tf_op jit(solution)/shard_map/ppermute | solution.py:351
  157.7 2.2 %collective-permute-done.8 = bf16[3,128,128]{2,1,0:T(8,128)(2,1)S(1)} collective-permute-done((bf16[3,128,128]{2,1,0:T(8,128)(2,1)S(1)}, bf16[3,128,128]{2,1,0:T(8,128)(2,1)S(1)}, u32[]{:S(2)}, u32[]{:S(2)}) %collective-permute-start.8) | collective-permute-done | bytes 98336 | tf_op jit(solution)/shard_map/ppermute | solution.py:351
  159.8 0.1 fusion.1
  159.9 0.7 collective-permute-start.9
  160.6 1.9 collective-permute-start.5
  162.5 0.1 convert_add_fusion.gtot
  162.6 4.0 %collective-permute-done.5.hback = bf16[192,128]{1,0:T(8,128)(2,1)S(1)} collective-permute-done((bf16[192,128]{1,0:T(8,128)(2,1)S(1)}, bf16[192,128]{1,0:T(8,128)(2,1)S(1)}, u32[]{:S(2)}, u32[]{:S(2)}) %collective-permute-start.5) | collective-permute-done | bytes 49184 | tf_op jit(solution)/shard_map/ppermute | solution.py:340
  166.6 0.0 all-to-all-done.2.z
  166.6 1.0 copy-done.7
  167.6 1.2 shard_map.99
  168.8 28.8 %all_to_all.20.w = bf16[16,192,128]{2,1,0:T(8,128)(2,1)S(1)} all-to-all(bf16[16,192,128]{2,1,0:T(8,128)(2,1)S(1)} %shard_map.99), channel_id=1, replica_groups=mesh['seq'=16,'head'=16] {'head'}, dimensions={0} | all-to-all | bytes 1572864 | tf_op jit(solution)/shard_map/all_to_all | solution.py:297
  197.7 1.1 shard_map.100
  (28 shorter events, 0.2 us)
Async XLA Ops:
  0.6 1.0 copy-start.8
  1.6 0.9 copy-start.9
  2.5 0.9 copy-start.10
  3.5 0.9 copy-start.11
  4.4 0.9 copy-start.12
  6.7 10.3 %copy-start.14 = (s32[256,3]{0,1:T(4,128)S(1)}, s32[256,3]{0,1:T(4,128)}, u32[]{:S(2)}) copy-start(s32[256,3]{0,1:T(4,128)} %param.13) | copy-start | bytes 9220
  6.7 43.3 %copy-start.13 = (f32[1,1024]{1,0:T(1,128)S(1)}, f32[1,1024]{1,0:T(1,128)}, u32[]{:S(2)}) copy-start(f32[1,1024]{1,0:T(1,128)} %lse.3) | copy-start | bytes 12292
  6.7 43.3 %all-to-all-start = ((bf16[16,272,128]{2,1,0:T(8,128)(2,1)}), bf16[16,272,128]{2,1,0:T(8,128)(2,1)S(1)}, u32[]{:S(2)}, u32[]{:S(2)}) async-start(bf16[16,272,128]{2,1,0:T(8,128)(2,1)} %shard_map.95), calls=%async_computation | async-start | bytes 2228224 | tf_op jit(solution)/shard_map/all_to_all | solution.py:297
  52.2 1.2 copy-start.4
  53.4 60.8 %all-to-all-start.1 = ((bf16[16,400,128]{2,1,0:T(8,128)(2,1)}), bf16[16,400,128]{2,1,0:T(8,128)(2,1)S(1)}, u32[]{:S(2)}, u32[]{:S(2)}) async-start(bf16[16,400,128]{2,1,0:T(8,128)(2,1)} %copy-done.4), calls=%async_computation.1 | async-start | bytes 3276800 | tf_op jit(solution)/shard_map/all_to_all | solution.py:297
  59.8 0.7 collective-permute-start
  60.6 33.0 %collective-permute-start.1 = (bf16[2,272,128]{2,1,0:T(8,128)(2,1)S(1)}, bf16[2,272,128]{2,1,0:T(8,128)(2,1)S(1)}, u32[]{:S(2)}, u32[]{:S(2)}) collective-permute-start(bf16[2,272,128]{2,1,0:T(8,128)(2,1)S(1)} %broadcast_select_fusion.1), channel_id=1, source_target_pairs={{0,64},{128,192},{1,65},{129,193},{2,66},{130,194},{3,67},{131,195... | collective-permute-start | bytes 417800 | tf_op jit(solution)/shard_map/ppermute | solution.py:322
  93.5 4.8 %collective-permute-start.2 = (bf16[2,272,128]{2,1,0:T(8,128)(2,1)S(1)}, bf16[2,272,128]{2,1,0:T(8,128)(2,1)S(1)}, u32[]{:S(2)}, u32[]{:S(2)}) collective-permute-start(bf16[2,272,128]{2,1,0:T(8,128)(2,1)S(1)} %broadcast_select_fusion.2), channel_id=1, source_target_pairs={{0,32},{64,96},{128,160},{192,224},{1,33},{65,97},{129,161},{193,2... | collective-permute-start | bytes 417800 | tf_op jit(solution)/shard_map/ppermute | solution.py:322
  98.3 3.9 %collective-permute-start.3 = (bf16[2,272,128]{2,1,0:T(8,128)(2,1)S(1)}, bf16[2,272,128]{2,1,0:T(8,128)(2,1)S(1)}, u32[]{:S(2)}, u32[]{:S(2)}) collective-permute-start(bf16[2,272,128]{2,1,0:T(8,128)(2,1)S(1)} %broadcast_select_fusion.3), channel_id=1, source_target_pairs={{0,16},{32,48},{64,80},{96,112},{128,144},{160,176},{192,208},{224... | collective-permute-start | bytes 417800 | tf_op jit(solution)/shard_map/ppermute | solution.py:322
  99.7 8.3 %collective-permute-start.4 = (bf16[272,128]{1,0:T(8,128)(2,1)S(1)}, bf16[272,128]{1,0:T(8,128)(2,1)S(1)}, u32[]{:S(2)}, u32[]{:S(2)}) collective-permute-start(bf16[272,128]{1,0:T(8,128)(2,1)S(1)} %get-tuple-element.15), channel_id=1, source_target_pairs={{0,16},{16,32},{32,48},{48,64},{64,80},{80,96},{96,112},{112,128},... | collective-permute-start | bytes 208904 | tf_op jit(solution)/shard_map/ppermute | solution.py:319
  112.6 0.8 copy-start
  113.4 0.8 copy-start.6
  114.2 1.0 copy-start.1
  127.9 0.8 copy-start.2
  128.7 0.9 copy-start.5
  129.6 36.9 %all-to-all-start.2 = ((bf16[16,192,128]{2,1,0:T(8,128)(2,1)}), bf16[16,192,128]{2,1,0:T(8,128)(2,1)S(1)}, u32[]{:S(2)}, u32[]{:S(2)}) async-start(bf16[16,192,128]{2,1,0:T(8,128)(2,1)} %copy-done.5), calls=%async_computation.2 | async-start | bytes 1572864 | tf_op jit(solution)/shard_map/all_to_all | solution.py:297
  138.3 28.3 %copy-start.3 = (f32[1024,128]{1,0:T(8,128)S(1)}, f32[1024,128]{1,0:T(8,128)}, u32[]{:S(2)}) copy-start(f32[1024,128]{1,0:T(8,128)} %copy-done.2) | copy-start | bytes 1572868
  138.3 6.6 %collective-permute-start.6 = (bf16[3,128,128]{2,1,0:T(8,128)(2,1)S(1)}, bf16[3,128,128]{2,1,0:T(8,128)(2,1)S(1)}, u32[]{:S(2)}, u32[]{:S(2)}) collective-permute-start(bf16[3,128,128]{2,1,0:T(8,128)(2,1)S(1)} %convert_element_type.26), channel_id=1, source_target_pairs={{16,0},{48,32},{80,64},{112,96},{144,128},{176,160},{208,192},{240... | collective-permute-start | bytes 294920 | tf_op jit(solution)/shard_map/ppermute | solution.py:351
  145.0 8.5 %collective-permute-start.7 = (bf16[3,128,128]{2,1,0:T(8,128)(2,1)S(1)}, bf16[3,128,128]{2,1,0:T(8,128)(2,1)S(1)}, u32[]{:S(2)}, u32[]{:S(2)}) collective-permute-start(bf16[3,128,128]{2,1,0:T(8,128)(2,1)S(1)} %fusion), channel_id=1, source_target_pairs={{32,0},{96,64},{160,128},{224,192},{33,1},{97,65},{161,129},{225,1... | collective-permute-start | bytes 294920 | tf_op jit(solution)/shard_map/ppermute | solution.py:351
  153.5 6.3 %collective-permute-start.8 = (bf16[3,128,128]{2,1,0:T(8,128)(2,1)S(1)}, bf16[3,128,128]{2,1,0:T(8,128)(2,1)S(1)}, u32[]{:S(2)}, u32[]{:S(2)}) collective-permute-start(bf16[3,128,128]{2,1,0:T(8,128)(2,1)S(1)} %fusion.2), channel_id=1, source_target_pairs={{64,0},{192,128},{65,1},{193,129},{66,2},{194,130},{67,3},{195,131... | collective-permute-start | bytes 294920 | tf_op jit(solution)/shard_map/ppermute | solution.py:351
  159.9 2.6 %collective-permute-start.9 = (bf16[3,128,128]{2,1,0:T(8,128)(2,1)S(1)}, bf16[3,128,128]{2,1,0:T(8,128)(2,1)S(1)}, u32[]{:S(2)}, u32[]{:S(2)}) collective-permute-start(bf16[3,128,128]{2,1,0:T(8,128)(2,1)S(1)} %fusion.1), channel_id=1, source_target_pairs={{128,0},{129,1},{130,2},{131,3},{132,4},{133,5},{134,6},{135,7},{1... | collective-permute-start | bytes 294920 | tf_op jit(solution)/shard_map/ppermute | solution.py:351
  160.6 6.0 %collective-permute-start.5 = (bf16[192,128]{1,0:T(8,128)(2,1)S(1)}, bf16[192,128]{1,0:T(8,128)(2,1)S(1)}, u32[]{:S(2)}, u32[]{:S(2)}) collective-permute-start(bf16[192,128]{1,0:T(8,128)(2,1)S(1)} %get-tuple-element.23), channel_id=1, source_target_pairs={{16,0},{32,16},{48,32},{64,48},{80,64},{96,80},{112,96},{128,112},... | collective-permute-start | bytes 147464 | tf_op jit(solution)/shard_map/ppermute | solution.py:340
  166.6 1.0 copy-start.7

commit v2 on v1

--- a/solution.py
+++ b/solution.py
@@ -1,3 +1,5 @@
+import functools
+
 import jax
 import jax.numpy as jnp
 from jax import lax
@@ -13,24 +15,26 @@
 NB = 16
 FACTOR = HD ** (-0.5)
 OFF = 1e30
+EDGES = (0, 1, NB - 1)
 SLAB = 4 * BLK + 16
 PAIR = RAND * 2 * BLK + 16
 F32 = jnp.float32
 BF16 = jnp.bfloat16
 
+HB = pl.BlockSpec(memory_space=pltpu.HBM)
 VM = pl.BlockSpec(memory_space=pltpu.VMEM)
 SM = pl.BlockSpec(memory_space=pltpu.SMEM)
 
 
-def call(body, outs, in_specs, flops=0, nbytes=0, scratch=(), aliases={}):
+def call(body, outs, in_specs, out_specs, flops=0, nbytes=0, scratch=(), aliases={}, limit=8):
     return pl.pallas_call(
         body,
         out_shape=outs,
         in_specs=in_specs,
-        out_specs=jax.tree.map(lambda _: VM, outs),
+        out_specs=out_specs,
         scratch_shapes=list(scratch),
         input_output_aliases=aliases,
-        compiler_params=pltpu.CompilerParams(vmem_limit_bytes=32 << 20),
+        compiler_params=pltpu.CompilerParams(vmem_limit_bytes=limit << 20),
         cost_estimate=pl.CostEstimate(flops=flops, bytes_accessed=nbytes, transcendentals=0),
     )
 
@@ -52,24 +56,41 @@
     return high, (x - high).astype(BF16).astype(F32)
 
 
-def pack_body(q, k, v, o, g, out):
+def pack_body(q, k, v, o, g, out, qs, ks, vs, os, gs, ps, in_sem, out_sem):
+    pulls = [
+        pltpu.make_async_copy(src, dst, in_sem.at[i])
+        for i, (src, dst) in enumerate(zip((o, g, q, k, v), (os, gs, qs, ks, vs)))
+    ]
+    for pull in pulls:
+        pull.start()
     lane = lax.broadcasted_iota(jnp.int32, (BLK, HD), 1)
     row = lax.broadcasted_iota(jnp.int32, (16, HD), 0)
     deltas = jnp.zeros((BLK, HD), F32)
+    pulls[0].wait()
+    pulls[1].wait()
     for h in range(HEADS):
         cols = pl.ds(h * HD, HD)
-        gh = g[:, cols]
-        out[h, 0:64] = q[:, cols]
-        out[h, 64:128] = k[:, cols]
-        out[h, 128:192] = v[:, cols]
-        out[h, 192:256] = gh
-        part = jnp.sum(gh.astype(F32) * o[:, cols].astype(F32), axis=1, keepdims=True)
+        gh = gs[:, cols]
+        ps[h, 192:256] = gh
+        part = jnp.sum(gh.astype(F32) * os[:, cols].astype(F32), axis=1, keepdims=True)
         deltas = jnp.where(lane == h, part, deltas)
     turned = jnp.transpose(jnp.concatenate([deltas, jnp.zeros((BLK, HD), F32)], axis=0))
     high, low = pieces(turned)
+    for pull in pulls[2:]:
+        pull.wait()
+    pushes = []
     for h in range(HEADS):
+        cols = pl.ds(h * HD, HD)
+        ps[h, 0:64] = qs[:, cols]
+        ps[h, 64:128] = ks[:, cols]
+        ps[h, 128:192] = vs[:, cols]
         tile = jnp.where(row == 0, high[h : h + 1], jnp.where(row == 1, low[h : h + 1], 0.0))
-        out[h, 256:272] = tile.astype(BF16)
+        ps[h, 256:272] = tile.astype(BF16)
+        push = pltpu.make_async_copy(ps.at[h], out.at[h], out_sem.at[h])
+        push.start()
+        pushes.append(push)
+    for push in pushes:
+        push.wait()
 
 
 def table_body(pos, entries, out):
@@ -102,7 +123,7 @@
     return pair[:, 64:128] if b % 2 else pair[:, 0:64]
 
 
-def select_body(pos, table, x, lse, out, halo, glob, ext):
+def select_body(pos, table, x, lse, dest, halo, glob, ext, out, sem):
     row = lax.broadcasted_iota(jnp.int32, (16, BLK), 0)
     lse_all = lse[...]
 
@@ -115,8 +136,10 @@
         norm = norm_rows(lse_all, b)
         if b < GLOB:
             plain = ext_of(b, norm)
-            glob[b, 0:256] = x[b, 0:256]
-            glob[b, 256:272] = jnp.concatenate([plain, plain], axis=1).astype(BF16)
+            full = jnp.concatenate([plain, plain], axis=1).astype(BF16)
+            keep = pos[0] == 0
+            glob[b, 0:256] = jnp.where(keep, x[b, 0:256], jnp.zeros((256, HD), BF16))
+            glob[b, 256:272] = jnp.where(keep, full, jnp.zeros((16, HD), BF16))
             norm = jnp.where(pos[0] == 0, OFF, norm)
         ext[b] = ext_of(b, norm)
         if b == NB - 1:
@@ -136,9 +159,16 @@
                 part = pltpu.roll(part, 4 * r, 0)
             tile = tile + part
         out[t, 384:400] = jnp.concatenate([tile, tile], axis=1).astype(BF16)
+        pltpu.make_async_copy(out.at[t], dest.at[t], sem.at[t]).start()
         return carry
 
     lax.fori_loop(0, NB, step, 0)
+
+    def finish(t, carry):
+        pltpu.make_async_copy(out.at[t], dest.at[t], sem.at[t]).wait()
+        return carry
+
+    lax.fori_loop(0, NB, finish, 0)
 
 
 def grads(q, g, norm, delta, k, v, keep=None):
@@ -150,8 +180,17 @@
     return tn(dst, k), nn(dst, q), nn(pt.astype(BF16), g)
 
 
-def home_body(pos, x, lse, glob, halo, dq, dk, dv, gpart, hback):
+def home_body(
+    pos, x, lse, glob, halo, dk_far, dv_far, w, dq, edge, gpart, glow, hback,
+    dk, dv, dk_in, dv_in, buf, in_sem, out_sem,
+):
     here = pos[0]
+    pulls = [
+        pltpu.make_async_copy(dk_far, dk_in, in_sem.at[0]),
+        pltpu.make_async_copy(dv_far, dv_in, in_sem.at[1]),
+    ]
+    for pull in pulls:
+        pull.start()
     lse_all = lse[...]
     lanes = lax.broadcasted_iota(jnp.int32, lse_all.shape, 1)
     lse_all = jnp.where((here == 0) & (lanes < GLOB * BLK), OFF, lse_all)
@@ -181,8 +220,9 @@
         b = 2 * i
         fq, fk, fv = grads(gq, gg, gnorm, gdelta, rows(b, 1), rows(b, 2))
         gq_sum = gq_sum + fq
-        dk[b * 64 : b * 64 + 128] = fk
-        dv[b * 64 : b * 64 + 128] = fv
+        span = slice(b * 64, b * 64 + 128)
+        dk[span] = fk
+        dv[span] = fv
     for i in range(NB // 2):
         b = 2 * i
         q2, g2 = rows(b, 0), rows(b, 3)
@@ -224,36 +264,97 @@
     hback[0:64] = (bq * FACTOR).astype(BF16)
     hback[64:128] = (ak * FACTOR).astype(BF16)
     hback[128:192] = av.astype(BF16)
-    gpart[0] = gq_sum * FACTOR
-    gpart[1] = gk_sum * FACTOR
-    gpart[2] = gv_sum
-
-
-def rand_body(table, x, y, dk_in, dv_in, dk, dv, z):
-    dk[...] = dk_in[...]
-    dv[...] = dv_in[...]
-
-    def step(t, carry):
-        ext = y[t, 384:400].astype(F32)
-        for r in range(RAND):
-            j = table[NB + t, r]
-            k = x[j, 64:128]
-            v = x[j, 128:192]
-            q = y[t, r * 128 : r * 128 + 64]
-            g = y[t, r * 128 + 64 : r * 128 + 128]
-            delta = (ext[4 * r : 4 * r + 1] + ext[4 * r + 1 : 4 * r + 2])[:, 0:64]
-            norm = (ext[4 * r + 2 : 4 * r + 3] + ext[4 * r + 3 : 4 * r + 4])[:, 0:64]
-            pq, pk, pv = grads(q, g, norm, delta, k, v)
-            z[t, r * 64 : r * 64 + 64] = (pq * FACTOR).astype(BF16)
+    for n, total in enumerate((gq_sum * FACTOR, gk_sum * FACTOR, gv_sum)):
+        gpart[n] = total
+        glow[n] = total.astype(BF16)
+    for pull in pulls:
+        pull.wait()
+    pushes = []
+    for b in range(NB):
+        span = slice(b * 64, b * 64 + 64)
+        rk = (dk[span] + dk_in[span]) * FACTOR
+        rv = dv[span] + dv_in[span]
+        if b in EDGES:
+            at = EDGES.index(b) * 128
+            edge[at : at + 64] = rk
+            edge[at + 64 : at + 128] = rv
+            continue
+        buf[b, 0:64] = rk.astype(BF16)
+        buf[b, 64:128] = rv.astype(BF16)
+        push = pltpu.make_async_copy(buf.at[b], w.at[b, pl.ds(64, 128)], out_sem.at[b])
+        push.start()
+        pushes.append(push)
+    for push in pushes:
+        push.wait()
+
+
+def rand_body(first, last, per_step, table, x, y, *refs):
+    ended = last == NB
+    if first:
+        dk_in, dv_in, z_in = refs[:3]
+        refs = refs[3:]
+    if ended:
+        dk_out, dv_out, z, dk, dv, buf, sem, acc_sem = refs
+        head = pltpu.make_async_copy(z_in, z.at[pl.ds(0, first)], sem.at[NB])
+        head.start()
+        target, base = buf, first
+    else:
+        dk, dv, z = refs
+        target, base = z, 0
+        if first:
+            z[0:first] = z_in[...]
+    if first:
+        dk[...] = dk_in[...]
+        dv[...] = dv_in[...]
+    else:
+        dk[...] = jnp.zeros_like(dk)
+        dv[...] = jnp.zeros_like(dv)
+
+    def step(i, carry):
+        done = []
+        for c in range(per_step):
+            t = first + i * per_step + c
+            ext = y[t, 384:400].astype(F32)
+            for r in range(RAND):
+                j = table[NB + t, r]
+                k = x[j, 64:128]
+                v = x[j, 128:192]
+                q = y[t, r * 128 : r * 128 + 64]
+                g = y[t, r * 128 + 64 : r * 128 + 128]
+                delta = (ext[4 * r : 4 * r + 1] + ext[4 * r + 1 : 4 * r + 2])[:, 0:64]
+                norm = (ext[4 * r + 2 : 4 * r + 3] + ext[4 * r + 3 : 4 * r + 4])[:, 0:64]
+                pq, pk, pv = grads(q, g, norm, delta, k, v)
+                target[t - base, r * 64 : r * 64 + 64] = (pq * FACTOR).astype(BF16)
+                done.append((j, pk, pv))
+            if ended:
+                pltpu.make_async_copy(buf.at[t - base], z.at[t], sem.at[t]).start()
+        for j, pk, pv in done:
             span = pl.ds(pl.multiple_of(j * 64, 64), 64)
             dk[span] = dk[span] + pk
             dv[span] = dv[span] + pv
         return carry
 
-    lax.fori_loop(0, NB, step, 0)
-
-
-def merge_body(pos, table, dq, dk, dv, z, hback, gtot, out, acc):
+    lax.fori_loop(0, (last - first) // per_step, step, 0)
+    if ended:
+        drains = []
+        for n in range(4):
+            span = pl.ds(n * 256, 256)
+            for m, (src, dst) in enumerate(((dk, dk_out), (dv, dv_out))):
+                drain = pltpu.make_async_copy(src.at[span], dst.at[span], acc_sem.at[2 * n + m])
+                drain.start()
+                drains.append(drain)
+        for drain in drains:
+            drain.wait()
+        head.wait()
+
+        def finish(t, carry):
+            pltpu.make_async_copy(buf.at[t - base], z.at[t], sem.at[t]).wait()
+            return carry
+
+        lax.fori_loop(first, last, finish, 0)
+
+
+def merge_body(pos, table, dq, edge, z, hback, gtot, w_in, w, acc, out, out_edge, sem):
     acc[...] = dq[...] * FACTOR
 
     def step(t, carry):
@@ -265,20 +366,35 @@
 
     lax.fori_loop(0, NB, step, 0)
     home = jnp.where(pos[0] == 0, 1.0, 0.0)
+    pushes = []
+
+    def send(src, dst, n):
+        push = pltpu.make_async_copy(src, dst, sem.at[n])
+        push.start()
+        pushes.append(push)
+
+    for n, b in enumerate(EDGES):
+        rk, rv = edge[n * 128 : n * 128 + 64], edge[n * 128 + 64 : n * 128 + 128]
+        if b < GLOB:
+            rk = rk + home * gtot[1, b * 64 : b * 64 + 64]
+            rv = rv + home * gtot[2, b * 64 : b * 64 + 64]
+        else:
+            rk = rk + hback[64:128].astype(F32)
+            rv = rv + hback[128:192].astype(F32)
+        out_edge[n, 0:64] = rk.astype(BF16)
+        out_edge[n, 64:128] = rv.astype(BF16)
+        send(out_edge.at[n], w.at[b, pl.ds(64, 128)], NB + n)
     for b in range(NB):
         span = slice(b * 64, b * 64 + 64)
-        rq, rk, rv = acc[span], dk[span] * FACTOR, dv[span]
+        rq = acc[span]
         if b < GLOB:
             rq = rq + home * gtot[0, span]
-            rk = rk + home * gtot[1, span]
-            rv = rv + home * gtot[2, span]
         if b == NB - 1:
             rq = rq + hback[0:64].astype(F32)
-            rk = rk + hback[64:128].astype(F32)
-            rv = rv + hback[128:192].astype(F32)
-        out[b, 0:64] = rq.astype(BF16)
-        out[b, 64:128] = rk.astype(BF16)
-        out[b, 128:192] = rv.astype(BF16)
+        out[b] = rq.astype(BF16)
+        send(out.at[b], w.at[b, pl.ds(0, 64)], b)
+    for push in pushes:
+        push.wait()
 
 
 def unpack_body(w, q, k, v):
@@ -293,6 +409,22 @@
     return jax.ShapeDtypeStruct(shape, dtype)
 
 
+def far(shape, dtype=BF16):
+    return pltpu.HBM(shape, dtype)
+
+
+def near(shape, dtype=BF16):
+    return pltpu.VMEM(shape, dtype)
+
+
+def hold(x):
+    return pltpu.with_memory_space_constraint(x, pltpu.VMEM)
+
+
+def keep_far(x):
+    return pltpu.with_memory_space_constraint(x, pltpu.HBM)
+
+
 def exchange(x, axis):
     return lax.all_to_all(x, axis, split_axis=0, concat_axis=0, tiled=True)
 
@@ -301,69 +433,116 @@
     position = lax.axis_index("seq")
     pos = position.astype(jnp.int32).reshape(1)
     rows = NB * BLK
+    groups = NB
+    dma = pltpu.SemaphoreType.DMA
+    whole = pltpu.VMEM((BLK, HEADS * HD), BF16)
     packed = call(
-        pack_body, struct((HEADS, SLAB, HD)), [VM] * 5, nbytes=5 << 18
-    )(query, key, value, output, grad_out)
+        pack_body,
+        far((HEADS, SLAB, HD)),
+        [HB] * 5,
+        HB,
+        nbytes=5 << 18,
+        scratch=[whole] * 5 + [pltpu.VMEM((HEADS, SLAB, HD), BF16), dma((5,)), dma((HEADS,))],
+    )(*map(keep_far, (query, key, value, output, grad_out)))
     x = exchange(packed, "head")
-    table = call(table_body, struct((2 * NB, HD), jnp.int32), [SM, VM], nbytes=1 << 14)(
+    table = call(table_body, struct((2 * NB, HD), jnp.int32), [SM, VM], VM, nbytes=1 << 14)(
         pos, rand_blocks.reshape(NB, NB * RAND)
     )
     y, halo, glob = call(
         select_body,
-        (struct((NB, PAIR, HD)), struct((SLAB, HD)), struct((GLOB, SLAB, HD))),
+        (far((NB, PAIR, HD)), struct((SLAB, HD)), struct((GLOB, SLAB, HD))),
         [SM, SM, VM, VM],
+        (HB, VM, VM),
         nbytes=3 << 20,
-        scratch=[pltpu.VMEM((NB, 16, BLK), F32)],
+        scratch=[
+            pltpu.VMEM((NB, 16, BLK), F32),
+            pltpu.VMEM((NB, PAIR, HD), BF16),
+            dma((NB,)),
+        ],
     )(pos, table, x, logsumexp)
-    groups = NB
+    y = exchange(y, "seq")
     halo = lax.ppermute(halo, "seq", [(s, s + 1) for s in range(groups - 1)])
-    glob = jnp.where(position == 0, glob, 0).astype(BF16)
-    for reach in (8, 4, 2, 1):
-        moved = lax.ppermute(
+
+    def spread(glob, reach):
+        return glob + lax.ppermute(
             glob, "seq", [(s, s + reach) for s in range(0, groups, 2 * reach)]
         )
-        glob = jnp.where(position % (2 * reach) == reach, moved, glob)
-    y = exchange(y, "seq")
-    dq, dk, dv, gpart, hback = call(
+
+    glob = spread(glob, 8)
+    glob, halo, y = lax.optimization_barrier((glob, halo, y))
+    grid = pltpu.VMEM((rows, HD), F32)
+    carried = ()
+    cuts = (0, 5, 10, 16)
+    for n in range(3):
+        first, last = cuts[n], cuts[n + 1]
+        final = last == NB
+        place = far if final else near
+        scratch = []
+        if final:
+            scratch = [
+                grid,
+                grid,
+                pltpu.VMEM((last - first, RAND * BLK, HD), BF16),
+                dma((NB + 1,)),
+                dma((8,)),
+            ]
+        moving = spread(glob, 4 >> n)
+        carried = call(
+            functools.partial(rand_body, first, last, 2 if final else 5),
+            (
+                place((rows, HD), F32),
+                place((rows, HD), F32),
+                place((last, RAND * BLK, HD)),
+            ),
+            [SM] + [VM] * (2 + len(carried)),
+            (HB if final else VM,) * 3,
+            flops=1 << 28,
+            nbytes=3 << 20,
+            scratch=scratch,
+        )(table, x, y, *map(hold, carried))
+        glob, carried = lax.optimization_barrier((moving, carried))
+    dk, dv, z = carried
+    z = exchange(z, "seq")
+    w, dq, edge, gpart, glow, hback = call(
         home_body,
         (
-            struct((rows, HD), F32),
-            struct((rows, HD), F32),
-            struct((rows, HD), F32),
+            far((NB, 3 * BLK, HD)),
+            near((rows, HD), F32),
+            struct((len(EDGES) * 2 * BLK, HD), F32),
             struct((3, HD, HD), F32),
+            struct((3, HD, HD)),
             struct((3 * BLK, HD)),
         ),
-        [SM, VM, VM, VM, VM],
+        [SM] + [VM] * 4 + [HB] * 2,
+        (HB,) + (VM,) * 5,
         flops=1 << 30,
         nbytes=4 << 20,
-    )(pos, x, logsumexp, glob, halo)
+        scratch=[grid] * 4 + [pltpu.VMEM((NB, 2 * BLK, HD), BF16), dma((2,)), dma((NB,))],
+    )(pos, x, logsumexp, glob, halo, keep_far(dk), keep_far(dv))
     hback = lax.ppermute(hback, "seq", [(s, s - 1) for s in range(1, groups)])
-    dk, dv, z = call(
-        rand_body,
-        (struct((rows, HD), F32), struct((rows, HD), F32), struct((NB, RAND * BLK, HD))),
-        [SM, VM, VM, VM, VM],
-        flops=1 << 28,
-        nbytes=6 << 20,
-        aliases={3: 0, 4: 1},
-    )(table, x, y, dk, dv)
-    z = exchange(z, "seq")
-    for reach in (1, 2, 4, 8):
-        moved = lax.ppermute(
-            gpart.astype(BF16),
-            "seq",
-            [(s + reach, s) for s in range(0, groups, 2 * reach)],
-        )
-        gpart = gpart + moved.astype(F32)
+    for reach in (1, 4):
+        span = range(0, groups, 4) if reach == 1 else (0,)
+        for n in (1, 2, 3):
+            moved = lax.ppermute(glow, "seq", [(s + n * reach, s) for s in span])
+            gpart = gpart + moved.astype(F32)
+        glow = gpart.astype(BF16)
     w = call(
         merge_body,
-        struct((NB, 3 * BLK, HD)),
-        [SM, SM, VM, VM, VM, VM, VM, VM],
+        far((NB, 3 * BLK, HD)),
+        [SM, SM] + [VM] * 5 + [HB],
+        HB,
         nbytes=4 << 20,
-        scratch=[pltpu.VMEM((rows, HD), F32)],
-    )(pos, table, dq, dk, dv, z, hback, gpart)
+        scratch=[
+            grid,
+            pltpu.VMEM((NB, BLK, HD), BF16),
+            pltpu.VMEM((len(EDGES), 2 * BLK, HD), BF16),
+            dma((NB + len(EDGES),)),
+        ],
+        aliases={7: 0},
+    )(pos, table, hold(dq), edge, z, hback, gpart, w)
     w = exchange(w, "head")
     shape = struct((BLK, HEADS * HD))
-    return call(unpack_body, (shape, shape, shape), [VM], nbytes=3 << 19)(w)
+    return call(unpack_body, (shape, shape, shape), [VM], (VM,) * 3, nbytes=3 << 19)(w)
 
 
 def solution(mesh):

time: 202 us -> 181 us (0.90); the launches traced: 199 us -> 180 us
  waiting for transfers between devices: 92.6 us -> 78.8 us
  local copies, waits for them, and re-layouts: 11.6 us -> 0.26 us
  Pallas kernels: 23.3 us -> 28.9 us
    ppermute x8 -> x10, waiting for transfers between devices: 50.4 us -> 9.99 us  [the longest x6 8.3 us: per_device(): moved = lax.ppermute(glow, 'seq', [(s + n * reach, s) for s in span])]
    ppermute x1, waiting for transfers between devices: 5.73 us -> 26.6 us  [per_device(): halo = lax.ppermute(halo, 'seq', [(s, s + 1) for s in range(groups - 1)])]
    unnamed x31 -> x5, local copies, waits for them, and re-layouts: 11.5 us -> 0.15 us
    all_to_all x3, waiting for transfers between devices: 32.5 us -> 39.8 us  [exchange(): return lax.all_to_all(x, axis, split_axis=0, concat_axis=0, tiled=True)]
    pallas_call x7 -> x9, Pallas kernels: 23.3 us -> 28.9 us  [the longest x3 14.1 us: per_device(): call(functools.partial(rand_body, first, last, 2 if final else 5), (place...]
    all_to_all x3, starting transfers between devices: 25.3 us -> 23 us  [exchange(): return lax.all_to_all(x, axis, split_axis=0, concat_axis=0, tiled=True)]
    ppermute x8 -> x10, starting transfers between devices: 12 us -> 13.1 us  [the longest x6 7.75 us: per_device(): moved = lax.ppermute(glow, 'seq', [(s + n * reach, s) for s in span])]
  transfers between devices with their start and end apart: 13 -> 15, of which waited for: 9 -> 7; matrix products, arithmetic and copies ran while one was open for 0% -> 0% of each run, Pallas kernels for 2% -> 11%
where the time goes in v2:
time: 181 us; the launch traced here: 180 us
  waiting for transfers between devices  78.8 us (44%)
  starting transfers between devices  41.4 us (23%)
  blocking collectives  29.6 us (16%)
  Pallas kernels  28.9 us (16%)
    all_to_all x3, waiting for transfers between devices, exchange(): return lax.all_to_all(x, axis, split_axis=0, concat_axis=0, tiled=True)  39.8 us
    all_to_all x1, blocking collectives, exchange(): return lax.all_to_all(x, axis, split_axis=0, concat_axis=0, tiled=True)  29.6 us
    ppermute x1, waiting for transfers between devices, per_device(): halo = lax.ppermute(halo, 'seq', [(s, s + 1) for s in range(groups - 1)])  26.6 us
    all_to_all x3, starting transfers between devices, exchange(): return lax.all_to_all(x, axis, split_axis=0, concat_axis=0, tiled=True)  23 us
    pallas_call x3, Pallas kernels, per_device(): call(functools.partial(rand_body, first, last, 2 if final else 5), (place...  14.1 us
    ppermute x6, waiting for transfers between devices, per_device(): moved = lax.ppermute(glow, 'seq', [(s + n * reach, s) for s in span])  8.3 us
    ppermute x6, starting transfers between devices, per_device(): moved = lax.ppermute(glow, 'seq', [(s + n * reach, s) for s in span])  7.75 us
    pallas_call x1, Pallas kernels, per_device(): call(home_body, (far((NB, 3 * BLK, HD)), near((rows, HD), F32), struct((l...  5.92 us
  transfers between devices with their start and end apart: 15, of which 7 were waited for; matrix products, arithmetic and copies ran while one was open for 0% of the time, Pallas kernels for 11%

profile of v2, /device:TPU:32, one launch (start us, length us, event | category | flops | bytes accessed | tf_op | source)
XLA Modules:
  0.0 180.2 jit_solution(3700925764796174953)
XLA Ops:
  0.6 2.5 %shard_map.95 = bf16[16,272,128]{2,1,0:T(8,128)(2,1)} custom-call(bf16[64,2048]{1,0:T(8,128)(2,1)} %q.1, bf16[64,2048]{1,0:T(8,128)(2,1)} %k.1, bf16[64,2048]{1,0:T(8,128)(2,1)} %v.1, bf16[64,2048]{1,0:T(8,128)(2,1)} %o.1, bf16[64,2048]{1,0:T(8,128)(2,1)} %g.1), custom_call_target="tpu_custom_call" | custom-call | bytes 1310720 | tf_op jit(solution)/shard_map/pallas_call | solution.py:439
  3.2 0.0 copy-start.1
  3.2 0.0 copy-start
  3.2 10.1 %all-to-all-start = ((bf16[16,272,128]{2,1,0:T(8,128)(2,1)}), bf16[16,272,128]{2,1,0:T(8,128)(2,1)S(1)}, u32[]{:S(2)}, u32[]{:S(2)}) async-start(bf16[16,272,128]{2,1,0:T(8,128)(2,1)} %shard_map.95), calls=%async_computation | async-start | bytes 2228224 | tf_op jit(solution)/shard_map/all_to_all | solution.py:429
  13.4 0.0 copy-done.1
  13.4 0.1 copy.12
  13.5 0.1 reshape.13.entries
  13.6 0.2 shard_map.94.table
  13.9 32.5 %all-to-all-done.x = bf16[16,272,128]{2,1,0:T(8,128)(2,1)S(1)} async-done(((bf16[16,272,128]{2,1,0:T(8,128)(2,1)}), bf16[16,272,128]{2,1,0:T(8,128)(2,1)S(1)}, u32[]{:S(2)}, u32[]{:S(2)}) %all-to-all-start) | async-done | bytes 1114144 | tf_op jit(solution)/shard_map/all_to_all | solution.py:429
  46.4 0.0 copy-done
  46.4 3.0 %shard_map.96 = (bf16[16,400,128]{2,1,0:T(8,128)(2,1)}, bf16[272,128]{1,0:T(8,128)(2,1)S(1)}, bf16[2,272,128]{2,1,0:T(8,128)(2,1)S(1)}) custom-call(s32[1]{0:T(128)} %bitcast.pos, s32[32,128]{1,0:T(8,128)S(1)} %shard_map.94.table, bf16[16,272,128]{2,1,0:T(8,128)(2,1)S(1)} %all-to-all-done.x, f32[1,1024]{1,0:T(1,128)S(1)} %copy-done), custom_call_target="tpu_custom_call" | custom-call | bytes 3145728 | tf_op jit(solution)/shard_map/pallas_call | solution.py:451
  49.4 6.4 %all-to-all-start.1 = ((bf16[16,400,128]{2,1,0:T(8,128)(2,1)}), bf16[16,400,128]{2,1,0:T(8,128)(2,1)S(1)}, u32[]{:S(2)}, u32[]{:S(2)}) async-start(bf16[16,400,128]{2,1,0:T(8,128)(2,1)} %get-tuple-element.38), calls=%async_computation.1 | async-start | bytes 3276800 | tf_op jit(solution)/shard_map/all_to_all | solution.py:429
  55.8 0.7 collective-permute-start
  56.5 3.4 %collective-permute-start.1 = (bf16[272,128]{1,0:T(8,128)(2,1)S(1)}, bf16[272,128]{1,0:T(8,128)(2,1)S(1)}, u32[]{:S(2)}, u32[]{:S(2)}) collective-permute-start(bf16[272,128]{1,0:T(8,128)(2,1)S(1)} %get-tuple-element.37), channel_id=1, source_target_pairs={{0,16},{16,32},{32,48},{48,64},{64,80},{80,96},{96,112},{112,128},... | collective-permute-start | bytes 208904 | tf_op jit(solution)/shard_map/ppermute | solution.py:464
  59.9 0.0 collective-permute-done
  59.9 26.6 %collective-permute-done.1.halo = bf16[272,128]{1,0:T(8,128)(2,1)S(1)} collective-permute-done((bf16[272,128]{1,0:T(8,128)(2,1)S(1)}, bf16[272,128]{1,0:T(8,128)(2,1)S(1)}, u32[]{:S(2)}, u32[]{:S(2)}) %collective-permute-start.1) | collective-permute-done | bytes 69664 | tf_op jit(solution)/shard_map/ppermute | solution.py:464
  86.5 7.2 %all-to-all-done.1.y = bf16[16,400,128]{2,1,0:T(8,128)(2,1)S(1)} async-done(((bf16[16,400,128]{2,1,0:T(8,128)(2,1)}), bf16[16,400,128]{2,1,0:T(8,128)(2,1)S(1)}, u32[]{:S(2)}, u32[]{:S(2)}) %all-to-all-start.1) | async-done | bytes 1638432 | tf_op jit(solution)/shard_map/all_to_all | solution.py:429
  93.7 1.3 collective-permute-start.2
  95.0 4.0 %shard_map.97 = (f32[1024,128]{1,0:T(8,128)S(1)}, f32[1024,128]{1,0:T(8,128)S(1)}, bf16[5,192,128]{2,1,0:T(8,128)(2,1)S(1)}) custom-call(s32[32,128]{1,0:T(8,128)S(1)} %shard_map.94.table, bf16[16,272,128]{2,1,0:T(8,128)(2,1)S(1)} %all-to-all-done.x, bf16[16,400,128]{2,1,0:T(8,128)(2,1)S(1)} %all-to-all-done.1.y), custom_call_target="tpu_custom_call" | custom-call | flops 268435456 | bytes 3145728 | tf_op jit(solution)/shard_map/pallas_call | solution.py:490
  99.0 1.7 collective-permute-done.2
  100.7 2.1 %collective-permute-start.3 = (bf16[2,272,128]{2,1,0:T(8,128)(2,1)S(1)}, bf16[2,272,128]{2,1,0:T(8,128)(2,1)S(1)}, u32[]{:S(2)}, u32[]{:S(2)}) collective-permute-start(bf16[2,272,128]{2,1,0:T(8,128)(2,1)S(1)} %add.31), channel_id=1, source_target_pairs={{0,32},{64,96},{128,160},{192,224},{1,33},{65,97},{129,161},{193,2... | collective-permute-start | bytes 417800 | tf_op jit(solution)/shard_map/ppermute | solution.py:467
  102.9 4.0 %shard_map.98 = (f32[1024,128]{1,0:T(8,128)S(1)}, f32[1024,128]{1,0:T(8,128)S(1)}, bf16[10,192,128]{2,1,0:T(8,128)(2,1)S(1)}) custom-call(s32[32,128]{1,0:T(8,128)S(1)} %shard_map.94.table, bf16[16,272,128]{2,1,0:T(8,128)(2,1)S(1)} %all-to-all-done.x, bf16[16,400,128]{2,1,0:T(8,128)(2,1)S(1)} %all-to-all-done.1.y, ...), custom_call_target="tpu_custom_call" | custom-call | flops 268435456 | bytes 3145728 | tf_op jit(solution)/shard_map/pallas_call | solution.py:490
  106.9 0.0 collective-permute-done.3
  106.9 1.3 collective-permute-start.4
  108.2 6.1 %shard_map.99 = (f32[1024,128]{1,0:T(8,128)}, f32[1024,128]{1,0:T(8,128)}, bf16[16,192,128]{2,1,0:T(8,128)(2,1)}) custom-call(s32[32,128]{1,0:T(8,128)S(1)} %shard_map.94.table, bf16[16,272,128]{2,1,0:T(8,128)(2,1)S(1)} %all-to-all-done.x, bf16[16,400,128]{2,1,0:T(8,128)(2,1)S(1)} %all-to-all-done.1.y, f32[1024,128]{1,0:T(8,128)S(1)} %get-tuple-element.52.refs_0_, ...), custom_call_target="tpu_custom_call" | custom-call | flops 268435456 | bytes 3145728 | tf_op jit(solution)/shard_map/pallas_call | solution.py:490
  114.4 0.0 collective-permute-done.4
  114.4 6.5 %all-to-all-start.2 = ((bf16[16,192,128]{2,1,0:T(8,128)(2,1)}), bf16[16,192,128]{2,1,0:T(8,128)(2,1)S(1)}, u32[]{:S(2)}, u32[]{:S(2)}) async-start(bf16[16,192,128]{2,1,0:T(8,128)(2,1)} %get-tuple-element.64), calls=%async_computation.2 | async-start | bytes 1572864 | tf_op jit(solution)/shard_map/all_to_all | solution.py:429
  120.9 5.9 %shard_map.100 = (bf16[16,192,128]{2,1,0:T(8,128)(2,1)}, f32[1024,128]{1,0:T(8,128)S(1)}, f32[384,128]{1,0:T(8,128)S(1)}, f32[3,128,128]{2,1,0:T(8,128)S(1)}, bf...) custom-call(s32[1]{0:T(128)} %bitcast.pos, bf16[16,272,128]{2,1,0:T(8,128)(2,1)S(1)} %all-to-all-done.x, ...), custom_call_target="tpu_custom_call" | custom-call | flops 1073741824 | bytes 4194304 | tf_op jit(solution)/shard_map/pallas_call | solution.py:506
  126.8 1.3 collective-permute-start.8
  128.1 1.3 collective-permute-start.7
  129.4 1.3 collective-permute-start.6
  130.7 6.8 %collective-permute-done.8 = bf16[3,128,128]{2,1,0:T(8,128)(2,1)S(1)} collective-permute-done((bf16[3,128,128]{2,1,0:T(8,128)(2,1)S(1)}, bf16[3,128,128]{2,1,0:T(8,128)(2,1)S(1)}, u32[]{:S(2)}, u32[]{:S(2)}) %collective-permute-start.8) | collective-permute-done | bytes 98336 | tf_op jit(solution)/shard_map/ppermute | solution.py:526
  137.5 0.0 collective-permute-done.7
  137.5 0.0 collective-permute-done.6
  137.5 0.1 fusion
  137.6 0.7 collective-permute-start.11
  138.3 0.7 collective-permute-start.10
  138.9 2.5 %collective-permute-start.9 = (bf16[3,128,128]{2,1,0:T(8,128)(2,1)S(1)}, bf16[3,128,128]{2,1,0:T(8,128)(2,1)S(1)}, u32[]{:S(2)}, u32[]{:S(2)}) collective-permute-start(bf16[3,128,128]{2,1,0:T(8,128)(2,1)S(1)} %fusion), channel_id=1, source_target_pairs={{64,0},{65,1},{66,2},{67,3},{68,4},{69,5},{70,6},{71,7},{72,8},{73... | collective-permute-start | bytes 294920 | tf_op jit(solution)/shard_map/ppermute | solution.py:526
  141.5 1.9 %collective-permute-start.5 = (bf16[192,128]{1,0:T(8,128)(2,1)S(1)}, bf16[192,128]{1,0:T(8,128)(2,1)S(1)}, u32[]{:S(2)}, u32[]{:S(2)}) collective-permute-start(bf16[192,128]{1,0:T(8,128)(2,1)S(1)} %get-tuple-element.65), channel_id=1, source_target_pairs={{16,0},{32,16},{48,32},{64,48},{80,64},{96,80},{112,96},{128,112},... | collective-permute-start | bytes 147464 | tf_op jit(solution)/shard_map/ppermute | solution.py:522
  143.4 0.0 collective-permute-done.11
  143.4 0.0 collective-permute-done.10
  143.4 1.5 collective-permute-done.9
  144.9 0.1 convert_add_fusion.gtot
  145.0 2.5 %collective-permute-done.5.hback = bf16[192,128]{1,0:T(8,128)(2,1)S(1)} collective-permute-done((bf16[192,128]{1,0:T(8,128)(2,1)S(1)}, bf16[192,128]{1,0:T(8,128)(2,1)S(1)}, u32[]{:S(2)}, u32[]{:S(2)}) %collective-permute-start.5) | collective-permute-done | bytes 49184 | tf_op jit(solution)/shard_map/ppermute | solution.py:522
  147.5 0.0 all-to-all-done.2.z
  147.5 2.1 %shard_map.101 = bf16[16,192,128]{2,1,0:T(8,128)(2,1)} custom-call(s32[1]{0:T(128)} %bitcast.pos, s32[32,128]{1,0:T(8,128)S(1)} %shard_map.94.table, f32[1024,128]{1,0:T(8,128)S(1)} %get-tuple-element.62.dq, f32[384,128]{1,0:T(8,128)S(1)} %get-tuple-element.63.edge, bf16[16,192,128]{2,1,0:T(8,128)(2,1)S(1)} %all-to-all-done.2.z, ...), custom_call_target="tpu_custom_call", output_to_operand_aliasing={{}: (7, {})} | custom-call | bytes 4194304 | tf_op jit(solution)/shard_map/pallas_call | solution.py:529
  149.6 29.6 %all_to_all.20.w = bf16[16,192,128]{2,1,0:T(8,128)(2,1)S(1)} all-to-all(bf16[16,192,128]{2,1,0:T(8,128)(2,1)} %shard_map.101), channel_id=1, replica_groups=mesh['seq'=16,'head'=16] {'head'}, dimensions={0} | all-to-all | bytes 1572864 | tf_op jit(solution)/shard_map/all_to_all | solution.py:429
  179.1 1.1 shard_map.102
  (4 shorter events, 0.2 us)
Async XLA Ops:
  3.2 10.2 %copy-start.1 = (s32[256,3]{0,1:T(4,128)S(1)}, s32[256,3]{0,1:T(4,128)}, u32[]{:S(2)}) copy-start(s32[256,3]{0,1:T(4,128)} %param.13) | copy-start | bytes 9220
  3.2 43.2 %copy-start = (f32[1,1024]{1,0:T(1,128)S(1)}, f32[1,1024]{1,0:T(1,128)}, u32[]{:S(2)}) copy-start(f32[1,1024]{1,0:T(1,128)} %lse.3) | copy-start | bytes 12292
  3.2 43.2 %all-to-all-start = ((bf16[16,272,128]{2,1,0:T(8,128)(2,1)}), bf16[16,272,128]{2,1,0:T(8,128)(2,1)S(1)}, u32[]{:S(2)}, u32[]{:S(2)}) async-start(bf16[16,272,128]{2,1,0:T(8,128)(2,1)} %shard_map.95), calls=%async_computation | async-start | bytes 2228224 | tf_op jit(solution)/shard_map/all_to_all | solution.py:429
  49.4 44.3 %all-to-all-start.1 = ((bf16[16,400,128]{2,1,0:T(8,128)(2,1)}), bf16[16,400,128]{2,1,0:T(8,128)(2,1)S(1)}, u32[]{:S(2)}, u32[]{:S(2)}) async-start(bf16[16,400,128]{2,1,0:T(8,128)(2,1)} %get-tuple-element.38), calls=%async_computation.1 | async-start | bytes 3276800 | tf_op jit(solution)/shard_map/all_to_all | solution.py:429
  55.8 4.0 %collective-permute-start = (bf16[2,272,128]{2,1,0:T(8,128)(2,1)S(1)}, bf16[2,272,128]{2,1,0:T(8,128)(2,1)S(1)}, u32[]{:S(2)}, u32[]{:S(2)}) collective-permute-start(bf16[2,272,128]{2,1,0:T(8,128)(2,1)S(1)} %get-tuple-element.36), channel_id=1, source_target_pairs={{0,128},{1,129},{2,130},{3,131},{4,132},{5,133},{6,134},{7,135},{8... | collective-permute-start | bytes 417800 | tf_op jit(solution)/shard_map/ppermute | solution.py:467
  56.5 30.0 %collective-permute-start.1 = (bf16[272,128]{1,0:T(8,128)(2,1)S(1)}, bf16[272,128]{1,0:T(8,128)(2,1)S(1)}, u32[]{:S(2)}, u32[]{:S(2)}) collective-permute-start(bf16[272,128]{1,0:T(8,128)(2,1)S(1)} %get-tuple-element.37), channel_id=1, source_target_pairs={{0,16},{16,32},{32,48},{48,64},{64,80},{80,96},{96,112},{112,128},... | collective-permute-start | bytes 208904 | tf_op jit(solution)/shard_map/ppermute | solution.py:464
  93.7 6.9 %collective-permute-start.2 = (bf16[2,272,128]{2,1,0:T(8,128)(2,1)S(1)}, bf16[2,272,128]{2,1,0:T(8,128)(2,1)S(1)}, u32[]{:S(2)}, u32[]{:S(2)}) collective-permute-start(bf16[2,272,128]{2,1,0:T(8,128)(2,1)S(1)} %add.30), channel_id=1, source_target_pairs={{0,64},{128,192},{1,65},{129,193},{2,66},{130,194},{3,67},{131,195... | collective-permute-start | bytes 417800 | tf_op jit(solution)/shard_map/ppermute | solution.py:467
  100.7 6.1 %collective-permute-start.3 = (bf16[2,272,128]{2,1,0:T(8,128)(2,1)S(1)}, bf16[2,272,128]{2,1,0:T(8,128)(2,1)S(1)}, u32[]{:S(2)}, u32[]{:S(2)}) collective-permute-start(bf16[2,272,128]{2,1,0:T(8,128)(2,1)S(1)} %add.31), channel_id=1, source_target_pairs={{0,32},{64,96},{128,160},{192,224},{1,33},{65,97},{129,161},{193,2... | collective-permute-start | bytes 417800 | tf_op jit(solution)/shard_map/ppermute | solution.py:467
  106.9 7.5 %collective-permute-start.4 = (bf16[2,272,128]{2,1,0:T(8,128)(2,1)S(1)}, bf16[2,272,128]{2,1,0:T(8,128)(2,1)S(1)}, u32[]{:S(2)}, u32[]{:S(2)}) collective-permute-start(bf16[2,272,128]{2,1,0:T(8,128)(2,1)S(1)} %add.32), channel_id=1, source_target_pairs={{0,16},{32,48},{64,80},{96,112},{128,144},{160,176},{192,208},{224... | collective-permute-start | bytes 417800 | tf_op jit(solution)/shard_map/ppermute | solution.py:467
  114.4 33.1 %all-to-all-start.2 = ((bf16[16,192,128]{2,1,0:T(8,128)(2,1)}), bf16[16,192,128]{2,1,0:T(8,128)(2,1)S(1)}, u32[]{:S(2)}, u32[]{:S(2)}) async-start(bf16[16,192,128]{2,1,0:T(8,128)(2,1)} %get-tuple-element.64), calls=%async_computation.2 | async-start | bytes 1572864 | tf_op jit(solution)/shard_map/all_to_all | solution.py:429
  126.8 10.7 %collective-permute-start.8 = (bf16[3,128,128]{2,1,0:T(8,128)(2,1)S(1)}, bf16[3,128,128]{2,1,0:T(8,128)(2,1)S(1)}, u32[]{:S(2)}, u32[]{:S(2)}) collective-permute-start(bf16[3,128,128]{2,1,0:T(8,128)(2,1)S(1)} %get-tuple-element.67), channel_id=1, source_target_pairs={{48,0},{112,64},{176,128},{240,192},{49,1},{113,65},{177,129},{241... | collective-permute-start | bytes 294920 | tf_op jit(solution)/shard_map/ppermute | solution.py:526
  128.1 9.4 %collective-permute-start.7 = (bf16[3,128,128]{2,1,0:T(8,128)(2,1)S(1)}, bf16[3,128,128]{2,1,0:T(8,128)(2,1)S(1)}, u32[]{:S(2)}, u32[]{:S(2)}) collective-permute-start(bf16[3,128,128]{2,1,0:T(8,128)(2,1)S(1)} %get-tuple-element.67), channel_id=1, source_target_pairs={{32,0},{96,64},{160,128},{224,192},{33,1},{97,65},{161,129},{225,1... | collective-permute-start | bytes 294920 | tf_op jit(solution)/shard_map/ppermute | solution.py:526
  129.4 8.1 %collective-permute-start.6 = (bf16[3,128,128]{2,1,0:T(8,128)(2,1)S(1)}, bf16[3,128,128]{2,1,0:T(8,128)(2,1)S(1)}, u32[]{:S(2)}, u32[]{:S(2)}) collective-permute-start(bf16[3,128,128]{2,1,0:T(8,128)(2,1)S(1)} %get-tuple-element.67), channel_id=1, source_target_pairs={{16,0},{80,64},{144,128},{208,192},{17,1},{81,65},{145,129},{209,1... | collective-permute-start | bytes 294920 | tf_op jit(solution)/shard_map/ppermute | solution.py:526
  137.6 5.8 %collective-permute-start.11 = (bf16[3,128,128]{2,1,0:T(8,128)(2,1)S(1)}, bf16[3,128,128]{2,1,0:T(8,128)(2,1)S(1)}, u32[]{:S(2)}, u32[]{:S(2)}) collective-permute-start(bf16[3,128,128]{2,1,0:T(8,128)(2,1)S(1)} %fusion), channel_id=1, source_target_pairs={{192,0},{193,1},{194,2},{195,3},{196,4},{197,5},{198,6},{199,7},{2... | collective-permute-start | bytes 294920 | tf_op jit(solution)/shard_map/ppermute | solution.py:526
  138.3 5.2 %collective-permute-start.10 = (bf16[3,128,128]{2,1,0:T(8,128)(2,1)S(1)}, bf16[3,128,128]{2,1,0:T(8,128)(2,1)S(1)}, u32[]{:S(2)}, u32[]{:S(2)}) collective-permute-start(bf16[3,128,128]{2,1,0:T(8,128)(2,1)S(1)} %fusion), channel_id=1, source_target_pairs={{128,0},{129,1},{130,2},{131,3},{132,4},{133,5},{134,6},{135,7},{1... | collective-permute-start | bytes 294920 | tf_op jit(solution)/shard_map/ppermute | solution.py:526
  138.9 6.0 %collective-permute-start.9 = (bf16[3,128,128]{2,1,0:T(8,128)(2,1)S(1)}, bf16[3,128,128]{2,1,0:T(8,128)(2,1)S(1)}, u32[]{:S(2)}, u32[]{:S(2)}) collective-permute-start(bf16[3,128,128]{2,1,0:T(8,128)(2,1)S(1)} %fusion), channel_id=1, source_target_pairs={{64,0},{65,1},{66,2},{67,3},{68,4},{69,5},{70,6},{71,7},{72,8},{73... | collective-permute-start | bytes 294920 | tf_op jit(solution)/shard_map/ppermute | solution.py:526
  141.5 6.0 %collective-permute-start.5 = (bf16[192,128]{1,0:T(8,128)(2,1)S(1)}, bf16[192,128]{1,0:T(8,128)(2,1)S(1)}, u32[]{:S(2)}, u32[]{:S(2)}) collective-permute-start(bf16[192,128]{1,0:T(8,128)(2,1)S(1)} %get-tuple-element.65), channel_id=1, source_target_pairs={{16,0},{32,16},{48,32},{64,48},{80,64},{96,80},{112,96},{128,112},... | collective-permute-start | bytes 147464 | tf_op jit(solution)/shard_map/ppermute | solution.py:522

commit v3 on v2

--- a/solution.py
+++ b/solution.py
@@ -1,5 +1,3 @@
-import functools
-
 import jax
 import jax.numpy as jnp
 from jax import lax
@@ -148,21 +146,23 @@
 
     rows16 = lax.broadcasted_iota(jnp.int32, (16, BLK), 0)
 
-    def step(t, carry):
-        tile = jnp.zeros((16, BLK), F32)
-        for r in range(RAND):
-            b = table[t, r]
-            out[t, r * 128 : r * 128 + 64] = x[b, 0:64]
-            out[t, r * 128 + 64 : r * 128 + 128] = x[b, 192:256]
-            part = ext[b]
-            if r:
-                part = pltpu.roll(part, 4 * r, 0)
-            tile = tile + part
-        out[t, 384:400] = jnp.concatenate([tile, tile], axis=1).astype(BF16)
-        pltpu.make_async_copy(out.at[t], dest.at[t], sem.at[t]).start()
+    def step(i, carry):
+        for c in range(2):
+            t = i * 2 + c
+            tile = jnp.zeros((16, BLK), F32)
+            for r in range(RAND):
+                b = table[t, r]
+                out[t, r * 64 : r * 64 + 64] = x[b, 0:64]
+                out[t, 192 + r * 64 : 256 + r * 64] = x[b, 192:256]
+                part = ext[b]
+                if r:
+                    part = pltpu.roll(part, 4 * r, 0)
+                tile = tile + part
+            out[t, 384:400] = jnp.concatenate([tile, tile], axis=1).astype(BF16)
+            pltpu.make_async_copy(out.at[t], dest.at[t], sem.at[t]).start()
         return carry
 
-    lax.fori_loop(0, NB, step, 0)
+    lax.fori_loop(0, NB // 2, step, 0)
 
     def finish(t, carry):
         pltpu.make_async_copy(out.at[t], dest.at[t], sem.at[t]).wait()
@@ -180,84 +180,159 @@
     return tn(dst, k), nn(dst, q), nn(pt.astype(BF16), g)
 
 
-def home_body(
-    pos, x, lse, glob, halo, dk_far, dv_far, w, dq, edge, gpart, glow, hback,
-    dk, dv, dk_in, dv_in, buf, in_sem, out_sem,
-):
-    here = pos[0]
-    pulls = [
-        pltpu.make_async_copy(dk_far, dk_in, in_sem.at[0]),
-        pltpu.make_async_copy(dv_far, dv_in, in_sem.at[1]),
-    ]
-    for pull in pulls:
-        pull.start()
+def two(ext, a):
+    return ext[a : a + 1].astype(F32) + ext[a + 1 : a + 2].astype(F32)
+
+
+def joined(ref, a, first, last):
+    return jnp.concatenate([ref[n, a * 64 : (a + 1) * 64] for n in range(first, last)], axis=0)
+
+
+def pair_delta(x, b):
+    e0 = x[b, 256:272].astype(F32)
+    e1 = x[b + 1, 256:272].astype(F32)
+    return jnp.concatenate([two(e0, 0)[:, 0:64], two(e1, 0)[:, 0:64]], axis=1)
+
+
+def masked_norms(pos, lse):
     lse_all = lse[...]
     lanes = lax.broadcasted_iota(jnp.int32, lse_all.shape, 1)
-    lse_all = jnp.where((here == 0) & (lanes < GLOB * BLK), OFF, lse_all)
-
-    def two(ext, a):
-        return ext[a : a + 1].astype(F32) + ext[a + 1 : a + 2].astype(F32)
-
-    def part(b, a):
-        return x[b, a * 64 : (a + 1) * 64]
-
-    def rows(b, a):
-        return jnp.concatenate([part(b, a), part(b + 1, a)], axis=0)
-
-    gq = jnp.concatenate([glob[0, 0:64], glob[1, 0:64]], axis=0)
-    gk = jnp.concatenate([glob[0, 64:128], glob[1, 64:128]], axis=0)
-    gv = jnp.concatenate([glob[0, 128:192], glob[1, 128:192]], axis=0)
-    gg = jnp.concatenate([glob[0, 192:256], glob[1, 192:256]], axis=0)
+    return jnp.where((pos[0] == 0) & (lanes < GLOB * BLK), OFF, lse_all)
+
+
+def window_body(pos, x, lse, dq_out, dk_out, dv_out, dq, dk, dv, sem):
+    lse_all = masked_norms(pos, lse)
+    for i in range(NB // 2):
+        b = 2 * i
+        norm = lse_all[:, i * HD : (i + 1) * HD]
+        low, high = max(b - 1, 0), min(b + 3, NB)
+        shape = ((high - low) * BLK, HD)
+        kb = (lax.broadcasted_iota(jnp.int32, shape, 0) >> 6) + low
+        qb = (lax.broadcasted_iota(jnp.int32, shape, 1) >> 6) + b
+        keep = jnp.abs(kb - qb) <= 1
+        if low < GLOB:
+            keep = keep & ((pos[0] > 0) | (kb >= GLOB))
+        wq, wk, wv = grads(
+            joined(x, 0, b, b + 2),
+            joined(x, 3, b, b + 2),
+            norm,
+            pair_delta(x, b),
+            joined(x, 1, low, high),
+            joined(x, 2, low, high),
+            keep,
+        )
+        dq[b * 64 : b * 64 + 128] = wq
+        for acc, part in ((dk, wk), (dv, wv)):
+            old = min(b + 1, NB) * 64 if b else 0
+            seen = slice(low * 64, old)
+            if b:
+                acc[seen] = acc[seen] + part[0 : old - low * 64]
+            acc[old : high * 64] = part[old - low * 64 :]
+    pushes = [
+        pltpu.make_async_copy(src, dst, sem.at[n])
+        for n, (src, dst) in enumerate(((dq, dq_out), (dk, dk_out), (dv, dv_out)))
+    ]
+    for push in pushes:
+        push.start()
+    for push in pushes:
+        push.wait()
+
+
+def rand_body(table, x, y, dk_out, dv_out, z, dk, dv, buf, sem, acc_sem):
+    dk[...] = jnp.zeros_like(dk)
+    dv[...] = jnp.zeros_like(dv)
+    sub = lax.broadcasted_iota(jnp.int32, (HD, HD), 0)
+    lane = lax.broadcasted_iota(jnp.int32, (HD, HD), 1)
+    keep = (sub >> 6) == (lane >> 6)
+    left = lax.broadcasted_iota(jnp.int32, (1, HD), 1) < 64
+    per_step = 4
+
+    def step(i, carry):
+        t0 = i * per_step
+        exts = [y[t0 + c, 384:400].astype(F32) for c in range(per_step)]
+        entries = [(c, r) for c in range(per_step) for r in range(RAND)]
+        done = []
+        for n in range(0, len(entries), 2):
+            pair = entries[n : n + 2]
+
+            def both(base):
+                return jnp.concatenate(
+                    [y[t0 + c, base + r * 64 : base + r * 64 + 64] for c, r in pair], axis=0
+                )
+
+            def row(a):
+                one, other = (two(exts[c], 4 * r + a) for c, r in pair)
+                return jnp.where(left, one, other)
+
+            js = [table[NB + t0 + c, r] for c, r in pair]
+            k = jnp.concatenate([x[j, 64:128] for j in js], axis=0)
+            v = jnp.concatenate([x[j, 128:192] for j in js], axis=0)
+            pq, pk, pv = grads(both(0), both(192), row(2), row(0), k, v, keep)
+            low = (pq * FACTOR).astype(BF16)
+            for m, (c, r) in enumerate(pair):
+                buf[t0 + c, r * 64 : r * 64 + 64] = low[m * 64 : m * 64 + 64]
+            done.append((js, pk, pv))
+        for c in range(per_step):
+            t = t0 + c
+            pltpu.make_async_copy(buf.at[t], z.at[t], sem.at[t]).start()
+        for js, pk, pv in done:
+            for m, j in enumerate(js):
+                span = pl.ds(pl.multiple_of(j * 64, 64), 64)
+                dk[span] = dk[span] + pk[m * 64 : m * 64 + 64]
+                dv[span] = dv[span] + pv[m * 64 : m * 64 + 64]
+        return carry
+
+    lax.fori_loop(0, NB // per_step, step, 0)
+    drains = []
+    for n in range(4):
+        span = pl.ds(n * 256, 256)
+        for m, (src, dst) in enumerate(((dk, dk_out), (dv, dv_out))):
+            drain = pltpu.make_async_copy(src.at[span], dst.at[span], acc_sem.at[2 * n + m])
+            drain.start()
+            drains.append(drain)
+    for drain in drains:
+        drain.wait()
+
+    def finish(t, carry):
+        pltpu.make_async_copy(buf.at[t], z.at[t], sem.at[t]).wait()
+        return carry
+
+    lax.fori_loop(0, NB, finish, 0)
+
+
+def global_body(pos, x, lse, glob, halo, dq, dk, dv, gpart, glow, hback):
+    here = pos[0]
+    lse_all = masked_norms(pos, lse)
+    gq, gk, gv, gg = (joined(glob, a, 0, GLOB) for a in range(4))
     ext0 = glob[0, 256:272].astype(F32)
     ext1 = glob[1, 256:272].astype(F32)
     gdelta = jnp.concatenate([two(ext0, 0)[:, 0:64], two(ext1, 0)[:, 0:64]], axis=1)
     gnorm = jnp.concatenate([two(ext0, 2)[:, 0:64], two(ext1, 2)[:, 0:64]], axis=1)
-
     gq_sum = jnp.zeros((HD, HD), F32)
     gk_sum = jnp.zeros((HD, HD), F32)
     gv_sum = jnp.zeros((HD, HD), F32)
     for i in range(NB // 2):
         b = 2 * i
-        fq, fk, fv = grads(gq, gg, gnorm, gdelta, rows(b, 1), rows(b, 2))
+        span = slice(b * 64, b * 64 + 128)
+        q2, k2, v2, g2 = (joined(x, a, b, b + 2) for a in range(4))
+        fq, fk, fv = grads(gq, gg, gnorm, gdelta, k2, v2)
         gq_sum = gq_sum + fq
-        span = slice(b * 64, b * 64 + 128)
         dk[span] = fk
         dv[span] = fv
-    for i in range(NB // 2):
-        b = 2 * i
-        q2, g2 = rows(b, 0), rows(b, 3)
         norm = lse_all[:, i * HD : (i + 1) * HD]
-        e0 = x[b, 256:272].astype(F32)
-        e1 = x[b + 1, 256:272].astype(F32)
-        delta = jnp.concatenate([two(e0, 0)[:, 0:64], two(e1, 0)[:, 0:64]], axis=1)
-        low, high = max(b - 1, 0), min(b + 3, NB)
-        count = high - low
-        keys = jnp.concatenate([gk] + [part(n, 1) for n in range(low, high)], axis=0)
-        vals = jnp.concatenate([gv] + [part(n, 2) for n in range(low, high)], axis=0)
-        shape = (HD + count * BLK, HD)
-        sub = lax.broadcasted_iota(jnp.int32, shape, 0)
-        lane = lax.broadcasted_iota(jnp.int32, shape, 1)
-        kb = (sub >> 6) - 2 + low
-        qb = (lane >> 6) + b
-        keep = (sub < HD) | (jnp.abs(kb - qb) <= 1)
-        if i <= 1:
-            keep = keep & ((sub < HD) | (here > 0) | (kb >= GLOB))
-        wq, wk, wv = grads(q2, g2, norm, delta, keys, vals, keep)
-        dq[b * 64 : b * 64 + 128] = wq
-        gk_sum = gk_sum + wk[0:HD]
-        gv_sum = gv_sum + wv[0:HD]
-        span = slice(low * 64, high * 64)
-        dk[span] = dk[span] + wk[HD:]
-        dv[span] = dv[span] + wv[HD:]
+        wq, wk, wv = grads(q2, g2, norm, pair_delta(x, b), gk, gv)
+        dq[span] = wq
+        gk_sum = gk_sum + wk
+        gv_sum = gv_sum + wv
     hext = halo[256:272].astype(F32)
     hdelta = two(hext, 0)[:, 0:64]
     hnorm = jnp.where(here == 0, OFF, two(hext, 2)[:, 0:64])
     hq, hk, hv, hg = halo[0:64], halo[64:128], halo[128:192], halo[192:256]
     e0 = x[0, 256:272].astype(F32)
     aq, ak, av = grads(
-        part(0, 0), part(0, 3), lse_all[:, 0:64], two(e0, 0)[:, 0:64], hk, hv
+        x[0, 0:64], x[0, 192:256], lse_all[:, 0:64], two(e0, 0)[:, 0:64], hk, hv
     )
-    bq, bk, bv = grads(hq, hg, hnorm, hdelta, part(0, 1), part(0, 2))
+    bq, bk, bv = grads(hq, hg, hnorm, hdelta, x[0, 64:128], x[0, 128:192])
     dq[0:64] = dq[0:64] + aq
     dk[0:64] = dk[0:64] + bk
     dv[0:64] = dv[0:64] + bv
@@ -267,13 +342,27 @@
     for n, total in enumerate((gq_sum * FACTOR, gk_sum * FACTOR, gv_sum)):
         gpart[n] = total
         glow[n] = total.astype(BF16)
+
+
+def gather_body(
+    dq_g, dk_g, dv_g, dq_w, dk_w, dv_w, dk_r, dv_r, w, dq, edge,
+    s0, s1, s2, s3, s4, buf, in_sem, out_sem,
+):
+    held = (s0, s1, s2, s3, s4)
+    pulls = [
+        pltpu.make_async_copy(src, dst, in_sem.at[n])
+        for n, (src, dst) in enumerate(zip((dq_w, dk_w, dv_w, dk_r, dv_r), held))
+    ]
+    for pull in pulls:
+        pull.start()
     for pull in pulls:
         pull.wait()
+    dq[...] = dq_g[...] + s0[...]
     pushes = []
     for b in range(NB):
         span = slice(b * 64, b * 64 + 64)
-        rk = (dk[span] + dk_in[span]) * FACTOR
-        rv = dv[span] + dv_in[span]
+        rk = (dk_g[span] + s1[span] + s3[span]) * FACTOR
+        rv = dv_g[span] + s2[span] + s4[span]
         if b in EDGES:
             at = EDGES.index(b) * 128
             edge[at : at + 64] = rk
@@ -286,72 +375,6 @@
         pushes.append(push)
     for push in pushes:
         push.wait()
-
-
-def rand_body(first, last, per_step, table, x, y, *refs):
-    ended = last == NB
-    if first:
-        dk_in, dv_in, z_in = refs[:3]
-        refs = refs[3:]
-    if ended:
-        dk_out, dv_out, z, dk, dv, buf, sem, acc_sem = refs
-        head = pltpu.make_async_copy(z_in, z.at[pl.ds(0, first)], sem.at[NB])
-        head.start()
-        target, base = buf, first
-    else:
-        dk, dv, z = refs
-        target, base = z, 0
-        if first:
-            z[0:first] = z_in[...]
-    if first:
-        dk[...] = dk_in[...]
-        dv[...] = dv_in[...]
-    else:
-        dk[...] = jnp.zeros_like(dk)
-        dv[...] = jnp.zeros_like(dv)
-
-    def step(i, carry):
-        done = []
-        for c in range(per_step):
-            t = first + i * per_step + c
-            ext = y[t, 384:400].astype(F32)
-            for r in range(RAND):
-                j = table[NB + t, r]
-                k = x[j, 64:128]
-                v = x[j, 128:192]
-                q = y[t, r * 128 : r * 128 + 64]
-                g = y[t, r * 128 + 64 : r * 128 + 128]
-                delta = (ext[4 * r : 4 * r + 1] + ext[4 * r + 1 : 4 * r + 2])[:, 0:64]
-                norm = (ext[4 * r + 2 : 4 * r + 3] + ext[4 * r + 3 : 4 * r + 4])[:, 0:64]
-                pq, pk, pv = grads(q, g, norm, delta, k, v)
-                target[t - base, r * 64 : r * 64 + 64] = (pq * FACTOR).astype(BF16)
-                done.append((j, pk, pv))
-            if ended:
-                pltpu.make_async_copy(buf.at[t - base], z.at[t], sem.at[t]).start()
-        for j, pk, pv in done:
-            span = pl.ds(pl.multiple_of(j * 64, 64), 64)
-            dk[span] = dk[span] + pk
-            dv[span] = dv[span] + pv
-        return carry
-
-    lax.fori_loop(0, (last - first) // per_step, step, 0)
-    if ended:
-        drains = []
-        for n in range(4):
-            span = pl.ds(n * 256, 256)
-            for m, (src, dst) in enumerate(((dk, dk_out), (dv, dv_out))):
-                drain = pltpu.make_async_copy(src.at[span], dst.at[span], acc_sem.at[2 * n + m])
-                drain.start()
-                drains.append(drain)
-        for drain in drains:
-            drain.wait()
-        head.wait()
-
-        def finish(t, carry):
-            pltpu.make_async_copy(buf.at[t - base], z.at[t], sem.at[t]).wait()
-            return carry
-
-        lax.fori_loop(first, last, finish, 0)
 
 
 def merge_body(pos, table, dq, edge, z, hback, gtot, w_in, w, acc, out, out_edge, sem):
@@ -464,61 +487,46 @@
     halo = lax.ppermute(halo, "seq", [(s, s + 1) for s in range(groups - 1)])
 
     def spread(glob, reach):
-        return glob + lax.ppermute(
-            glob, "seq", [(s, s + reach) for s in range(0, groups, 2 * reach)]
-        )
-
-    glob = spread(glob, 8)
-    glob, halo, y = lax.optimization_barrier((glob, halo, y))
+        starts = range(0, groups, 4 * reach)
+        source = glob
+        for n in (1, 2, 3):
+            glob = glob + lax.ppermute(source, "seq", [(s, s + n * reach) for s in starts])
+        return glob
+
+    glob = spread(glob, 4)
     grid = pltpu.VMEM((rows, HD), F32)
-    carried = ()
-    cuts = (0, 5, 10, 16)
-    for n in range(3):
-        first, last = cuts[n], cuts[n + 1]
-        final = last == NB
-        place = far if final else near
-        scratch = []
-        if final:
-            scratch = [
-                grid,
-                grid,
-                pltpu.VMEM((last - first, RAND * BLK, HD), BF16),
-                dma((NB + 1,)),
-                dma((8,)),
-            ]
-        moving = spread(glob, 4 >> n)
-        carried = call(
-            functools.partial(rand_body, first, last, 2 if final else 5),
-            (
-                place((rows, HD), F32),
-                place((rows, HD), F32),
-                place((last, RAND * BLK, HD)),
-            ),
-            [SM] + [VM] * (2 + len(carried)),
-            (HB if final else VM,) * 3,
-            flops=1 << 28,
-            nbytes=3 << 20,
-            scratch=scratch,
-        )(table, x, y, *map(hold, carried))
-        glob, carried = lax.optimization_barrier((moving, carried))
-    dk, dv, z = carried
+    far_acc = far((rows, HD), F32)
+    acc = near((rows, HD), F32)
+    dq_w, dk_w, dv_w = call(
+        window_body,
+        (far_acc,) * 3,
+        [SM, VM, VM],
+        (HB,) * 3,
+        flops=1 << 29,
+        nbytes=2 << 20,
+        scratch=[grid] * 3 + [dma((3,))],
+    )(pos, x, logsumexp)
+    glob, halo, y, dq_w = lax.optimization_barrier((glob, halo, y, dq_w))
+    glob = spread(glob, 1)
+    dk_r, dv_r, z = call(
+        rand_body,
+        (far_acc, far_acc, far((NB, RAND * BLK, HD))),
+        [SM, VM, VM],
+        (HB,) * 3,
+        flops=1 << 29,
+        nbytes=4 << 20,
+        scratch=[grid, grid, pltpu.VMEM((NB, RAND * BLK, HD), BF16), dma((NB,)), dma((8,))],
+    )(table, x, y)
+    glob, z = lax.optimization_barrier((glob, z))
     z = exchange(z, "seq")
-    w, dq, edge, gpart, glow, hback = call(
-        home_body,
-        (
-            far((NB, 3 * BLK, HD)),
-            near((rows, HD), F32),
-            struct((len(EDGES) * 2 * BLK, HD), F32),
-            struct((3, HD, HD), F32),
-            struct((3, HD, HD)),
-            struct((3 * BLK, HD)),
-        ),
-        [SM] + [VM] * 4 + [HB] * 2,
-        (HB,) + (VM,) * 5,
-        flops=1 << 30,
+    dq_g, dk_g, dv_g, gpart, glow, hback = call(
+        global_body,
+        (acc,) * 3 + (struct((3, HD, HD), F32), struct((3, HD, HD)), struct((3 * BLK, HD))),
+        [SM] + [VM] * 4,
+        (VM,) * 6,
+        flops=1 << 29,
         nbytes=4 << 20,
-        scratch=[grid] * 4 + [pltpu.VMEM((NB, 2 * BLK, HD), BF16), dma((2,)), dma((NB,))],
-    )(pos, x, logsumexp, glob, halo, keep_far(dk), keep_far(dv))
+    )(pos, x, logsumexp, glob, halo)
     hback = lax.ppermute(hback, "seq", [(s, s - 1) for s in range(1, groups)])
     for reach in (1, 4):
         span = range(0, groups, 4) if reach == 1 else (0,)
@@ -526,6 +534,15 @@
             moved = lax.ppermute(glow, "seq", [(s + n * reach, s) for s in span])
             gpart = gpart + moved.astype(F32)
         glow = gpart.astype(BF16)
+    w, dq, edge = call(
+        gather_body,
+        (far((NB, 3 * BLK, HD)), acc, struct((len(EDGES) * 2 * BLK, HD), F32)),
+        [VM] * 3 + [HB] * 5,
+        (HB, VM, VM),
+        flops=1 << 24,
+        nbytes=4 << 20,
+        scratch=[grid] * 5 + [pltpu.VMEM((NB, 2 * BLK, HD), BF16), dma((5,)), dma((NB,))],
+    )(*map(hold, (dq_g, dk_g, dv_g)), *map(keep_far, (dq_w, dk_w, dv_w, dk_r, dv_r)))
     w = call(
         merge_body,
         far((NB, 3 * BLK, HD)),

time: 181 us -> 175 us (0.967)
  the two profiles are of different devices: /device:TPU:32 before, /device:TPU:64 now
where the time goes in v3:
time: 175 us; the launch traced here: 174 us
  waiting for transfers between devices  72.4 us (41%)
  starting transfers between devices  44.5 us (25%)
  blocking collectives  29.6 us (17%)
  Pallas kernels  26.4 us (15%)
    all_to_all x3, waiting for transfers between devices, exchange(): return lax.all_to_all(x, axis, split_axis=0, concat_axis=0, tiled=True)  32.5 us
    all_to_all x1, blocking collectives, exchange(): return lax.all_to_all(x, axis, split_axis=0, concat_axis=0, tiled=True)  29.6 us
    ppermute x6, waiting for transfers between devices, spread(): lax.ppermute(source, 'seq', [(s, s + n * reach) for s in starts])  25.9 us
    all_to_all x3, starting transfers between devices, exchange(): return lax.all_to_all(x, axis, split_axis=0, concat_axis=0, tiled=True)  23.9 us
    pallas_call x1, Pallas kernels, per_device(): call(rand_body, (far_acc, far_acc, far((NB, RAND * BLK, HD))), [SM, VM, V...  8.24 us
    ppermute x6, starting transfers between devices, spread(): lax.ppermute(source, 'seq', [(s, s + n * reach) for s in starts])  8.11 us
    ppermute x6, starting transfers between devices, per_device(): moved = lax.ppermute(glow, 'seq', [(s + n * reach, s) for s in span])  7.81 us
    ppermute x6, waiting for transfers between devices, per_device(): moved = lax.ppermute(glow, 'seq', [(s + n * reach, s) for s in span])  7.45 us
  transfers between devices with their start and end apart: 17, of which 6 were waited for; matrix products, arithmetic and copies ran while one was open for 0% of the time, Pallas kernels for 10%

profile of v3, /device:TPU:64, one launch (start us, length us, event | category | flops | bytes accessed | tf_op | source)
XLA Modules:
  0.0 174.3 jit_solution(2637331416884868410)
XLA Ops:
  0.6 2.5 %shard_map.95 = bf16[16,272,128]{2,1,0:T(8,128)(2,1)} custom-call(bf16[64,2048]{1,0:T(8,128)(2,1)} %q.1, bf16[64,2048]{1,0:T(8,128)(2,1)} %k.1, bf16[64,2048]{1,0:T(8,128)(2,1)} %v.1, bf16[64,2048]{1,0:T(8,128)(2,1)} %o.1, bf16[64,2048]{1,0:T(8,128)(2,1)} %g.1), custom_call_target="tpu_custom_call" | custom-call | bytes 1310720 | tf_op jit(solution)/shard_map/pallas_call | solution.py:462
  3.2 0.0 copy-start.1
  3.2 0.0 copy-start
  3.2 9.2 %all-to-all-start = ((bf16[16,272,128]{2,1,0:T(8,128)(2,1)}), bf16[16,272,128]{2,1,0:T(8,128)(2,1)S(1)}, u32[]{:S(2)}, u32[]{:S(2)}) async-start(bf16[16,272,128]{2,1,0:T(8,128)(2,1)} %shard_map.95), calls=%async_computation | async-start | bytes 2228224 | tf_op jit(solution)/shard_map/all_to_all | solution.py:452
  12.5 0.1 copy.12
  12.6 0.1 reshape.13.entries
  12.7 0.2 shard_map.94.table
  13.0 32.5 %all-to-all-done.x = bf16[16,272,128]{2,1,0:T(8,128)(2,1)S(1)} async-done(((bf16[16,272,128]{2,1,0:T(8,128)(2,1)}), bf16[16,272,128]{2,1,0:T(8,128)(2,1)S(1)}, u32[]{:S(2)}, u32[]{:S(2)}) %all-to-all-start) | async-done | bytes 1114144 | tf_op jit(solution)/shard_map/all_to_all | solution.py:452
  45.5 2.5 %shard_map.96 = (bf16[16,400,128]{2,1,0:T(8,128)(2,1)}, bf16[272,128]{1,0:T(8,128)(2,1)S(1)}, bf16[2,272,128]{2,1,0:T(8,128)(2,1)S(1)}) custom-call(s32[1]{0:T(128)} %bitcast.pos, s32[32,128]{1,0:T(8,128)S(1)} %shard_map.94.table, bf16[16,272,128]{2,1,0:T(8,128)(2,1)S(1)} %all-to-all-done.x, f32[1,1024]{1,0:T(1,128)S(1)} %copy-done), custom_call_target="tpu_custom_call" | custom-call | bytes 3145728 | tf_op jit(solution)/shard_map/pallas_call | solution.py:474
  47.9 6.9 %all-to-all-start.1 = ((bf16[16,400,128]{2,1,0:T(8,128)(2,1)}), bf16[16,400,128]{2,1,0:T(8,128)(2,1)S(1)}, u32[]{:S(2)}, u32[]{:S(2)}) async-start(bf16[16,400,128]{2,1,0:T(8,128)(2,1)} %get-tuple-element.29), calls=%async_computation.1 | async-start | bytes 3276800 | tf_op jit(solution)/shard_map/all_to_all | solution.py:452
  54.8 0.7 collective-permute-start
  55.5 1.3 collective-permute-start.1
  56.8 0.7 collective-permute-start.2
  57.5 2.7 %collective-permute-start.3 = (bf16[272,128]{1,0:T(8,128)(2,1)S(1)}, bf16[272,128]{1,0:T(8,128)(2,1)S(1)}, u32[]{:S(2)}, u32[]{:S(2)}) collective-permute-start(bf16[272,128]{1,0:T(8,128)(2,1)S(1)} %get-tuple-element.28), channel_id=1, source_target_pairs={{0,16},{16,32},{32,48},{48,64},{64,80},{80,96},{96,112},{112,128},... | collective-permute-start | bytes 208904 | tf_op jit(solution)/shard_map/ppermute | solution.py:487
  60.2 2.9 %shard_map.97 = (f32[1024,128]{1,0:T(8,128)}, f32[1024,128]{1,0:T(8,128)}, f32[1024,128]{1,0:T(8,128)}) custom-call(s32[1]{0:T(128)} %bitcast.pos, bf16[16,272,128]{2,1,0:T(8,128)(2,1)S(1)} %all-to-all-done.x, f32[1,1024]{1,0:T(1,128)S(1)} %copy-done), custom_call_target="tpu_custom_call" | custom-call | flops 536870912 | bytes 2097152 | tf_op jit(solution)/shard_map/pallas_call | solution.py:500
  63.1 0.0 collective-permute-done
  63.1 25.8 %collective-permute-done.1 = bf16[2,272,128]{2,1,0:T(8,128)(2,1)S(1)} collective-permute-done((bf16[2,272,128]{2,1,0:T(8,128)(2,1)S(1)}, bf16[2,272,128]{2,1,0:T(8,128)(2,1)S(1)}, u32[]{:S(2)}, u32[]{:S(2)}) %collective-permute-start.1) | collective-permute-done | bytes 139296 | tf_op jit(solution)/shard_map/ppermute | solution.py:493
  89.0 0.0 collective-permute-done.2
  89.0 5.3 %collective-permute-done.3.halo = bf16[272,128]{1,0:T(8,128)(2,1)S(1)} collective-permute-done((bf16[272,128]{1,0:T(8,128)(2,1)S(1)}, bf16[272,128]{1,0:T(8,128)(2,1)S(1)}, u32[]{:S(2)}, u32[]{:S(2)}) %collective-permute-start.3) | collective-permute-done | bytes 69664 | tf_op jit(solution)/shard_map/ppermute | solution.py:487
  94.3 0.0 all-to-all-done.1.y
  94.3 1.9 %collective-permute-start.4 = (bf16[2,272,128]{2,1,0:T(8,128)(2,1)S(1)}, bf16[2,272,128]{2,1,0:T(8,128)(2,1)S(1)}, u32[]{:S(2)}, u32[]{:S(2)}) collective-permute-start(bf16[2,272,128]{2,1,0:T(8,128)(2,1)S(1)} %add_add_fusion.1), channel_id=1, source_target_pairs={{0,16},{64,80},{128,144},{192,208},{1,17},{65,81},{129,145},{193,2... | collective-permute-start | bytes 417800 | tf_op jit(solution)/shard_map/ppermute | solution.py:493
  96.3 1.3 collective-permute-start.5
  97.6 2.3 %collective-permute-start.6 = (bf16[2,272,128]{2,1,0:T(8,128)(2,1)S(1)}, bf16[2,272,128]{2,1,0:T(8,128)(2,1)S(1)}, u32[]{:S(2)}, u32[]{:S(2)}) collective-permute-start(bf16[2,272,128]{2,1,0:T(8,128)(2,1)S(1)} %add_add_fusion.1), channel_id=1, source_target_pairs={{0,48},{64,112},{128,176},{192,240},{1,49},{65,113},{129,177},{193... | collective-permute-start | bytes 417800 | tf_op jit(solution)/shard_map/ppermute | solution.py:493
  99.8 8.2 %shard_map.98 = (f32[1024,128]{1,0:T(8,128)}, f32[1024,128]{1,0:T(8,128)}, bf16[16,192,128]{2,1,0:T(8,128)(2,1)}) custom-call(s32[32,128]{1,0:T(8,128)S(1)} %shard_map.94.table, bf16[16,272,128]{2,1,0:T(8,128)(2,1)S(1)} %all-to-all-done.x, bf16[16,400,128]{2,1,0:T(8,128)(2,1)S(1)} %all-to-all-done.1.y), custom_call_target="tpu_custom_call" | custom-call | flops 536870912 | bytes 4194304 | tf_op jit(solution)/shard_map/pallas_call | solution.py:511
  108.1 0.0 collective-permute-done.4
  108.1 0.0 collective-permute-done.5
  108.2 7.8 %all-to-all-start.2 = ((bf16[16,192,128]{2,1,0:T(8,128)(2,1)}), bf16[16,192,128]{2,1,0:T(8,128)(2,1)S(1)}, u32[]{:S(2)}, u32[]{:S(2)}) async-start(bf16[16,192,128]{2,1,0:T(8,128)(2,1)} %get-tuple-element.46), calls=%async_computation.2 | async-start | bytes 1572864 | tf_op jit(solution)/shard_map/all_to_all | solution.py:452
  116.0 4.2 %shard_map.99 = (f32[1024,128]{1,0:T(8,128)S(1)}, f32[1024,128]{1,0:T(8,128)S(1)}, f32[1024,128]{1,0:T(8,128)S(1)}, f32[3,128,128]{2,1,0:T(8,128)S(1)}, bf16[3,1...) custom-call(s32[1]{0:T(128)} %bitcast.pos, bf16[16,272,128]{2,1,0:T(8,128)(2,1)S(1)} %all-to-all-done.x, ...), custom_call_target="tpu_custom_call" | custom-call | flops 536870912 | bytes 4194304 | tf_op jit(solution)/shard_map/pallas_call | solution.py:522
  120.2 1.3 collective-permute-start.10
  121.5 1.3 collective-permute-start.8
  122.8 1.3 collective-permute-start.9
  124.1 5.0 %collective-permute-done.10 = bf16[3,128,128]{2,1,0:T(8,128)(2,1)S(1)} collective-permute-done((bf16[3,128,128]{2,1,0:T(8,128)(2,1)S(1)}, bf16[3,128,128]{2,1,0:T(8,128)(2,1)S(1)}, u32[]{:S(2)}, u32[]{:S(2)}) %collective-permute-start.10) | collective-permute-done | bytes 98336 | tf_op jit(solution)/shard_map/ppermute | solution.py:534
  129.1 0.0 collective-permute-done.8
  129.1 2.4 %collective-permute-done.9 = bf16[3,128,128]{2,1,0:T(8,128)(2,1)S(1)} collective-permute-done((bf16[3,128,128]{2,1,0:T(8,128)(2,1)S(1)}, bf16[3,128,128]{2,1,0:T(8,128)(2,1)S(1)}, u32[]{:S(2)}, u32[]{:S(2)}) %collective-permute-start.9) | collective-permute-done | bytes 98336 | tf_op jit(solution)/shard_map/ppermute | solution.py:534
  131.5 0.1 fusion
  131.6 0.7 collective-permute-start.11
  132.3 2.6 %collective-permute-start.12 = (bf16[3,128,128]{2,1,0:T(8,128)(2,1)S(1)}, bf16[3,128,128]{2,1,0:T(8,128)(2,1)S(1)}, u32[]{:S(2)}, u32[]{:S(2)}) collective-permute-start(bf16[3,128,128]{2,1,0:T(8,128)(2,1)S(1)} %fusion), channel_id=1, source_target_pairs={{128,0},{129,1},{130,2},{131,3},{132,4},{133,5},{134,6},{135,7},{1... | collective-permute-start | bytes 294920 | tf_op jit(solution)/shard_map/ppermute | solution.py:534
  134.9 0.7 collective-permute-start.13
  135.6 1.9 %collective-permute-start.7 = (bf16[192,128]{1,0:T(8,128)(2,1)S(1)}, bf16[192,128]{1,0:T(8,128)(2,1)S(1)}, u32[]{:S(2)}, u32[]{:S(2)}) collective-permute-start(bf16[192,128]{1,0:T(8,128)(2,1)S(1)} %get-tuple-element.47), channel_id=1, source_target_pairs={{16,0},{32,16},{48,32},{64,48},{80,64},{96,80},{112,96},{128,112},... | collective-permute-start | bytes 147464 | tf_op jit(solution)/shard_map/ppermute | solution.py:530
  137.5 2.7 %shard_map.100 = (bf16[16,192,128]{2,1,0:T(8,128)(2,1)}, f32[1024,128]{1,0:T(8,128)S(1)}, f32[384,128]{1,0:T(8,128)S(1)}) custom-call(f32[1024,128]{1,0:T(8,128)S(1)} %get-tuple-element.36.dq_g, f32[1024,128]{1,0:T(8,128)S(1)} %get-tuple-element.37.dk_g, f32[1024,128]{1,0:T(8,128)S(1)} %get-tuple-element.38.dv_g, f32[1024,128]{1,0:T(8,128)} %get-tuple-element.39.dq_w, ...), custom_call_target="tpu_custom_call" | custom-call | flops 16777216 | bytes 4194304 | tf_op jit(solution)/shard_map/pallas_call | solution.py:537
  140.2 0.0 collective-permute-done.12
  140.2 0.0 collective-permute-done.13
  140.2 0.1 convert_add_fusion.gtot
  140.3 1.3 collective-permute-done.7.hback
  141.5 0.0 all-to-all-done.2.z
  141.5 2.1 %shard_map.101 = bf16[16,192,128]{2,1,0:T(8,128)(2,1)} custom-call(s32[1]{0:T(128)} %bitcast.pos, s32[32,128]{1,0:T(8,128)S(1)} %shard_map.94.table, f32[1024,128]{1,0:T(8,128)S(1)} %get-tuple-element.44.dq, f32[384,128]{1,0:T(8,128)S(1)} %get-tuple-element.45.edge, bf16[16,192,128]{2,1,0:T(8,128)(2,1)S(1)} %all-to-all-done.2.z, ...), custom_call_target="tpu_custom_call", output_to_operand_aliasing={{}: (7, {})} | custom-call | bytes 4194304 | tf_op jit(solution)/shard_map/pallas_call | solution.py:546
  143.6 29.6 %all_to_all.20.w = bf16[16,192,128]{2,1,0:T(8,128)(2,1)S(1)} all-to-all(bf16[16,192,128]{2,1,0:T(8,128)(2,1)} %shard_map.101), channel_id=1, replica_groups=mesh['seq'=16,'head'=16] {'head'}, dimensions={0} | all-to-all | bytes 1572864 | tf_op jit(solution)/shard_map/all_to_all | solution.py:452
  173.2 1.1 shard_map.102
  (6 shorter events, 0.1 us)
Async XLA Ops:
  3.2 9.3 %copy-start.1 = (s32[256,3]{0,1:T(4,128)S(1)}, s32[256,3]{0,1:T(4,128)}, u32[]{:S(2)}) copy-start(s32[256,3]{0,1:T(4,128)} %param.13) | copy-start | bytes 9220
  3.2 42.3 %copy-start = (f32[1,1024]{1,0:T(1,128)S(1)}, f32[1,1024]{1,0:T(1,128)}, u32[]{:S(2)}) copy-start(f32[1,1024]{1,0:T(1,128)} %lse.5) | copy-start | bytes 12292
  3.2 42.3 %all-to-all-start = ((bf16[16,272,128]{2,1,0:T(8,128)(2,1)}), bf16[16,272,128]{2,1,0:T(8,128)(2,1)S(1)}, u32[]{:S(2)}, u32[]{:S(2)}) async-start(bf16[16,272,128]{2,1,0:T(8,128)(2,1)} %shard_map.95), calls=%async_computation | async-start | bytes 2228224 | tf_op jit(solution)/shard_map/all_to_all | solution.py:452
  47.9 46.4 %all-to-all-start.1 = ((bf16[16,400,128]{2,1,0:T(8,128)(2,1)}), bf16[16,400,128]{2,1,0:T(8,128)(2,1)S(1)}, u32[]{:S(2)}, u32[]{:S(2)}) async-start(bf16[16,400,128]{2,1,0:T(8,128)(2,1)} %get-tuple-element.29), calls=%async_computation.1 | async-start | bytes 3276800 | tf_op jit(solution)/shard_map/all_to_all | solution.py:452
  54.8 8.3 %collective-permute-start = (bf16[2,272,128]{2,1,0:T(8,128)(2,1)S(1)}, bf16[2,272,128]{2,1,0:T(8,128)(2,1)S(1)}, u32[]{:S(2)}, u32[]{:S(2)}) collective-permute-start(bf16[2,272,128]{2,1,0:T(8,128)(2,1)S(1)} %get-tuple-element.27), channel_id=1, source_target_pairs={{0,64},{1,65},{2,66},{3,67},{4,68},{5,69},{6,70},{7,71},{8,72},{9,... | collective-permute-start | bytes 417800 | tf_op jit(solution)/shard_map/ppermute | solution.py:493
  55.5 33.5 %collective-permute-start.1 = (bf16[2,272,128]{2,1,0:T(8,128)(2,1)S(1)}, bf16[2,272,128]{2,1,0:T(8,128)(2,1)S(1)}, u32[]{:S(2)}, u32[]{:S(2)}) collective-permute-start(bf16[2,272,128]{2,1,0:T(8,128)(2,1)S(1)} %get-tuple-element.27), channel_id=1, source_target_pairs={{0,128},{1,129},{2,130},{3,131},{4,132},{5,133},{6,134},{7,135},{8... | collective-permute-start | bytes 417800 | tf_op jit(solution)/shard_map/ppermute | solution.py:493
  56.8 32.2 %collective-permute-start.2 = (bf16[2,272,128]{2,1,0:T(8,128)(2,1)S(1)}, bf16[2,272,128]{2,1,0:T(8,128)(2,1)S(1)}, u32[]{:S(2)}, u32[]{:S(2)}) collective-permute-start(bf16[2,272,128]{2,1,0:T(8,128)(2,1)S(1)} %get-tuple-element.27), channel_id=1, source_target_pairs={{0,192},{1,193},{2,194},{3,195},{4,196},{5,197},{6,198},{7,199},{8... | collective-permute-start | bytes 417800 | tf_op jit(solution)/shard_map/ppermute | solution.py:493
  57.5 36.9 %collective-permute-start.3 = (bf16[272,128]{1,0:T(8,128)(2,1)S(1)}, bf16[272,128]{1,0:T(8,128)(2,1)S(1)}, u32[]{:S(2)}, u32[]{:S(2)}) collective-permute-start(bf16[272,128]{1,0:T(8,128)(2,1)S(1)} %get-tuple-element.28), channel_id=1, source_target_pairs={{0,16},{16,32},{32,48},{48,64},{64,80},{80,96},{96,112},{112,128},... | collective-permute-start | bytes 208904 | tf_op jit(solution)/shard_map/ppermute | solution.py:487
  94.3 13.8 %collective-permute-start.4 = (bf16[2,272,128]{2,1,0:T(8,128)(2,1)S(1)}, bf16[2,272,128]{2,1,0:T(8,128)(2,1)S(1)}, u32[]{:S(2)}, u32[]{:S(2)}) collective-permute-start(bf16[2,272,128]{2,1,0:T(8,128)(2,1)S(1)} %add_add_fusion.1), channel_id=1, source_target_pairs={{0,16},{64,80},{128,144},{192,208},{1,17},{65,81},{129,145},{193,2... | collective-permute-start | bytes 417800 | tf_op jit(solution)/shard_map/ppermute | solution.py:493
  96.3 11.8 %collective-permute-start.5 = (bf16[2,272,128]{2,1,0:T(8,128)(2,1)S(1)}, bf16[2,272,128]{2,1,0:T(8,128)(2,1)S(1)}, u32[]{:S(2)}, u32[]{:S(2)}) collective-permute-start(bf16[2,272,128]{2,1,0:T(8,128)(2,1)S(1)} %add_add_fusion.1), channel_id=1, source_target_pairs={{0,32},{64,96},{128,160},{192,224},{1,33},{65,97},{129,161},{193,2... | collective-permute-start | bytes 417800 | tf_op jit(solution)/shard_map/ppermute | solution.py:493
  97.6 10.5 %collective-permute-start.6 = (bf16[2,272,128]{2,1,0:T(8,128)(2,1)S(1)}, bf16[2,272,128]{2,1,0:T(8,128)(2,1)S(1)}, u32[]{:S(2)}, u32[]{:S(2)}) collective-permute-start(bf16[2,272,128]{2,1,0:T(8,128)(2,1)S(1)} %add_add_fusion.1), channel_id=1, source_target_pairs={{0,48},{64,112},{128,176},{192,240},{1,49},{65,113},{129,177},{193... | collective-permute-start | bytes 417800 | tf_op jit(solution)/shard_map/ppermute | solution.py:493
  108.2 33.4 %all-to-all-start.2 = ((bf16[16,192,128]{2,1,0:T(8,128)(2,1)}), bf16[16,192,128]{2,1,0:T(8,128)(2,1)S(1)}, u32[]{:S(2)}, u32[]{:S(2)}) async-start(bf16[16,192,128]{2,1,0:T(8,128)(2,1)} %get-tuple-element.46), calls=%async_computation.2 | async-start | bytes 1572864 | tf_op jit(solution)/shard_map/all_to_all | solution.py:452
  120.2 8.9 %collective-permute-start.10 = (bf16[3,128,128]{2,1,0:T(8,128)(2,1)S(1)}, bf16[3,128,128]{2,1,0:T(8,128)(2,1)S(1)}, u32[]{:S(2)}, u32[]{:S(2)}) collective-permute-start(bf16[3,128,128]{2,1,0:T(8,128)(2,1)S(1)} %get-tuple-element.49), channel_id=1, source_target_pairs={{48,0},{112,64},{176,128},{240,192},{49,1},{113,65},{177,129},{241... | collective-permute-start | bytes 294920 | tf_op jit(solution)/shard_map/ppermute | solution.py:534
  121.5 7.6 %collective-permute-start.8 = (bf16[3,128,128]{2,1,0:T(8,128)(2,1)S(1)}, bf16[3,128,128]{2,1,0:T(8,128)(2,1)S(1)}, u32[]{:S(2)}, u32[]{:S(2)}) collective-permute-start(bf16[3,128,128]{2,1,0:T(8,128)(2,1)S(1)} %get-tuple-element.49), channel_id=1, source_target_pairs={{16,0},{80,64},{144,128},{208,192},{17,1},{81,65},{145,129},{209,1... | collective-permute-start | bytes 294920 | tf_op jit(solution)/shard_map/ppermute | solution.py:534
  122.8 8.7 %collective-permute-start.9 = (bf16[3,128,128]{2,1,0:T(8,128)(2,1)S(1)}, bf16[3,128,128]{2,1,0:T(8,128)(2,1)S(1)}, u32[]{:S(2)}, u32[]{:S(2)}) collective-permute-start(bf16[3,128,128]{2,1,0:T(8,128)(2,1)S(1)} %get-tuple-element.49), channel_id=1, source_target_pairs={{32,0},{96,64},{160,128},{224,192},{33,1},{97,65},{161,129},{225,1... | collective-permute-start | bytes 294920 | tf_op jit(solution)/shard_map/ppermute | solution.py:534
  131.6 8.6 %collective-permute-start.11 = (bf16[3,128,128]{2,1,0:T(8,128)(2,1)S(1)}, bf16[3,128,128]{2,1,0:T(8,128)(2,1)S(1)}, u32[]{:S(2)}, u32[]{:S(2)}) collective-permute-start(bf16[3,128,128]{2,1,0:T(8,128)(2,1)S(1)} %fusion), channel_id=1, source_target_pairs={{64,0},{65,1},{66,2},{67,3},{68,4},{69,5},{70,6},{71,7},{72,8},{73... | collective-permute-start | bytes 294920 | tf_op jit(solution)/shard_map/ppermute | solution.py:534
  132.3 7.9 %collective-permute-start.12 = (bf16[3,128,128]{2,1,0:T(8,128)(2,1)S(1)}, bf16[3,128,128]{2,1,0:T(8,128)(2,1)S(1)}, u32[]{:S(2)}, u32[]{:S(2)}) collective-permute-start(bf16[3,128,128]{2,1,0:T(8,128)(2,1)S(1)} %fusion), channel_id=1, source_target_pairs={{128,0},{129,1},{130,2},{131,3},{132,4},{133,5},{134,6},{135,7},{1... | collective-permute-start | bytes 294920 | tf_op jit(solution)/shard_map/ppermute | solution.py:534
  134.9 5.3 %collective-permute-start.13 = (bf16[3,128,128]{2,1,0:T(8,128)(2,1)S(1)}, bf16[3,128,128]{2,1,0:T(8,128)(2,1)S(1)}, u32[]{:S(2)}, u32[]{:S(2)}) collective-permute-start(bf16[3,128,128]{2,1,0:T(8,128)(2,1)S(1)} %fusion), channel_id=1, source_target_pairs={{192,0},{193,1},{194,2},{195,3},{196,4},{197,5},{198,6},{199,7},{2... | collective-permute-start | bytes 294920 | tf_op jit(solution)/shard_map/ppermute | solution.py:534
  135.6 6.0 %collective-permute-start.7 = (bf16[192,128]{1,0:T(8,128)(2,1)S(1)}, bf16[192,128]{1,0:T(8,128)(2,1)S(1)}, u32[]{:S(2)}, u32[]{:S(2)}) collective-permute-start(bf16[192,128]{1,0:T(8,128)(2,1)S(1)} %get-tuple-element.47), channel_id=1, source_target_pairs={{16,0},{32,16},{48,32},{64,48},{80,64},{96,80},{112,96},{128,112},... | collective-permute-start | bytes 147464 | tf_op jit(solution)/shard_map/ppermute | solution.py:530

commit v4 on v3

--- a/solution.py
+++ b/solution.py
@@ -178,6 +178,40 @@
         pt = jnp.where(keep, pt, 0.0)
     dst = (pt * (nt(v, g) - delta)).astype(BF16)
     return tn(dst, k), nn(dst, q), nn(pt.astype(BF16), g)
+
+
+def staged(tiles, scores, probs, lows):
+    depth = 3
+    held = {}
+    for step in range(len(tiles) + 2):
+        if step < len(tiles):
+            tile = tiles[step]()
+            held[step] = tile
+            shape = (tile["k"].shape[0], tile["q"].shape[0])
+            slot = step % depth
+            view = (slot, slice(0, shape[0]), slice(0, shape[1]))
+            scores[view] = nt(tile["k"], tile["q"])
+            probs[view] = nt(tile["v"], tile["g"])
+        n = step - 1
+        if 0 <= n < len(tiles):
+            tile = held[n]
+            shape = (tile["k"].shape[0], tile["q"].shape[0])
+            view = (n % depth, slice(0, shape[0]), slice(0, shape[1]))
+            pt = jnp.exp(scores[view] * FACTOR - tile["norm"])
+            if tile.get("keep") is not None:
+                pt = jnp.where(tile["keep"], pt, 0.0)
+            low_view = (n % depth, 0) + view[1:]
+            lows[low_view] = pt.astype(BF16)
+            low_view = (n % depth, 1) + view[1:]
+            lows[low_view] = (pt * (probs[view] - tile["delta"])).astype(BF16)
+        n = step - 2
+        if 0 <= n < len(tiles):
+            tile = held.pop(n)
+            shape = (tile["k"].shape[0], tile["q"].shape[0])
+            cut = (slice(0, shape[0]), slice(0, shape[1]))
+            pt = lows[(n % depth, 0) + cut]
+            dst = lows[(n % depth, 1) + cut]
+            tile["use"](tn(dst, tile["k"]), nn(dst, tile["q"]), nn(pt, tile["g"]))
 
 
 def two(ext, a):
@@ -238,51 +272,55 @@
         push.wait()
 
 
-def rand_body(table, x, y, dk_out, dv_out, z, dk, dv, buf, sem, acc_sem):
+def rand_body(table, x, y, dk_out, dv_out, z, dk, dv, buf, sem, acc_sem, scores, probs, lows):
     dk[...] = jnp.zeros_like(dk)
     dv[...] = jnp.zeros_like(dv)
     sub = lax.broadcasted_iota(jnp.int32, (HD, HD), 0)
     lane = lax.broadcasted_iota(jnp.int32, (HD, HD), 1)
     keep = (sub >> 6) == (lane >> 6)
     left = lax.broadcasted_iota(jnp.int32, (1, HD), 1) < 64
-    per_step = 4
-
-    def step(i, carry):
-        t0 = i * per_step
-        exts = [y[t0 + c, 384:400].astype(F32) for c in range(per_step)]
-        entries = [(c, r) for c in range(per_step) for r in range(RAND)]
-        done = []
-        for n in range(0, len(entries), 2):
-            pair = entries[n : n + 2]
-
+    entries = [(t, r) for t in range(NB) for r in range(RAND)]
+
+    def tile_of(n):
+        pair = entries[2 * n : 2 * n + 2]
+
+        def make():
             def both(base):
                 return jnp.concatenate(
-                    [y[t0 + c, base + r * 64 : base + r * 64 + 64] for c, r in pair], axis=0
+                    [y[t, base + r * 64 : base + r * 64 + 64] for t, r in pair], axis=0
                 )
 
             def row(a):
-                one, other = (two(exts[c], 4 * r + a) for c, r in pair)
+                one, other = (two(y[t, 384:400].astype(F32), 4 * r + a) for t, r in pair)
                 return jnp.where(left, one, other)
 
-            js = [table[NB + t0 + c, r] for c, r in pair]
-            k = jnp.concatenate([x[j, 64:128] for j in js], axis=0)
-            v = jnp.concatenate([x[j, 128:192] for j in js], axis=0)
-            pq, pk, pv = grads(both(0), both(192), row(2), row(0), k, v, keep)
-            low = (pq * FACTOR).astype(BF16)
-            for m, (c, r) in enumerate(pair):
-                buf[t0 + c, r * 64 : r * 64 + 64] = low[m * 64 : m * 64 + 64]
-            done.append((js, pk, pv))
-        for c in range(per_step):
-            t = t0 + c
-            pltpu.make_async_copy(buf.at[t], z.at[t], sem.at[t]).start()
-        for js, pk, pv in done:
-            for m, j in enumerate(js):
-                span = pl.ds(pl.multiple_of(j * 64, 64), 64)
-                dk[span] = dk[span] + pk[m * 64 : m * 64 + 64]
-                dv[span] = dv[span] + pv[m * 64 : m * 64 + 64]
-        return carry
-
-    lax.fori_loop(0, NB // per_step, step, 0)
+            js = [table[NB + t, r] for t, r in pair]
+
+            def use(pq, pk, pv):
+                low = (pq * FACTOR).astype(BF16)
+                for m, (t, r) in enumerate(pair):
+                    rows = slice(m * 64, m * 64 + 64)
+                    buf[t, r * 64 : r * 64 + 64] = low[rows]
+                    span = pl.ds(pl.multiple_of(js[m] * 64, 64), 64)
+                    dk[span] = dk[span] + pk[rows]
+                    dv[span] = dv[span] + pv[rows]
+                    if r == RAND - 1:
+                        pltpu.make_async_copy(buf.at[t], z.at[t], sem.at[t]).start()
+
+            return dict(
+                q=both(0),
+                g=both(192),
+                k=jnp.concatenate([x[j, 64:128] for j in js], axis=0),
+                v=jnp.concatenate([x[j, 128:192] for j in js], axis=0),
+                norm=row(2),
+                delta=row(0),
+                keep=keep,
+                use=use,
+            )
+
+        return make
+
+    staged([tile_of(n) for n in range(len(entries) // 2)], scores, probs, lows)
     drains = []
     for n in range(4):
         span = pl.ds(n * 256, 256)
@@ -300,7 +338,9 @@
     lax.fori_loop(0, NB, finish, 0)
 
 
-def global_body(pos, x, lse, glob, halo, dq, dk, dv, gpart, glow, hback):
+def global_body(
+    pos, x, lse, glob, halo, dq, dk, dv, gpart, glow, hback, sums, scores, probs, lows
+):
     here = pos[0]
     lse_all = masked_norms(pos, lse)
     gq, gk, gv, gg = (joined(glob, a, 0, GLOB) for a in range(4))
@@ -308,22 +348,47 @@
     ext1 = glob[1, 256:272].astype(F32)
     gdelta = jnp.concatenate([two(ext0, 0)[:, 0:64], two(ext1, 0)[:, 0:64]], axis=1)
     gnorm = jnp.concatenate([two(ext0, 2)[:, 0:64], two(ext1, 2)[:, 0:64]], axis=1)
-    gq_sum = jnp.zeros((HD, HD), F32)
-    gk_sum = jnp.zeros((HD, HD), F32)
-    gv_sum = jnp.zeros((HD, HD), F32)
-    for i in range(NB // 2):
-        b = 2 * i
-        span = slice(b * 64, b * 64 + 128)
-        q2, k2, v2, g2 = (joined(x, a, b, b + 2) for a in range(4))
-        fq, fk, fv = grads(gq, gg, gnorm, gdelta, k2, v2)
-        gq_sum = gq_sum + fq
-        dk[span] = fk
-        dv[span] = fv
-        norm = lse_all[:, i * HD : (i + 1) * HD]
-        wq, wk, wv = grads(q2, g2, norm, pair_delta(x, b), gk, gv)
-        dq[span] = wq
-        gk_sum = gk_sum + wk
-        gv_sum = gv_sum + wv
+    sums[...] = jnp.zeros_like(sums)
+    tiles = []
+    for i in range(4):
+        b = 4 * i
+        span = slice(b * 64, b * 64 + 256)
+
+        def down(b=b, span=span):
+            def use(fq, fk, fv):
+                sums[0] = sums[0] + fq
+                dk[span] = fk
+                dv[span] = fv
+
+            return dict(
+                q=gq,
+                g=gg,
+                k=joined(x, 1, b, b + 4),
+                v=joined(x, 2, b, b + 4),
+                norm=gnorm,
+                delta=gdelta,
+                use=use,
+            )
+
+        def across(b=b, span=span):
+            def use(wq, wk, wv):
+                dq[span] = wq
+                sums[1] = sums[1] + wk
+                sums[2] = sums[2] + wv
+
+            return dict(
+                q=joined(x, 0, b, b + 4),
+                g=joined(x, 3, b, b + 4),
+                k=gk,
+                v=gv,
+                norm=lse_all[:, span],
+                delta=jnp.concatenate([pair_delta(x, b), pair_delta(x, b + 2)], axis=1),
+                use=use,
+            )
+
+        tiles += [down, across]
+    staged(tiles, scores, probs, lows)
+    gq_sum, gk_sum, gv_sum = sums[0], sums[1], sums[2]
     hext = halo[256:272].astype(F32)
     hdelta = two(hext, 0)[:, 0:64]
     hnorm = jnp.where(here == 0, OFF, two(hext, 2)[:, 0:64])
@@ -515,7 +580,16 @@
         (HB,) * 3,
         flops=1 << 29,
         nbytes=4 << 20,
-        scratch=[grid, grid, pltpu.VMEM((NB, RAND * BLK, HD), BF16), dma((NB,)), dma((8,))],
+        scratch=[
+            grid,
+            grid,
+            pltpu.VMEM((NB, RAND * BLK, HD), BF16),
+            dma((NB,)),
+            dma((8,)),
+            pltpu.VMEM((3, HD, HD), F32),
+            pltpu.VMEM((3, HD, HD), F32),
+            pltpu.VMEM((3, 2, HD, HD), BF16),
+        ],
     )(table, x, y)
     glob, z = lax.optimization_barrier((glob, z))
     z = exchange(z, "seq")
@@ -526,14 +600,23 @@
         (VM,) * 6,
         flops=1 << 29,
         nbytes=4 << 20,
+        scratch=[
+            pltpu.VMEM((3, HD, HD), F32),
+            pltpu.VMEM((3, 256, 256), F32),
+            pltpu.VMEM((3, 256, 256), F32),
+            pltpu.VMEM((3, 2, 256, 256), BF16),
+        ],
     )(pos, x, logsumexp, glob, halo)
     hback = lax.ppermute(hback, "seq", [(s, s - 1) for s in range(1, groups)])
-    for reach in (1, 4):
-        span = range(0, groups, 4) if reach == 1 else (0,)
+
+    def collect(gpart, glow, reach):
+        span = range(0, groups, 4 * reach)
         for n in (1, 2, 3):
             moved = lax.ppermute(glow, "seq", [(s + n * reach, s) for s in span])
             gpart = gpart + moved.astype(F32)
-        glow = gpart.astype(BF16)
+        return gpart
+
+    gpart = collect(gpart, glow, 1)
     w, dq, edge = call(
         gather_body,
         (far((NB, 3 * BLK, HD)), acc, struct((len(EDGES) * 2 * BLK, HD), F32)),
@@ -543,6 +626,8 @@
         nbytes=4 << 20,
         scratch=[grid] * 5 + [pltpu.VMEM((NB, 2 * BLK, HD), BF16), dma((5,)), dma((NB,))],
     )(*map(hold, (dq_g, dk_g, dv_g)), *map(keep_far, (dq_w, dk_w, dv_w, dk_r, dv_r)))
+    gpart, w, dq, edge, hback = lax.optimization_barrier((gpart, w, dq, edge, hback))
+    gpart = collect(gpart, gpart.astype(BF16), 4)
     w = call(
         merge_body,
         far((NB, 3 * BLK, HD)),

time: 175 us -> 169 us (0.966)
  the two profiles are of different devices: /device:TPU:64 before, /device:TPU:32 now
where the time goes in v4:
time: 169 us; the launch traced here: 167 us
  waiting for transfers between devices  69.5 us (41%)
  starting transfers between devices  49.4 us (29%)
  blocking collectives  26.9 us (16%)
  Pallas kernels  20 us (12%)
    all_to_all x3, waiting for transfers between devices, exchange(): return lax.all_to_all(x, axis, split_axis=0, concat_axis=0, tiled=True)  37.6 us
    ppermute x6, waiting for transfers between devices, spread(): lax.ppermute(source, 'seq', [(s, s + n * reach) for s in starts])  27.5 us
    all_to_all x1, blocking collectives, exchange(): return lax.all_to_all(x, axis, split_axis=0, concat_axis=0, tiled=True)  26.9 us
    all_to_all x3, starting transfers between devices, exchange(): return lax.all_to_all(x, axis, split_axis=0, concat_axis=0, tiled=True)  26.1 us
    ppermute x6, starting transfers between devices, collect(): moved = lax.ppermute(glow, 'seq', [(s + n * reach, s) for s in span])  9.99 us
    ppermute x6, starting transfers between devices, spread(): lax.ppermute(source, 'seq', [(s, s + n * reach) for s in starts])  6.5 us
    pallas_call x1, Pallas kernels, per_device(): call(rand_body, (far_acc, far_acc, far((NB, RAND * BLK, HD))), [SM, VM, V...  4.55 us
    ppermute x6, waiting for transfers between devices, collect(): moved = lax.ppermute(glow, 'seq', [(s + n * reach, s) for s in span])  4.42 us
  transfers between devices with their start and end apart: 17, of which 5 were waited for; matrix products, arithmetic and copies ran while one was open for 0% of the time, Pallas kernels for 7%

profile of v4, /device:TPU:32, one launch (start us, length us, event | category | flops | bytes accessed | tf_op | source)
XLA Modules:
  0.0 167.1 jit_solution(6670133424921036210)
XLA Ops:
  0.6 2.5 %shard_map.95 = bf16[16,272,128]{2,1,0:T(8,128)(2,1)} custom-call(bf16[64,2048]{1,0:T(8,128)(2,1)} %q.1, bf16[64,2048]{1,0:T(8,128)(2,1)} %k.1, bf16[64,2048]{1,0:T(8,128)(2,1)} %v.1, bf16[64,2048]{1,0:T(8,128)(2,1)} %o.1, bf16[64,2048]{1,0:T(8,128)(2,1)} %g.1), custom_call_target="tpu_custom_call" | custom-call | bytes 1310720 | tf_op jit(solution)/shard_map/pallas_call | solution.py:527
  3.2 0.0 copy-start.1
  3.2 0.0 copy-start
  3.2 10.1 %all-to-all-start = ((bf16[16,272,128]{2,1,0:T(8,128)(2,1)}), bf16[16,272,128]{2,1,0:T(8,128)(2,1)S(1)}, u32[]{:S(2)}, u32[]{:S(2)}) async-start(bf16[16,272,128]{2,1,0:T(8,128)(2,1)} %shard_map.95), calls=%async_computation | async-start | bytes 2228224 | tf_op jit(solution)/shard_map/all_to_all | solution.py:517
  13.4 0.1 copy.12
  13.5 0.1 reshape.13.entries
  13.6 0.2 shard_map.94.table
  13.9 32.5 %all-to-all-done.x = bf16[16,272,128]{2,1,0:T(8,128)(2,1)S(1)} async-done(((bf16[16,272,128]{2,1,0:T(8,128)(2,1)}), bf16[16,272,128]{2,1,0:T(8,128)(2,1)S(1)}, u32[]{:S(2)}, u32[]{:S(2)}) %all-to-all-start) | async-done | bytes 1114144 | tf_op jit(solution)/shard_map/all_to_all | solution.py:517
  46.4 2.5 %shard_map.96 = (bf16[16,400,128]{2,1,0:T(8,128)(2,1)}, bf16[272,128]{1,0:T(8,128)(2,1)S(1)}, bf16[2,272,128]{2,1,0:T(8,128)(2,1)S(1)}) custom-call(s32[1]{0:T(128)} %bitcast.pos, s32[32,128]{1,0:T(8,128)S(1)} %shard_map.94.table, bf16[16,272,128]{2,1,0:T(8,128)(2,1)S(1)} %all-to-all-done.x, f32[1,1024]{1,0:T(1,128)S(1)} %copy-done), custom_call_target="tpu_custom_call" | custom-call | bytes 3145728 | tf_op jit(solution)/shard_map/pallas_call | solution.py:539
  48.8 6.4 %all-to-all-start.1 = ((bf16[16,400,128]{2,1,0:T(8,128)(2,1)}), bf16[16,400,128]{2,1,0:T(8,128)(2,1)S(1)}, u32[]{:S(2)}, u32[]{:S(2)}) async-start(bf16[16,400,128]{2,1,0:T(8,128)(2,1)} %get-tuple-element.34), calls=%async_computation.1 | async-start | bytes 3276800 | tf_op jit(solution)/shard_map/all_to_all | solution.py:517
  55.3 0.7 collective-permute-start.2
  55.9 0.7 collective-permute-start.1
  56.6 1.3 collective-permute-start
  57.9 2.7 %collective-permute-start.3 = (bf16[272,128]{1,0:T(8,128)(2,1)S(1)}, bf16[272,128]{1,0:T(8,128)(2,1)S(1)}, u32[]{:S(2)}, u32[]{:S(2)}) collective-permute-start(bf16[272,128]{1,0:T(8,128)(2,1)S(1)} %get-tuple-element.33), channel_id=1, source_target_pairs={{0,16},{16,32},{32,48},{48,64},{64,80},{80,96},{96,112},{112,128},... | collective-permute-start | bytes 208904 | tf_op jit(solution)/shard_map/ppermute | solution.py:552
  60.7 2.9 %shard_map.97 = (f32[1024,128]{1,0:T(8,128)}, f32[1024,128]{1,0:T(8,128)}, f32[1024,128]{1,0:T(8,128)}) custom-call(s32[1]{0:T(128)} %bitcast.pos, bf16[16,272,128]{2,1,0:T(8,128)(2,1)S(1)} %all-to-all-done.x, f32[1,1024]{1,0:T(1,128)S(1)} %copy-done), custom_call_target="tpu_custom_call" | custom-call | flops 536870912 | bytes 2097152 | tf_op jit(solution)/shard_map/pallas_call | solution.py:565
  63.6 0.0 collective-permute-done.2
  63.6 0.0 collective-permute-done.1
  63.6 27.4 %collective-permute-done = bf16[2,272,128]{2,1,0:T(8,128)(2,1)S(1)} collective-permute-done((bf16[2,272,128]{2,1,0:T(8,128)(2,1)S(1)}, bf16[2,272,128]{2,1,0:T(8,128)(2,1)S(1)}, u32[]{:S(2)}, u32[]{:S(2)}) %collective-permute-start) | collective-permute-done | bytes 139296 | tf_op jit(solution)/shard_map/ppermute | solution.py:558
  91.1 0.0 collective-permute-done.3.halo
  91.1 5.1 %all-to-all-done.1.y = bf16[16,400,128]{2,1,0:T(8,128)(2,1)S(1)} async-done(((bf16[16,400,128]{2,1,0:T(8,128)(2,1)}), bf16[16,400,128]{2,1,0:T(8,128)(2,1)S(1)}, u32[]{:S(2)}, u32[]{:S(2)}) %all-to-all-start.1) | async-done | bytes 1638432 | tf_op jit(solution)/shard_map/all_to_all | solution.py:517
  96.2 1.3 collective-permute-start.6
  97.5 1.3 collective-permute-start.5
  98.8 1.3 collective-permute-start.4
  100.1 4.5 %shard_map.98 = (f32[1024,128]{1,0:T(8,128)}, f32[1024,128]{1,0:T(8,128)}, bf16[16,192,128]{2,1,0:T(8,128)(2,1)}) custom-call(s32[32,128]{1,0:T(8,128)S(1)} %shard_map.94.table, bf16[16,272,128]{2,1,0:T(8,128)(2,1)S(1)} %all-to-all-done.x, bf16[16,400,128]{2,1,0:T(8,128)(2,1)S(1)} %all-to-all-done.1.y), custom_call_target="tpu_custom_call" | custom-call | flops 536870912 | bytes 4194304 | tf_op jit(solution)/shard_map/pallas_call | solution.py:576
  104.6 0.0 collective-permute-done.6
  104.6 0.0 collective-permute-done.5
  104.6 0.0 collective-permute-done.4
  104.7 9.6 %all-to-all-start.2 = ((bf16[16,192,128]{2,1,0:T(8,128)(2,1)}), bf16[16,192,128]{2,1,0:T(8,128)(2,1)S(1)}, u32[]{:S(2)}, u32[]{:S(2)}) async-start(bf16[16,192,128]{2,1,0:T(8,128)(2,1)} %get-tuple-element.57), calls=%async_computation.2 | async-start | bytes 1572864 | tf_op jit(solution)/shard_map/all_to_all | solution.py:517
  114.3 1.5 shard_map.99
  115.7 1.3 collective-permute-start.9
  117.0 1.3 collective-permute-start.8
  118.3 1.3 collective-permute-start.7
  119.6 4.1 %collective-permute-start.10 = (bf16[192,128]{1,0:T(8,128)(2,1)S(1)}, bf16[192,128]{1,0:T(8,128)(2,1)S(1)}, u32[]{:S(2)}, u32[]{:S(2)}) collective-permute-start(bf16[192,128]{1,0:T(8,128)(2,1)S(1)} %get-tuple-element.54), channel_id=1, source_target_pairs={{16,0},{32,16},{48,32},{64,48},{80,64},{96,80},{112,96},{128,112},... | collective-permute-start | bytes 147464 | tf_op jit(solution)/shard_map/ppermute | solution.py:610
  123.7 2.7 %shard_map.100 = (bf16[16,192,128]{2,1,0:T(8,128)(2,1)}, f32[1024,128]{1,0:T(8,128)S(1)}, f32[384,128]{1,0:T(8,128)S(1)}) custom-call(f32[1024,128]{1,0:T(8,128)S(1)} %get-tuple-element.43.dq_g, f32[1024,128]{1,0:T(8,128)S(1)} %get-tuple-element.44.dk_g, f32[1024,128]{1,0:T(8,128)S(1)} %get-tuple-element.45.dv_g, f32[1024,128]{1,0:T(8,128)} %get-tuple-element.46.dq_w, ...), custom_call_target="tpu_custom_call" | custom-call | flops 16777216 | bytes 4194304 | tf_op jit(solution)/shard_map/pallas_call | solution.py:620
  126.3 0.4 collective-permute-done.9
  126.7 0.0 collective-permute-done.8
  126.7 0.0 collective-permute-done.7
  126.8 0.0 collective-permute-done.10.hback
  126.8 0.7 collective-permute-start.13
  127.5 0.7 collective-permute-start.12
  128.2 4.8 %collective-permute-start.11 = (bf16[3,128,128]{2,1,0:T(8,128)(2,1)S(1)}, bf16[3,128,128]{2,1,0:T(8,128)(2,1)S(1)}, u32[]{:S(2)}, u32[]{:S(2)}) collective-permute-start(bf16[3,128,128]{2,1,0:T(8,128)(2,1)S(1)} %convert_element_type.24), channel_id=1, source_target_pairs={{64,0},{65,1},{66,2},{67,3},{68,4},{69,5},{70,6},{71,7},{72,8},{73... | collective-permute-start | bytes 294920 | tf_op jit(solution)/shard_map/ppermute | solution.py:615
  133.0 0.0 collective-permute-done.13
  133.0 0.0 collective-permute-done.12
  133.0 4.0 %collective-permute-done.11 = bf16[3,128,128]{2,1,0:T(8,128)(2,1)S(1)} collective-permute-done((bf16[3,128,128]{2,1,0:T(8,128)(2,1)S(1)}, bf16[3,128,128]{2,1,0:T(8,128)(2,1)S(1)}, u32[]{:S(2)}, u32[]{:S(2)}) %collective-permute-start.11) | collective-permute-done | bytes 98336 | tf_op jit(solution)/shard_map/ppermute | solution.py:615
  137.0 0.0 all-to-all-done.2.z
  137.1 2.1 %shard_map.101 = bf16[16,192,128]{2,1,0:T(8,128)(2,1)} custom-call(s32[1]{0:T(128)} %bitcast.pos, s32[32,128]{1,0:T(8,128)S(1)} %shard_map.94.table, f32[1024,128]{1,0:T(8,128)S(1)} %get-tuple-element.55.dq, f32[384,128]{1,0:T(8,128)S(1)} %get-tuple-element.56.edge, bf16[16,192,128]{2,1,0:T(8,128)(2,1)S(1)} %all-to-all-done.2.z, ...), custom_call_target="tpu_custom_call", output_to_operand_aliasing={{}: (7, {})} | custom-call | bytes 4194304 | tf_op jit(solution)/shard_map/pallas_call | solution.py:631
  139.1 26.9 %all_to_all.20.w = bf16[16,192,128]{2,1,0:T(8,128)(2,1)S(1)} all-to-all(bf16[16,192,128]{2,1,0:T(8,128)(2,1)} %shard_map.101), channel_id=1, replica_groups=mesh['seq'=16,'head'=16] {'head'}, dimensions={0} | all-to-all | bytes 1572864 | tf_op jit(solution)/shard_map/all_to_all | solution.py:517
  166.1 1.1 shard_map.102
  (7 shorter events, 0.2 us)
Async XLA Ops:
  3.2 10.2 %copy-start.1 = (s32[256,3]{0,1:T(4,128)S(1)}, s32[256,3]{0,1:T(4,128)}, u32[]{:S(2)}) copy-start(s32[256,3]{0,1:T(4,128)} %param.13) | copy-start | bytes 9220
  3.2 43.2 %copy-start = (f32[1,1024]{1,0:T(1,128)S(1)}, f32[1,1024]{1,0:T(1,128)}, u32[]{:S(2)}) copy-start(f32[1,1024]{1,0:T(1,128)} %lse.5) | copy-start | bytes 12292
  3.2 43.2 %all-to-all-start = ((bf16[16,272,128]{2,1,0:T(8,128)(2,1)}), bf16[16,272,128]{2,1,0:T(8,128)(2,1)S(1)}, u32[]{:S(2)}, u32[]{:S(2)}) async-start(bf16[16,272,128]{2,1,0:T(8,128)(2,1)} %shard_map.95), calls=%async_computation | async-start | bytes 2228224 | tf_op jit(solution)/shard_map/all_to_all | solution.py:517
  48.8 47.3 %all-to-all-start.1 = ((bf16[16,400,128]{2,1,0:T(8,128)(2,1)}), bf16[16,400,128]{2,1,0:T(8,128)(2,1)S(1)}, u32[]{:S(2)}, u32[]{:S(2)}) async-start(bf16[16,400,128]{2,1,0:T(8,128)(2,1)} %get-tuple-element.34), calls=%async_computation.1 | async-start | bytes 3276800 | tf_op jit(solution)/shard_map/all_to_all | solution.py:517
  55.3 8.3 %collective-permute-start.2 = (bf16[2,272,128]{2,1,0:T(8,128)(2,1)S(1)}, bf16[2,272,128]{2,1,0:T(8,128)(2,1)S(1)}, u32[]{:S(2)}, u32[]{:S(2)}) collective-permute-start(bf16[2,272,128]{2,1,0:T(8,128)(2,1)S(1)} %get-tuple-element.32), channel_id=1, source_target_pairs={{0,192},{1,193},{2,194},{3,195},{4,196},{5,197},{6,198},{7,199},{8... | collective-permute-start | bytes 417800 | tf_op jit(solution)/shard_map/ppermute | solution.py:558
  55.9 7.7 %collective-permute-start.1 = (bf16[2,272,128]{2,1,0:T(8,128)(2,1)S(1)}, bf16[2,272,128]{2,1,0:T(8,128)(2,1)S(1)}, u32[]{:S(2)}, u32[]{:S(2)}) collective-permute-start(bf16[2,272,128]{2,1,0:T(8,128)(2,1)S(1)} %get-tuple-element.32), channel_id=1, source_target_pairs={{0,128},{1,129},{2,130},{3,131},{4,132},{5,133},{6,134},{7,135},{8... | collective-permute-start | bytes 417800 | tf_op jit(solution)/shard_map/ppermute | solution.py:558
  56.6 34.4 %collective-permute-start = (bf16[2,272,128]{2,1,0:T(8,128)(2,1)S(1)}, bf16[2,272,128]{2,1,0:T(8,128)(2,1)S(1)}, u32[]{:S(2)}, u32[]{:S(2)}) collective-permute-start(bf16[2,272,128]{2,1,0:T(8,128)(2,1)S(1)} %get-tuple-element.32), channel_id=1, source_target_pairs={{0,64},{1,65},{2,66},{3,67},{4,68},{5,69},{6,70},{7,71},{8,72},{9,... | collective-permute-start | bytes 417800 | tf_op jit(solution)/shard_map/ppermute | solution.py:558
  57.9 33.2 %collective-permute-start.3 = (bf16[272,128]{1,0:T(8,128)(2,1)S(1)}, bf16[272,128]{1,0:T(8,128)(2,1)S(1)}, u32[]{:S(2)}, u32[]{:S(2)}) collective-permute-start(bf16[272,128]{1,0:T(8,128)(2,1)S(1)} %get-tuple-element.33), channel_id=1, source_target_pairs={{0,16},{16,32},{32,48},{48,64},{64,80},{80,96},{96,112},{112,128},... | collective-permute-start | bytes 208904 | tf_op jit(solution)/shard_map/ppermute | solution.py:552
  96.2 8.5 %collective-permute-start.6 = (bf16[2,272,128]{2,1,0:T(8,128)(2,1)S(1)}, bf16[2,272,128]{2,1,0:T(8,128)(2,1)S(1)}, u32[]{:S(2)}, u32[]{:S(2)}) collective-permute-start(bf16[2,272,128]{2,1,0:T(8,128)(2,1)S(1)} %add_add_fusion.1), channel_id=1, source_target_pairs={{0,48},{64,112},{128,176},{192,240},{1,49},{65,113},{129,177},{193... | collective-permute-start | bytes 417800 | tf_op jit(solution)/shard_map/ppermute | solution.py:558
  97.5 7.2 %collective-permute-start.5 = (bf16[2,272,128]{2,1,0:T(8,128)(2,1)S(1)}, bf16[2,272,128]{2,1,0:T(8,128)(2,1)S(1)}, u32[]{:S(2)}, u32[]{:S(2)}) collective-permute-start(bf16[2,272,128]{2,1,0:T(8,128)(2,1)S(1)} %add_add_fusion.1), channel_id=1, source_target_pairs={{0,32},{64,96},{128,160},{192,224},{1,33},{65,97},{129,161},{193,2... | collective-permute-start | bytes 417800 | tf_op jit(solution)/shard_map/ppermute | solution.py:558
  98.8 5.9 %collective-permute-start.4 = (bf16[2,272,128]{2,1,0:T(8,128)(2,1)S(1)}, bf16[2,272,128]{2,1,0:T(8,128)(2,1)S(1)}, u32[]{:S(2)}, u32[]{:S(2)}) collective-permute-start(bf16[2,272,128]{2,1,0:T(8,128)(2,1)S(1)} %add_add_fusion.1), channel_id=1, source_target_pairs={{0,16},{64,80},{128,144},{192,208},{1,17},{65,81},{129,145},{193,2... | collective-permute-start | bytes 417800 | tf_op jit(solution)/shard_map/ppermute | solution.py:558
  104.7 32.4 %all-to-all-start.2 = ((bf16[16,192,128]{2,1,0:T(8,128)(2,1)}), bf16[16,192,128]{2,1,0:T(8,128)(2,1)S(1)}, u32[]{:S(2)}, u32[]{:S(2)}) async-start(bf16[16,192,128]{2,1,0:T(8,128)(2,1)} %get-tuple-element.57), calls=%async_computation.2 | async-start | bytes 1572864 | tf_op jit(solution)/shard_map/all_to_all | solution.py:517
  115.7 11.0 %collective-permute-start.9 = (bf16[3,128,128]{2,1,0:T(8,128)(2,1)S(1)}, bf16[3,128,128]{2,1,0:T(8,128)(2,1)S(1)}, u32[]{:S(2)}, u32[]{:S(2)}) collective-permute-start(bf16[3,128,128]{2,1,0:T(8,128)(2,1)S(1)} %get-tuple-element.42), channel_id=1, source_target_pairs={{48,0},{112,64},{176,128},{240,192},{49,1},{113,65},{177,129},{241... | collective-permute-start | bytes 294920 | tf_op jit(solution)/shard_map/ppermute | solution.py:615
  117.0 9.7 %collective-permute-start.8 = (bf16[3,128,128]{2,1,0:T(8,128)(2,1)S(1)}, bf16[3,128,128]{2,1,0:T(8,128)(2,1)S(1)}, u32[]{:S(2)}, u32[]{:S(2)}) collective-permute-start(bf16[3,128,128]{2,1,0:T(8,128)(2,1)S(1)} %get-tuple-element.42), channel_id=1, source_target_pairs={{32,0},{96,64},{160,128},{224,192},{33,1},{97,65},{161,129},{225,1... | collective-permute-start | bytes 294920 | tf_op jit(solution)/shard_map/ppermute | solution.py:615
  118.3 8.4 %collective-permute-start.7 = (bf16[3,128,128]{2,1,0:T(8,128)(2,1)S(1)}, bf16[3,128,128]{2,1,0:T(8,128)(2,1)S(1)}, u32[]{:S(2)}, u32[]{:S(2)}) collective-permute-start(bf16[3,128,128]{2,1,0:T(8,128)(2,1)S(1)} %get-tuple-element.42), channel_id=1, source_target_pairs={{16,0},{80,64},{144,128},{208,192},{17,1},{81,65},{145,129},{209,1... | collective-permute-start | bytes 294920 | tf_op jit(solution)/shard_map/ppermute | solution.py:615
  119.6 7.2 %collective-permute-start.10 = (bf16[192,128]{1,0:T(8,128)(2,1)S(1)}, bf16[192,128]{1,0:T(8,128)(2,1)S(1)}, u32[]{:S(2)}, u32[]{:S(2)}) collective-permute-start(bf16[192,128]{1,0:T(8,128)(2,1)S(1)} %get-tuple-element.54), channel_id=1, source_target_pairs={{16,0},{32,16},{48,32},{64,48},{80,64},{96,80},{112,96},{128,112},... | collective-permute-start | bytes 147464 | tf_op jit(solution)/shard_map/ppermute | solution.py:610
  126.8 6.1 %collective-permute-start.13 = (bf16[3,128,128]{2,1,0:T(8,128)(2,1)S(1)}, bf16[3,128,128]{2,1,0:T(8,128)(2,1)S(1)}, u32[]{:S(2)}, u32[]{:S(2)}) collective-permute-start(bf16[3,128,128]{2,1,0:T(8,128)(2,1)S(1)} %convert_element_type.24), channel_id=1, source_target_pairs={{192,0},{193,1},{194,2},{195,3},{196,4},{197,5},{198,6},{199,7},{2... | collective-permute-start | bytes 294920 | tf_op jit(solution)/shard_map/ppermute | solution.py:615
  127.5 5.5 %collective-permute-start.12 = (bf16[3,128,128]{2,1,0:T(8,128)(2,1)S(1)}, bf16[3,128,128]{2,1,0:T(8,128)(2,1)S(1)}, u32[]{:S(2)}, u32[]{:S(2)}) collective-permute-start(bf16[3,128,128]{2,1,0:T(8,128)(2,1)S(1)} %convert_element_type.24), channel_id=1, source_target_pairs={{128,0},{129,1},{130,2},{131,3},{132,4},{133,5},{134,6},{135,7},{1... | collective-permute-start | bytes 294920 | tf_op jit(solution)/shard_map/ppermute | solution.py:615
  128.2 8.8 %collective-permute-start.11 = (bf16[3,128,128]{2,1,0:T(8,128)(2,1)S(1)}, bf16[3,128,128]{2,1,0:T(8,128)(2,1)S(1)}, u32[]{:S(2)}, u32[]{:S(2)}) collective-permute-start(bf16[3,128,128]{2,1,0:T(8,128)(2,1)S(1)} %convert_element_type.24), channel_id=1, source_target_pairs={{64,0},{65,1},{66,2},{67,3},{68,4},{69,5},{70,6},{71,7},{72,8},{73... | collective-permute-start | bytes 294920 | tf_op jit(solution)/shard_map/ppermute | solution.py:615

commit v5 on v4

--- a/solution.py
+++ b/solution.py
@@ -13,9 +13,9 @@
 NB = 16
 FACTOR = HD ** (-0.5)
 OFF = 1e30
-EDGES = (0, 1, NB - 1)
-SLAB = 4 * BLK + 16
-PAIR = RAND * 2 * BLK + 16
+EDGES = (0, 1)
+SLAB = 4 * BLK + 8
+PAIR = RAND * 2 * BLK + 8
 F32 = jnp.float32
 BF16 = jnp.bfloat16
 
@@ -62,7 +62,7 @@
     for pull in pulls:
         pull.start()
     lane = lax.broadcasted_iota(jnp.int32, (BLK, HD), 1)
-    row = lax.broadcasted_iota(jnp.int32, (16, HD), 0)
+    row = lax.broadcasted_iota(jnp.int32, (8, HD), 0)
     deltas = jnp.zeros((BLK, HD), F32)
     pulls[0].wait()
     pulls[1].wait()
@@ -83,7 +83,7 @@
         ps[h, 64:128] = ks[:, cols]
         ps[h, 128:192] = vs[:, cols]
         tile = jnp.where(row == 0, high[h : h + 1], jnp.where(row == 1, low[h : h + 1], 0.0))
-        ps[h, 256:272] = tile.astype(BF16)
+        ps[h, 256:264] = tile.astype(BF16)
         push = pltpu.make_async_copy(ps.at[h], out.at[h], out_sem.at[h])
         push.start()
         pushes.append(push)
@@ -116,49 +116,63 @@
     out[...] = result
 
 
+def left_half():
+    return lax.broadcasted_iota(jnp.int32, (1, HD), 1) < BLK
+
+
+def low_pair(one, other):
+    return jnp.where(left_half(), one, pltpu.roll(other, BLK, 1))
+
+
+def high_pair(one, other):
+    return jnp.where(left_half(), pltpu.roll(one, BLK, 1), other)
+
+
 def norm_rows(lse, b):
     pair = lse[:, (b // 2) * HD : (b // 2 + 1) * HD]
-    return pair[:, 64:128] if b % 2 else pair[:, 0:64]
-
-
-def select_body(pos, table, x, lse, dest, halo, glob, ext, out, sem):
-    row = lax.broadcasted_iota(jnp.int32, (16, BLK), 0)
+    return pair if b % 2 else pltpu.roll(pair, BLK, 1)
+
+
+def select_body(pos, table, x, lse, dest, last, first, glob, ext, out, sem):
+    row = lax.broadcasted_iota(jnp.int32, (8, HD), 0)
     lse_all = lse[...]
 
     def ext_of(b, norm):
         high, low = pieces(norm)
-        tile = jnp.where(row == 2, high, jnp.where(row == 3, low, 0.0))
-        return x[b, 256:272, 0:64].astype(F32) + tile
+        tile = jnp.where(row == 0, high, jnp.where(row == 1, low, 0.0))
+        return jnp.where(left_half(), x[b, 256:264].astype(F32), tile)
 
     for b in range(NB):
         norm = norm_rows(lse_all, b)
         if b < GLOB:
             plain = ext_of(b, norm)
-            full = jnp.concatenate([plain, plain], axis=1).astype(BF16)
+            full = plain.astype(BF16)
+            if b == 0:
+                first[0:256] = x[b, 0:256]
+                first[256:264] = full
             keep = pos[0] == 0
             glob[b, 0:256] = jnp.where(keep, x[b, 0:256], jnp.zeros((256, HD), BF16))
-            glob[b, 256:272] = jnp.where(keep, full, jnp.zeros((16, HD), BF16))
+            glob[b, 256:264] = jnp.where(keep, full, jnp.zeros((8, HD), BF16))
             norm = jnp.where(pos[0] == 0, OFF, norm)
         ext[b] = ext_of(b, norm)
         if b == NB - 1:
-            halo[0:256] = x[b, 0:256]
-            halo[256:272] = jnp.concatenate([ext[b], ext[b]], axis=1).astype(BF16)
-
-    rows16 = lax.broadcasted_iota(jnp.int32, (16, BLK), 0)
+            last[0:256] = x[b, 0:256]
+            last[256:264] = ext[b].astype(BF16)
+
 
     def step(i, carry):
         for c in range(2):
             t = i * 2 + c
-            tile = jnp.zeros((16, BLK), F32)
+            tile = jnp.zeros((8, HD), F32)
             for r in range(RAND):
                 b = table[t, r]
                 out[t, r * 64 : r * 64 + 64] = x[b, 0:64]
                 out[t, 192 + r * 64 : 256 + r * 64] = x[b, 192:256]
                 part = ext[b]
                 if r:
-                    part = pltpu.roll(part, 4 * r, 0)
+                    part = pltpu.roll(part, 2 * r, 0)
                 tile = tile + part
-            out[t, 384:400] = jnp.concatenate([tile, tile], axis=1).astype(BF16)
+            out[t, 384:392] = tile.astype(BF16)
             pltpu.make_async_copy(out.at[t], dest.at[t], sem.at[t]).start()
         return carry
 
@@ -223,9 +237,9 @@
 
 
 def pair_delta(x, b):
-    e0 = x[b, 256:272].astype(F32)
-    e1 = x[b + 1, 256:272].astype(F32)
-    return jnp.concatenate([two(e0, 0)[:, 0:64], two(e1, 0)[:, 0:64]], axis=1)
+    e0 = x[b, 256:264].astype(F32)
+    e1 = x[b + 1, 256:264].astype(F32)
+    return low_pair(two(e0, 0), two(e1, 0))
 
 
 def masked_norms(pos, lse):
@@ -278,7 +292,6 @@
     sub = lax.broadcasted_iota(jnp.int32, (HD, HD), 0)
     lane = lax.broadcasted_iota(jnp.int32, (HD, HD), 1)
     keep = (sub >> 6) == (lane >> 6)
-    left = lax.broadcasted_iota(jnp.int32, (1, HD), 1) < 64
     entries = [(t, r) for t in range(NB) for r in range(RAND)]
 
     def tile_of(n):
@@ -290,10 +303,7 @@
                     [y[t, base + r * 64 : base + r * 64 + 64] for t, r in pair], axis=0
                 )
 
-            def row(a):
-                one, other = (two(y[t, 384:400].astype(F32), 4 * r + a) for t, r in pair)
-                return jnp.where(left, one, other)
-
+            sides = [two(y[t, 384:392].astype(F32), 2 * r) for t, r in pair]
             js = [table[NB + t, r] for t, r in pair]
 
             def use(pq, pk, pv):
@@ -312,8 +322,8 @@
                 g=both(192),
                 k=jnp.concatenate([x[j, 64:128] for j in js], axis=0),
                 v=jnp.concatenate([x[j, 128:192] for j in js], axis=0),
-                norm=row(2),
-                delta=row(0),
+                norm=high_pair(*sides),
+                delta=low_pair(*sides),
                 keep=keep,
                 use=use,
             )
@@ -339,15 +349,15 @@
 
 
 def global_body(
-    pos, x, lse, glob, halo, dq, dk, dv, gpart, glow, hback, sums, scores, probs, lows
+    pos, x, lse, glob, dq_out, dk_out, dv_out, gpart, glow,
+    dq, dk, dv, sem, sums, scores, probs, lows,
 ):
     here = pos[0]
     lse_all = masked_norms(pos, lse)
     gq, gk, gv, gg = (joined(glob, a, 0, GLOB) for a in range(4))
-    ext0 = glob[0, 256:272].astype(F32)
-    ext1 = glob[1, 256:272].astype(F32)
-    gdelta = jnp.concatenate([two(ext0, 0)[:, 0:64], two(ext1, 0)[:, 0:64]], axis=1)
-    gnorm = jnp.concatenate([two(ext0, 2)[:, 0:64], two(ext1, 2)[:, 0:64]], axis=1)
+    sides = [two(glob[n, 256:264].astype(F32), 0) for n in range(GLOB)]
+    gdelta = low_pair(*sides)
+    gnorm = high_pair(*sides)
     sums[...] = jnp.zeros_like(sums)
     tiles = []
     for i in range(4):
@@ -389,45 +399,70 @@
         tiles += [down, across]
     staged(tiles, scores, probs, lows)
     gq_sum, gk_sum, gv_sum = sums[0], sums[1], sums[2]
-    hext = halo[256:272].astype(F32)
-    hdelta = two(hext, 0)[:, 0:64]
-    hnorm = jnp.where(here == 0, OFF, two(hext, 2)[:, 0:64])
-    hq, hk, hv, hg = halo[0:64], halo[64:128], halo[128:192], halo[192:256]
-    e0 = x[0, 256:272].astype(F32)
-    aq, ak, av = grads(
-        x[0, 0:64], x[0, 192:256], lse_all[:, 0:64], two(e0, 0)[:, 0:64], hk, hv
-    )
-    bq, bk, bv = grads(hq, hg, hnorm, hdelta, x[0, 64:128], x[0, 128:192])
-    dq[0:64] = dq[0:64] + aq
-    dk[0:64] = dk[0:64] + bk
-    dv[0:64] = dv[0:64] + bv
-    hback[0:64] = (bq * FACTOR).astype(BF16)
-    hback[64:128] = (ak * FACTOR).astype(BF16)
-    hback[128:192] = av.astype(BF16)
+    pushes = [
+        pltpu.make_async_copy(src, dst, sem.at[n])
+        for n, (src, dst) in enumerate(((dq, dq_out), (dk, dk_out), (dv, dv_out)))
+    ]
+    for push in pushes:
+        push.start()
     for n, total in enumerate((gq_sum * FACTOR, gk_sum * FACTOR, gv_sum)):
         gpart[n] = total
         glow[n] = total.astype(BF16)
+    for push in pushes:
+        push.wait()
 
 
 def gather_body(
-    dq_g, dk_g, dv_g, dq_w, dk_w, dv_w, dk_r, dv_r, w, dq, edge,
-    s0, s1, s2, s3, s4, buf, in_sem, out_sem,
+    pos, x, lse, before, after, dq_w, dk_w, dv_w, dq_g, dk_g, dv_g, dk_r, dv_r, w, dq, edge,
+    s0, s1, s2, dq_s, dk_s, dv_s, s3, s4, buf, in_sem, out_sem,
 ):
-    held = (s0, s1, s2, s3, s4)
+    here = pos[0]
+    held = (s0, s1, s2, dq_s, dk_s, dv_s, s3, s4)
+    sources = (dq_w, dk_w, dv_w, dq_g, dk_g, dv_g, dk_r, dv_r)
     pulls = [
         pltpu.make_async_copy(src, dst, in_sem.at[n])
-        for n, (src, dst) in enumerate(zip((dq_w, dk_w, dv_w, dk_r, dv_r), held))
+        for n, (src, dst) in enumerate(zip(sources, held))
     ]
     for pull in pulls:
         pull.start()
+    lse_all = masked_norms(pos, lse)
+    extra = []
+    for slab, b in ((before, 0), (after, NB - 1)):
+        span = slice(b * 64, b * 64 + 64)
+        far_ext = two(slab[256:264].astype(F32), 0)
+        own_ext = two(x[b, 256:264].astype(F32), 0)
+        far_norm = far_ext[:, 64:128]
+        if b == 0:
+            far_norm = jnp.where(here == 0, OFF, far_norm)
+        own_q, _, _ = grads(
+            x[b, 0:64],
+            x[b, 192:256],
+            lse_all[:, span],
+            own_ext[:, 0:64],
+            slab[64:128],
+            slab[128:192],
+        )
+        _, own_k, own_v = grads(
+            slab[0:64],
+            slab[192:256],
+            far_norm,
+            far_ext[:, 0:64],
+            x[b, 64:128],
+            x[b, 128:192],
+        )
+        extra.append((span, own_q, own_k, own_v))
     for pull in pulls:
         pull.wait()
-    dq[...] = dq_g[...] + s0[...]
+    for span, own_q, own_k, own_v in extra:
+        dq_s[span] = dq_s[span] + own_q
+        dk_s[span] = dk_s[span] + own_k
+        dv_s[span] = dv_s[span] + own_v
+    dq[...] = dq_s[...] + s0[...]
     pushes = []
     for b in range(NB):
         span = slice(b * 64, b * 64 + 64)
-        rk = (dk_g[span] + s1[span] + s3[span]) * FACTOR
-        rv = dv_g[span] + s2[span] + s4[span]
+        rk = (dk_s[span] + s1[span] + s3[span]) * FACTOR
+        rv = dv_s[span] + s2[span] + s4[span]
         if b in EDGES:
             at = EDGES.index(b) * 128
             edge[at : at + 64] = rk
@@ -442,7 +477,7 @@
         push.wait()
 
 
-def merge_body(pos, table, dq, edge, z, hback, gtot, w_in, w, acc, out, out_edge, sem):
+def merge_body(pos, table, dq, edge, z, gtot, w_in, w, acc, out, out_edge, sem):
     acc[...] = dq[...] * FACTOR
 
     def step(t, carry):
@@ -463,12 +498,8 @@
 
     for n, b in enumerate(EDGES):
         rk, rv = edge[n * 128 : n * 128 + 64], edge[n * 128 + 64 : n * 128 + 128]
-        if b < GLOB:
-            rk = rk + home * gtot[1, b * 64 : b * 64 + 64]
-            rv = rv + home * gtot[2, b * 64 : b * 64 + 64]
-        else:
-            rk = rk + hback[64:128].astype(F32)
-            rv = rv + hback[128:192].astype(F32)
+        rk = rk + home * gtot[1, b * 64 : b * 64 + 64]
+        rv = rv + home * gtot[2, b * 64 : b * 64 + 64]
         out_edge[n, 0:64] = rk.astype(BF16)
         out_edge[n, 64:128] = rv.astype(BF16)
         send(out_edge.at[n], w.at[b, pl.ds(64, 128)], NB + n)
@@ -477,8 +508,6 @@
         rq = acc[span]
         if b < GLOB:
             rq = rq + home * gtot[0, span]
-        if b == NB - 1:
-            rq = rq + hback[0:64].astype(F32)
         out[b] = rq.astype(BF16)
         send(out.at[b], w.at[b, pl.ds(0, 64)], b)
     for push in pushes:
@@ -536,29 +565,35 @@
     table = call(table_body, struct((2 * NB, HD), jnp.int32), [SM, VM], VM, nbytes=1 << 14)(
         pos, rand_blocks.reshape(NB, NB * RAND)
     )
-    y, halo, glob = call(
+    y, last, first, glob = call(
         select_body,
-        (far((NB, PAIR, HD)), struct((SLAB, HD)), struct((GLOB, SLAB, HD))),
+        (far((NB, PAIR, HD)), struct((SLAB, HD)), struct((SLAB, HD)), struct((GLOB, SLAB, HD))),
         [SM, SM, VM, VM],
-        (HB, VM, VM),
+        (HB, VM, VM, VM),
         nbytes=3 << 20,
         scratch=[
-            pltpu.VMEM((NB, 16, BLK), F32),
+            pltpu.VMEM((NB, 8, HD), F32),
             pltpu.VMEM((NB, PAIR, HD), BF16),
             dma((NB,)),
         ],
     )(pos, table, x, logsumexp)
-    y = exchange(y, "seq")
-    halo = lax.ppermute(halo, "seq", [(s, s + 1) for s in range(groups - 1)])
-
-    def spread(glob, reach):
-        starts = range(0, groups, 4 * reach)
+    def spread(glob, reach, starts):
         source = glob
         for n in (1, 2, 3):
             glob = glob + lax.ppermute(source, "seq", [(s, s + n * reach) for s in starts])
         return glob
 
-    glob = spread(glob, 4)
+    def collect(gpart, glow, reach, starts):
+        for n in (1, 2, 3):
+            moved = lax.ppermute(glow, "seq", [(s + n * reach, s) for s in starts])
+            gpart = gpart + moved.astype(F32)
+        return gpart
+
+    corners = range(0, groups, 4)
+    glob = spread(glob, 4, (0,))
+    glob, y = lax.optimization_barrier((glob, y))
+    y = exchange(y, "seq")
+    glob = spread(glob, 1, corners)
     grid = pltpu.VMEM((rows, HD), F32)
     far_acc = far((rows, HD), F32)
     acc = near((rows, HD), F32)
@@ -571,8 +606,28 @@
         nbytes=2 << 20,
         scratch=[grid] * 3 + [dma((3,))],
     )(pos, x, logsumexp)
-    glob, halo, y, dq_w = lax.optimization_barrier((glob, halo, y, dq_w))
-    glob = spread(glob, 1)
+    glob, dq_w = lax.optimization_barrier((glob, dq_w))
+    dq_g, dk_g, dv_g, gpart, glow = call(
+        global_body,
+        (far_acc,) * 3 + (struct((3, HD, HD), F32), struct((3, HD, HD))),
+        [SM] + [VM] * 3,
+        (HB,) * 3 + (VM,) * 2,
+        flops=1 << 29,
+        nbytes=4 << 20,
+        scratch=[grid] * 3
+        + [
+            dma((3,)),
+            pltpu.VMEM((3, HD, HD), F32),
+            pltpu.VMEM((3, 256, 256), F32),
+            pltpu.VMEM((3, 256, 256), F32),
+            pltpu.VMEM((3, 2, 256, 256), BF16),
+        ],
+    )(pos, x, logsumexp, glob)
+    glow, last, first = lax.optimization_barrier((glow, last, first))
+    gpart = collect(gpart, glow, 1, corners)
+    before = lax.ppermute(last, "seq", [(s, s + 1) for s in range(groups - 1)])
+    after = lax.ppermute(first, "seq", [(s + 1, s) for s in range(groups - 1)])
+    y, gpart, before, after = lax.optimization_barrier((y, gpart, before, after))
     dk_r, dv_r, z = call(
         rand_body,
         (far_acc, far_acc, far((NB, RAND * BLK, HD))),
@@ -591,47 +646,29 @@
             pltpu.VMEM((3, 2, HD, HD), BF16),
         ],
     )(table, x, y)
-    glob, z = lax.optimization_barrier((glob, z))
+    z, gpart = lax.optimization_barrier((z, gpart))
     z = exchange(z, "seq")
-    dq_g, dk_g, dv_g, gpart, glow, hback = call(
-        global_body,
-        (acc,) * 3 + (struct((3, HD, HD), F32), struct((3, HD, HD)), struct((3 * BLK, HD))),
-        [SM] + [VM] * 4,
-        (VM,) * 6,
-        flops=1 << 29,
-        nbytes=4 << 20,
-        scratch=[
-            pltpu.VMEM((3, HD, HD), F32),
-            pltpu.VMEM((3, 256, 256), F32),
-            pltpu.VMEM((3, 256, 256), F32),
-            pltpu.VMEM((3, 2, 256, 256), BF16),
-        ],
-    )(pos, x, logsumexp, glob, halo)
-    hback = lax.ppermute(hback, "seq", [(s, s - 1) for s in range(1, groups)])
-
-    def collect(gpart, glow, reach):
-        span = range(0, groups, 4 * reach)
-        for n in (1, 2, 3):
-            moved = lax.ppermute(glow, "seq", [(s + n * reach, s) for s in span])
-            gpart = gpart + moved.astype(F32)
-        return gpart
-
-    gpart = collect(gpart, glow, 1)
+    gpart = collect(gpart, gpart.astype(BF16), 4, (0,))
     w, dq, edge = call(
         gather_body,
         (far((NB, 3 * BLK, HD)), acc, struct((len(EDGES) * 2 * BLK, HD), F32)),
-        [VM] * 3 + [HB] * 5,
+        [SM] + [VM] * 4 + [HB] * 8,
         (HB, VM, VM),
         flops=1 << 24,
         nbytes=4 << 20,
-        scratch=[grid] * 5 + [pltpu.VMEM((NB, 2 * BLK, HD), BF16), dma((5,)), dma((NB,))],
-    )(*map(hold, (dq_g, dk_g, dv_g)), *map(keep_far, (dq_w, dk_w, dv_w, dk_r, dv_r)))
-    gpart, w, dq, edge, hback = lax.optimization_barrier((gpart, w, dq, edge, hback))
-    gpart = collect(gpart, gpart.astype(BF16), 4)
+        scratch=[grid] * 8 + [pltpu.VMEM((NB, 2 * BLK, HD), BF16), dma((8,)), dma((NB,))],
+    )(
+        pos,
+        x,
+        logsumexp,
+        before,
+        after,
+        *map(keep_far, (dq_w, dk_w, dv_w, dq_g, dk_g, dv_g, dk_r, dv_r)),
+    )
     w = call(
         merge_body,
         far((NB, 3 * BLK, HD)),
-        [SM, SM] + [VM] * 5 + [HB],
+        [SM, SM] + [VM] * 4 + [HB],
         HB,
         nbytes=4 << 20,
         scratch=[
@@ -640,8 +677,8 @@
             pltpu.VMEM((len(EDGES), 2 * BLK, HD), BF16),
             dma((NB + len(EDGES),)),
         ],
-        aliases={7: 0},
-    )(pos, table, hold(dq), edge, z, hback, gpart, w)
+        aliases={6: 0},
+    )(pos, table, hold(dq), edge, z, gpart, w)
     w = exchange(w, "head")
     shape = struct((BLK, HEADS * HD))
     return call(unpack_body, (shape, shape, shape), [VM], (VM,) * 3, nbytes=3 << 19)(w)

time: 169 us -> 164 us (0.970)
  waiting for transfers between devices: 69.5 us -> 60.6 us
  blocking collectives: 26.9 us -> 29.5 us
  Pallas kernels: 20 us -> 21.7 us
    ppermute x6, waiting for transfers between devices: 27.5 us -> 13.8 us  [spread(): lax.ppermute(source, 'seq', [(s, s + n * reach) for s in starts])]
    all_to_all x3, starting transfers between devices: 26.1 us -> 19.5 us  [exchange(): return lax.all_to_all(x, axis, split_axis=0, concat_axis=0, tiled=True)]
    ppermute x6, starting transfers between devices: 6.5 us -> 9.5 us  [spread(): lax.ppermute(source, 'seq', [(s, s + n * reach) for s in starts])]
    all_to_all x3, waiting for transfers between devices: 37.6 us -> 40.6 us  [exchange(): return lax.all_to_all(x, axis, split_axis=0, concat_axis=0, tiled=True)]
    all_to_all x1, blocking collectives: 26.9 us -> 29.5 us  [exchange(): return lax.all_to_all(x, axis, split_axis=0, concat_axis=0, tiled=True)]
    ppermute x8, starting transfers between devices: 16.8 us -> 19 us  [the longest x6 8.47 us: collect(): moved = lax.ppermute(glow, 'seq', [(s + n * reach, s) for s in starts])]
    ppermute x8, waiting for transfers between devices: 4.43 us -> 6.26 us  [the longest x6 4.44 us: collect(): moved = lax.ppermute(glow, 'seq', [(s + n * reach, s) for s in starts])]
  transfers between devices with their start and end apart: 17 -> 17, of which waited for: 5 -> 9; matrix products, arithmetic and copies ran while one was open for 0% -> 0% of each run, Pallas kernels for 7% -> 6%
where the time goes in v5:
time: 164 us; the launch traced here: 161 us
  waiting for transfers between devices  60.6 us (37%)
  starting transfers between devices  48 us (29%)
  blocking collectives  29.5 us (18%)
  Pallas kernels  21.7 us (13%)
    all_to_all x3, waiting for transfers between devices, exchange(): return lax.all_to_all(x, axis, split_axis=0, concat_axis=0, tiled=True)  40.6 us
    all_to_all x1, blocking collectives, exchange(): return lax.all_to_all(x, axis, split_axis=0, concat_axis=0, tiled=True)  29.5 us
    all_to_all x3, starting transfers between devices, exchange(): return lax.all_to_all(x, axis, split_axis=0, concat_axis=0, tiled=True)  19.5 us
    ppermute x6, waiting for transfers between devices, spread(): lax.ppermute(source, 'seq', [(s, s + n * reach) for s in starts])  13.8 us
    ppermute x6, starting transfers between devices, spread(): lax.ppermute(source, 'seq', [(s, s + n * reach) for s in starts])  9.5 us
    ppermute x6, starting transfers between devices, collect(): moved = lax.ppermute(glow, 'seq', [(s + n * reach, s) for s in starts])  8.47 us
    ppermute x1, starting transfers between devices, per_device(): after = lax.ppermute(first, 'seq', [(s + 1, s) for s in range(groups - 1)])  5.93 us
    pallas_call x1, Pallas kernels, per_device(): call(rand_body, (far_acc, far_acc, far((NB, RAND * BLK, HD))), [SM, VM, V...  4.62 us
  transfers between devices with their start and end apart: 17, of which 9 were waited for; matrix products, arithmetic and copies ran while one was open for 0% of the time, Pallas kernels for 6%

profile of v5, /device:TPU:32, one launch (start us, length us, event | category | flops | bytes accessed | tf_op | source)
XLA Modules:
  0.0 161.3 jit_solution(8975204116160978244)
XLA Ops:
  0.6 2.5 %shard_map.95 = bf16[16,264,128]{2,1,0:T(8,128)(2,1)} custom-call(bf16[64,2048]{1,0:T(8,128)(2,1)} %q.1, bf16[64,2048]{1,0:T(8,128)(2,1)} %k.1, bf16[64,2048]{1,0:T(8,128)(2,1)} %v.1, bf16[64,2048]{1,0:T(8,128)(2,1)} %o.1, bf16[64,2048]{1,0:T(8,128)(2,1)} %g.1), custom_call_target="tpu_custom_call" | custom-call | bytes 1310720 | tf_op jit(solution)/shard_map/pallas_call | solution.py:556
  3.2 0.0 copy-start.1
  3.2 0.0 copy-start
  3.2 10.1 %all-to-all-start = ((bf16[16,264,128]{2,1,0:T(8,128)(2,1)}), bf16[16,264,128]{2,1,0:T(8,128)(2,1)S(1)}, u32[]{:S(2)}, u32[]{:S(2)}) async-start(bf16[16,264,128]{2,1,0:T(8,128)(2,1)} %shard_map.95), calls=%async_computation | async-start | bytes 2162688 | tf_op jit(solution)/shard_map/all_to_all | solution.py:546
  13.4 0.1 copy.12
  13.5 0.1 reshape.13.entries
  13.6 0.2 shard_map.94.table
  13.9 31.8 %all-to-all-done.x = bf16[16,264,128]{2,1,0:T(8,128)(2,1)S(1)} async-done(((bf16[16,264,128]{2,1,0:T(8,128)(2,1)}), bf16[16,264,128]{2,1,0:T(8,128)(2,1)S(1)}, u32[]{:S(2)}, u32[]{:S(2)}) %all-to-all-start) | async-done | bytes 1081376 | tf_op jit(solution)/shard_map/all_to_all | solution.py:546
  45.7 2.2 %shard_map.96 = (bf16[16,392,128]{2,1,0:T(8,128)(2,1)}, bf16[264,128]{1,0:T(8,128)(2,1)S(1)}, bf16[264,128]{1,0:T(8,128)(2,1)S(1)}, bf16[2,264,128]{2,1,0:T(8,128)(2,1)S(1)}) custom-call(s32[1]{0:T(128)} %bitcast.pos, s32[32,128]{1,0:T(8,128)S(1)} %shard_map.94.table, bf16[16,264,128]{2,1,0:T(8,128)(2,1)S(1)} %all-to-all-done.x, f32[1,1024]{1,0:T(1,128)S(1)} %copy-done), custom_call_target="tpu_custom_call" | custom-call | bytes 3145728 | tf_op jit(solution)/shard_map/pallas_call | solution.py:568
  47.9 0.7 collective-permute-start.2
  48.6 0.7 collective-permute-start.1
  49.3 1.3 collective-permute-start
  50.6 0.0 collective-permute-done.2
  50.6 0.0 collective-permute-done.1
  50.6 8.4 %collective-permute-done = bf16[2,264,128]{2,1,0:T(8,128)(2,1)S(1)} collective-permute-done((bf16[2,264,128]{2,1,0:T(8,128)(2,1)S(1)}, bf16[2,264,128]{2,1,0:T(8,128)(2,1)S(1)}, u32[]{:S(2)}, u32[]{:S(2)}) %collective-permute-start) | collective-permute-done | bytes 135200 | tf_op jit(solution)/shard_map/ppermute | solution.py:583
  59.1 3.6 %all-to-all-start.1 = ((bf16[16,392,128]{2,1,0:T(8,128)(2,1)}), bf16[16,392,128]{2,1,0:T(8,128)(2,1)S(1)}, u32[]{:S(2)}, u32[]{:S(2)}) async-start(bf16[16,392,128]{2,1,0:T(8,128)(2,1)} %get-tuple-element.36), calls=%async_computation.1 | async-start | bytes 3211264 | tf_op jit(solution)/shard_map/all_to_all | solution.py:546
  62.7 4.3 %collective-permute-start.5 = (bf16[2,264,128]{2,1,0:T(8,128)(2,1)S(1)}, bf16[2,264,128]{2,1,0:T(8,128)(2,1)S(1)}, u32[]{:S(2)}, u32[]{:S(2)}) collective-permute-start(bf16[2,264,128]{2,1,0:T(8,128)(2,1)S(1)} %add_add_fusion.1), channel_id=1, source_target_pairs={{0,48},{64,112},{128,176},{192,240},{1,49},{65,113},{129,177},{193... | collective-permute-start | bytes 405512 | tf_op jit(solution)/shard_map/ppermute | solution.py:583
  67.0 1.3 collective-permute-start.4
  68.3 1.3 collective-permute-start.3
  69.6 2.9 %shard_map.97 = (f32[1024,128]{1,0:T(8,128)}, f32[1024,128]{1,0:T(8,128)}, f32[1024,128]{1,0:T(8,128)}) custom-call(s32[1]{0:T(128)} %bitcast.pos, bf16[16,264,128]{2,1,0:T(8,128)(2,1)S(1)} %all-to-all-done.x, f32[1,1024]{1,0:T(1,128)S(1)} %copy-done), custom_call_target="tpu_custom_call" | custom-call | flops 536870912 | bytes 2097152 | tf_op jit(solution)/shard_map/pallas_call | solution.py:600
  72.5 0.0 collective-permute-done.5
  72.5 2.6 %collective-permute-done.4 = bf16[2,264,128]{2,1,0:T(8,128)(2,1)S(1)} collective-permute-done((bf16[2,264,128]{2,1,0:T(8,128)(2,1)S(1)}, bf16[2,264,128]{2,1,0:T(8,128)(2,1)S(1)}, u32[]{:S(2)}, u32[]{:S(2)}) %collective-permute-start.4) | collective-permute-done | bytes 135200 | tf_op jit(solution)/shard_map/ppermute | solution.py:583
  75.2 2.7 %collective-permute-done.3 = bf16[2,264,128]{2,1,0:T(8,128)(2,1)S(1)} collective-permute-done((bf16[2,264,128]{2,1,0:T(8,128)(2,1)S(1)}, bf16[2,264,128]{2,1,0:T(8,128)(2,1)S(1)}, u32[]{:S(2)}, u32[]{:S(2)}) %collective-permute-start.3) | collective-permute-done | bytes 135200 | tf_op jit(solution)/shard_map/ppermute | solution.py:583
  77.9 2.3 %shard_map.98 = (f32[1024,128]{1,0:T(8,128)}, f32[1024,128]{1,0:T(8,128)}, f32[1024,128]{1,0:T(8,128)}, f32[3,128,128]{2,1,0:T(8,128)S(1)}, bf16[3,128,128]{2,1,0:T(8,128)(2,1)S(1)}) custom-call(s32[1]{0:T(128)} %bitcast.pos, bf16[16,264,128]{2,1,0:T(8,128)(2,1)S(1)} %all-to-all-done.x, f32[1,1024]{1,0:T(1,128)S(1)} %copy-done, ...), custom_call_target="tpu_custom_call" | custom-call | flops 536870912 | bytes 4194304 | tf_op jit(solution)/shard_map/pallas_call | solution.py:610
  80.2 1.3 collective-permute-start.8
  81.5 1.3 collective-permute-start.7
  82.8 1.3 collective-permute-start.6
  84.1 4.6 %collective-permute-start.9 = (bf16[264,128]{1,0:T(8,128)(2,1)S(1)}, bf16[264,128]{1,0:T(8,128)(2,1)S(1)}, u32[]{:S(2)}, u32[]{:S(2)}) collective-permute-start(bf16[264,128]{1,0:T(8,128)(2,1)S(1)} %get-tuple-element.45), channel_id=1, source_target_pairs={{0,16},{16,32},{32,48},{48,64},{64,80},{80,96},{96,112},{112,128},... | collective-permute-start | bytes 202760 | tf_op jit(solution)/shard_map/ppermute | solution.py:628
  88.7 5.9 %collective-permute-start.10 = (bf16[264,128]{1,0:T(8,128)(2,1)S(1)}, bf16[264,128]{1,0:T(8,128)(2,1)S(1)}, u32[]{:S(2)}, u32[]{:S(2)}) collective-permute-start(bf16[264,128]{1,0:T(8,128)(2,1)S(1)} %get-tuple-element.46), channel_id=1, source_target_pairs={{16,0},{32,16},{48,32},{64,48},{80,64},{96,80},{112,96},{128,112},... | collective-permute-start | bytes 202760 | tf_op jit(solution)/shard_map/ppermute | solution.py:629
  94.6 0.0 collective-permute-done.8
  94.6 0.0 collective-permute-done.6
  94.7 0.5 collective-permute-done.9.before
  95.2 1.3 collective-permute-done.10.after
  96.5 2.1 %all-to-all-done.1.y = bf16[16,392,128]{2,1,0:T(8,128)(2,1)S(1)} async-done(((bf16[16,392,128]{2,1,0:T(8,128)(2,1)}), bf16[16,392,128]{2,1,0:T(8,128)(2,1)S(1)}, u32[]{:S(2)}, u32[]{:S(2)}) %all-to-all-start.1) | async-done | bytes 1605664 | tf_op jit(solution)/shard_map/all_to_all | solution.py:546
  98.7 4.6 %shard_map.99 = (f32[1024,128]{1,0:T(8,128)}, f32[1024,128]{1,0:T(8,128)}, bf16[16,192,128]{2,1,0:T(8,128)(2,1)}) custom-call(s32[32,128]{1,0:T(8,128)S(1)} %shard_map.94.table, bf16[16,264,128]{2,1,0:T(8,128)(2,1)S(1)} %all-to-all-done.x, bf16[16,392,128]{2,1,0:T(8,128)(2,1)S(1)} %all-to-all-done.1.y), custom_call_target="tpu_custom_call" | custom-call | flops 536870912 | bytes 4194304 | tf_op jit(solution)/shard_map/pallas_call | solution.py:631
  103.3 5.8 %all-to-all-start.2 = ((bf16[16,192,128]{2,1,0:T(8,128)(2,1)}), bf16[16,192,128]{2,1,0:T(8,128)(2,1)S(1)}, u32[]{:S(2)}, u32[]{:S(2)}) async-start(bf16[16,192,128]{2,1,0:T(8,128)(2,1)} %get-tuple-element.62), calls=%async_computation.2 | async-start | bytes 1572864 | tf_op jit(solution)/shard_map/all_to_all | solution.py:546
  109.1 0.7 collective-permute-start.13
  109.8 0.7 collective-permute-start.12
  110.5 3.3 %collective-permute-start.11 = (bf16[3,128,128]{2,1,0:T(8,128)(2,1)S(1)}, bf16[3,128,128]{2,1,0:T(8,128)(2,1)S(1)}, u32[]{:S(2)}, u32[]{:S(2)}) collective-permute-start(bf16[3,128,128]{2,1,0:T(8,128)(2,1)S(1)} %convert_element_type.24), channel_id=1, source_target_pairs={{64,0},{65,1},{66,2},{67,3},{68,4},{69,5},{70,6},{71,7},{72,8},{73... | collective-permute-start | bytes 294920 | tf_op jit(solution)/shard_map/ppermute | solution.py:588
  113.7 3.7 %shard_map.100 = (bf16[16,192,128]{2,1,0:T(8,128)(2,1)}, f32[1024,128]{1,0:T(8,128)S(1)}, f32[256,128]{1,0:T(8,128)S(1)}) custom-call(s32[1]{0:T(128)} %bitcast.pos, bf16[16,264,128]{2,1,0:T(8,128)(2,1)S(1)} %all-to-all-done.x, f32[1,1024]{1,0:T(1,128)S(1)} %copy-done, bf16[264,128]{1,0:T(8,128)(2,1)S(1)} %collective-permute-done.9.before, ...), custom_call_target="tpu_custom_call" | custom-call | flops 16777216 | bytes 4194304 | tf_op jit(solution)/shard_map/pallas_call | solution.py:652
  117.5 0.0 collective-permute-done.13
  117.5 0.0 collective-permute-done.12
  117.5 4.4 %collective-permute-done.11 = bf16[3,128,128]{2,1,0:T(8,128)(2,1)S(1)} collective-permute-done((bf16[3,128,128]{2,1,0:T(8,128)(2,1)S(1)}, bf16[3,128,128]{2,1,0:T(8,128)(2,1)S(1)}, u32[]{:S(2)}, u32[]{:S(2)}) %collective-permute-start.11) | collective-permute-done | bytes 98336 | tf_op jit(solution)/shard_map/ppermute | solution.py:588
  121.9 0.1 convert_add_fusion.gtot
  122.0 6.6 %all-to-all-done.2.z = bf16[16,192,128]{2,1,0:T(8,128)(2,1)S(1)} async-done(((bf16[16,192,128]{2,1,0:T(8,128)(2,1)}), bf16[16,192,128]{2,1,0:T(8,128)(2,1)S(1)}, u32[]{:S(2)}, u32[]{:S(2)}) %all-to-all-start.2) | async-done | bytes 786464 | tf_op jit(solution)/shard_map/all_to_all | solution.py:546
  128.6 2.1 %shard_map.101 = bf16[16,192,128]{2,1,0:T(8,128)(2,1)} custom-call(s32[1]{0:T(128)} %bitcast.pos, s32[32,128]{1,0:T(8,128)S(1)} %shard_map.94.table, f32[1024,128]{1,0:T(8,128)S(1)} %get-tuple-element.58.dq, f32[256,128]{1,0:T(8,128)S(1)} %get-tuple-element.59.edge, bf16[16,192,128]{2,1,0:T(8,128)(2,1)S(1)} %all-to-all-done.2.z, ...), custom_call_target="tpu_custom_call", output_to_operand_aliasing={{}: (6, {})} | custom-call | bytes 4194304 | tf_op jit(solution)/shard_map/pallas_call | solution.py:668
  130.7 29.5 %all_to_all.20.w = bf16[16,192,128]{2,1,0:T(8,128)(2,1)S(1)} all-to-all(bf16[16,192,128]{2,1,0:T(8,128)(2,1)} %shard_map.101), channel_id=1, replica_groups=mesh['seq'=16,'head'=16] {'head'}, dimensions={0} | all-to-all | bytes 1572864 | tf_op jit(solution)/shard_map/all_to_all | solution.py:546
  160.2 1.1 shard_map.102
  (7 shorter events, 0.1 us)
Async XLA Ops:
  3.2 10.2 %copy-start.1 = (s32[256,3]{0,1:T(4,128)S(1)}, s32[256,3]{0,1:T(4,128)}, u32[]{:S(2)}) copy-start(s32[256,3]{0,1:T(4,128)} %param.13) | copy-start | bytes 9220
  3.2 42.5 %copy-start = (f32[1,1024]{1,0:T(1,128)S(1)}, f32[1,1024]{1,0:T(1,128)}, u32[]{:S(2)}) copy-start(f32[1,1024]{1,0:T(1,128)} %lse.7) | copy-start | bytes 12292
  3.2 42.5 %all-to-all-start = ((bf16[16,264,128]{2,1,0:T(8,128)(2,1)}), bf16[16,264,128]{2,1,0:T(8,128)(2,1)S(1)}, u32[]{:S(2)}, u32[]{:S(2)}) async-start(bf16[16,264,128]{2,1,0:T(8,128)(2,1)} %shard_map.95), calls=%async_computation | async-start | bytes 2162688 | tf_op jit(solution)/shard_map/all_to_all | solution.py:546
  47.9 2.7 %collective-permute-start.2 = (bf16[2,264,128]{2,1,0:T(8,128)(2,1)S(1)}, bf16[2,264,128]{2,1,0:T(8,128)(2,1)S(1)}, u32[]{:S(2)}, u32[]{:S(2)}) collective-permute-start(bf16[2,264,128]{2,1,0:T(8,128)(2,1)S(1)} %get-tuple-element.34), channel_id=1, source_target_pairs={{0,192},{1,193},{2,194},{3,195},{4,196},{5,197},{6,198},{7,199},{8... | collective-permute-start | bytes 405512 | tf_op jit(solution)/shard_map/ppermute | solution.py:583
  48.6 2.0 %collective-permute-start.1 = (bf16[2,264,128]{2,1,0:T(8,128)(2,1)S(1)}, bf16[2,264,128]{2,1,0:T(8,128)(2,1)S(1)}, u32[]{:S(2)}, u32[]{:S(2)}) collective-permute-start(bf16[2,264,128]{2,1,0:T(8,128)(2,1)S(1)} %get-tuple-element.34), channel_id=1, source_target_pairs={{0,128},{1,129},{2,130},{3,131},{4,132},{5,133},{6,134},{7,135},{8... | collective-permute-start | bytes 405512 | tf_op jit(solution)/shard_map/ppermute | solution.py:583
  49.3 9.8 %collective-permute-start = (bf16[2,264,128]{2,1,0:T(8,128)(2,1)S(1)}, bf16[2,264,128]{2,1,0:T(8,128)(2,1)S(1)}, u32[]{:S(2)}, u32[]{:S(2)}) collective-permute-start(bf16[2,264,128]{2,1,0:T(8,128)(2,1)S(1)} %get-tuple-element.34), channel_id=1, source_target_pairs={{0,64},{1,65},{2,66},{3,67},{4,68},{5,69},{6,70},{7,71},{8,72},{9,... | collective-permute-start | bytes 405512 | tf_op jit(solution)/shard_map/ppermute | solution.py:583
  59.1 39.6 %all-to-all-start.1 = ((bf16[16,392,128]{2,1,0:T(8,128)(2,1)}), bf16[16,392,128]{2,1,0:T(8,128)(2,1)S(1)}, u32[]{:S(2)}, u32[]{:S(2)}) async-start(bf16[16,392,128]{2,1,0:T(8,128)(2,1)} %get-tuple-element.36), calls=%async_computation.1 | async-start | bytes 3211264 | tf_op jit(solution)/shard_map/all_to_all | solution.py:546
  62.7 9.8 %collective-permute-start.5 = (bf16[2,264,128]{2,1,0:T(8,128)(2,1)S(1)}, bf16[2,264,128]{2,1,0:T(8,128)(2,1)S(1)}, u32[]{:S(2)}, u32[]{:S(2)}) collective-permute-start(bf16[2,264,128]{2,1,0:T(8,128)(2,1)S(1)} %add_add_fusion.1), channel_id=1, source_target_pairs={{0,48},{64,112},{128,176},{192,240},{1,49},{65,113},{129,177},{193... | collective-permute-start | bytes 405512 | tf_op jit(solution)/shard_map/ppermute | solution.py:583
  67.0 8.2 %collective-permute-start.4 = (bf16[2,264,128]{2,1,0:T(8,128)(2,1)S(1)}, bf16[2,264,128]{2,1,0:T(8,128)(2,1)S(1)}, u32[]{:S(2)}, u32[]{:S(2)}) collective-permute-start(bf16[2,264,128]{2,1,0:T(8,128)(2,1)S(1)} %add_add_fusion.1), channel_id=1, source_target_pairs={{0,32},{64,96},{128,160},{192,224},{1,33},{65,97},{129,161},{193,2... | collective-permute-start | bytes 405512 | tf_op jit(solution)/shard_map/ppermute | solution.py:583
  68.3 9.6 %collective-permute-start.3 = (bf16[2,264,128]{2,1,0:T(8,128)(2,1)S(1)}, bf16[2,264,128]{2,1,0:T(8,128)(2,1)S(1)}, u32[]{:S(2)}, u32[]{:S(2)}) collective-permute-start(bf16[2,264,128]{2,1,0:T(8,128)(2,1)S(1)} %add_add_fusion.1), channel_id=1, source_target_pairs={{0,16},{64,80},{128,144},{192,208},{1,17},{65,81},{129,145},{193,2... | collective-permute-start | bytes 405512 | tf_op jit(solution)/shard_map/ppermute | solution.py:583
  80.2 14.4 %collective-permute-start.8 = (bf16[3,128,128]{2,1,0:T(8,128)(2,1)S(1)}, bf16[3,128,128]{2,1,0:T(8,128)(2,1)S(1)}, u32[]{:S(2)}, u32[]{:S(2)}) collective-permute-start(bf16[3,128,128]{2,1,0:T(8,128)(2,1)S(1)} %get-tuple-element.44), channel_id=1, source_target_pairs={{48,0},{112,64},{176,128},{240,192},{49,1},{113,65},{177,129},{241... | collective-permute-start | bytes 294920 | tf_op jit(solution)/shard_map/ppermute | solution.py:588
  81.5 13.1 %collective-permute-start.7 = (bf16[3,128,128]{2,1,0:T(8,128)(2,1)S(1)}, bf16[3,128,128]{2,1,0:T(8,128)(2,1)S(1)}, u32[]{:S(2)}, u32[]{:S(2)}) collective-permute-start(bf16[3,128,128]{2,1,0:T(8,128)(2,1)S(1)} %get-tuple-element.44), channel_id=1, source_target_pairs={{32,0},{96,64},{160,128},{224,192},{33,1},{97,65},{161,129},{225,1... | collective-permute-start | bytes 294920 | tf_op jit(solution)/shard_map/ppermute | solution.py:588
  82.8 11.8 %collective-permute-start.6 = (bf16[3,128,128]{2,1,0:T(8,128)(2,1)S(1)}, bf16[3,128,128]{2,1,0:T(8,128)(2,1)S(1)}, u32[]{:S(2)}, u32[]{:S(2)}) collective-permute-start(bf16[3,128,128]{2,1,0:T(8,128)(2,1)S(1)} %get-tuple-element.44), channel_id=1, source_target_pairs={{16,0},{80,64},{144,128},{208,192},{17,1},{81,65},{145,129},{209,1... | collective-permute-start | bytes 294920 | tf_op jit(solution)/shard_map/ppermute | solution.py:588
  84.1 11.1 %collective-permute-start.9 = (bf16[264,128]{1,0:T(8,128)(2,1)S(1)}, bf16[264,128]{1,0:T(8,128)(2,1)S(1)}, u32[]{:S(2)}, u32[]{:S(2)}) collective-permute-start(bf16[264,128]{1,0:T(8,128)(2,1)S(1)} %get-tuple-element.45), channel_id=1, source_target_pairs={{0,16},{16,32},{32,48},{48,64},{64,80},{80,96},{96,112},{112,128},... | collective-permute-start | bytes 202760 | tf_op jit(solution)/shard_map/ppermute | solution.py:628
  88.7 7.8 %collective-permute-start.10 = (bf16[264,128]{1,0:T(8,128)(2,1)S(1)}, bf16[264,128]{1,0:T(8,128)(2,1)S(1)}, u32[]{:S(2)}, u32[]{:S(2)}) collective-permute-start(bf16[264,128]{1,0:T(8,128)(2,1)S(1)} %get-tuple-element.46), channel_id=1, source_target_pairs={{16,0},{32,16},{48,32},{64,48},{80,64},{96,80},{112,96},{128,112},... | collective-permute-start | bytes 202760 | tf_op jit(solution)/shard_map/ppermute | solution.py:629
  103.3 25.3 %all-to-all-start.2 = ((bf16[16,192,128]{2,1,0:T(8,128)(2,1)}), bf16[16,192,128]{2,1,0:T(8,128)(2,1)S(1)}, u32[]{:S(2)}, u32[]{:S(2)}) async-start(bf16[16,192,128]{2,1,0:T(8,128)(2,1)} %get-tuple-element.62), calls=%async_computation.2 | async-start | bytes 1572864 | tf_op jit(solution)/shard_map/all_to_all | solution.py:546
  109.1 8.4 %collective-permute-start.13 = (bf16[3,128,128]{2,1,0:T(8,128)(2,1)S(1)}, bf16[3,128,128]{2,1,0:T(8,128)(2,1)S(1)}, u32[]{:S(2)}, u32[]{:S(2)}) collective-permute-start(bf16[3,128,128]{2,1,0:T(8,128)(2,1)S(1)} %convert_element_type.24), channel_id=1, source_target_pairs={{192,0},{193,1},{194,2},{195,3},{196,4},{197,5},{198,6},{199,7},{2... | collective-permute-start | bytes 294920 | tf_op jit(solution)/shard_map/ppermute | solution.py:588
  109.8 7.7 %collective-permute-start.12 = (bf16[3,128,128]{2,1,0:T(8,128)(2,1)S(1)}, bf16[3,128,128]{2,1,0:T(8,128)(2,1)S(1)}, u32[]{:S(2)}, u32[]{:S(2)}) collective-permute-start(bf16[3,128,128]{2,1,0:T(8,128)(2,1)S(1)} %convert_element_type.24), channel_id=1, source_target_pairs={{128,0},{129,1},{130,2},{131,3},{132,4},{133,5},{134,6},{135,7},{1... | collective-permute-start | bytes 294920 | tf_op jit(solution)/shard_map/ppermute | solution.py:588
  110.5 11.5 %collective-permute-start.11 = (bf16[3,128,128]{2,1,0:T(8,128)(2,1)S(1)}, bf16[3,128,128]{2,1,0:T(8,128)(2,1)S(1)}, u32[]{:S(2)}, u32[]{:S(2)}) collective-permute-start(bf16[3,128,128]{2,1,0:T(8,128)(2,1)S(1)} %convert_element_type.24), channel_id=1, source_target_pairs={{64,0},{65,1},{66,2},{67,3},{68,4},{69,5},{70,6},{71,7},{72,8},{73... | collective-permute-start | bytes 294920 | tf_op jit(solution)/shard_map/ppermute | solution.py:588

commit v6 on v5

--- a/solution.py
+++ b/solution.py
@@ -161,8 +161,8 @@
 
 
     def step(i, carry):
-        for c in range(2):
-            t = i * 2 + c
+        for c in range(4):
+            t = i * 4 + c
             tile = jnp.zeros((8, HD), F32)
             for r in range(RAND):
                 b = table[t, r]
@@ -176,7 +176,7 @@
             pltpu.make_async_copy(out.at[t], dest.at[t], sem.at[t]).start()
         return carry
 
-    lax.fori_loop(0, NB // 2, step, 0)
+    lax.fori_loop(0, NB // 4, step, 0)
 
     def finish(t, carry):
         pltpu.make_async_copy(out.at[t], dest.at[t], sem.at[t]).wait()
@@ -194,7 +194,7 @@
     return tn(dst, k), nn(dst, q), nn(pt.astype(BF16), g)
 
 
-def staged(tiles, scores, probs, lows):
+def staged(tiles, scores, probs, lows, want="qkv"):
     depth = 3
     held = {}
     for step in range(len(tiles) + 2):
@@ -214,8 +214,9 @@
             pt = jnp.exp(scores[view] * FACTOR - tile["norm"])
             if tile.get("keep") is not None:
                 pt = jnp.where(tile["keep"], pt, 0.0)
-            low_view = (n % depth, 0) + view[1:]
-            lows[low_view] = pt.astype(BF16)
+            if "v" in want:
+                low_view = (n % depth, 0) + view[1:]
+                lows[low_view] = pt.astype(BF16)
             low_view = (n % depth, 1) + view[1:]
             lows[low_view] = (pt * (probs[view] - tile["delta"])).astype(BF16)
         n = step - 2
@@ -223,9 +224,15 @@
             tile = held.pop(n)
             shape = (tile["k"].shape[0], tile["q"].shape[0])
             cut = (slice(0, shape[0]), slice(0, shape[1]))
-            pt = lows[(n % depth, 0) + cut]
             dst = lows[(n % depth, 1) + cut]
-            tile["use"](tn(dst, tile["k"]), nn(dst, tile["q"]), nn(pt, tile["g"]))
+            parts = []
+            if "q" in want:
+                parts.append(tn(dst, tile["k"]))
+            if "k" in want:
+                parts.append(nn(dst, tile["q"]))
+            if "v" in want:
+                parts.append(nn(lows[(n % depth, 0) + cut], tile["g"]))
+            tile["use"](*parts)
 
 
 def two(ext, a):
@@ -286,9 +293,7 @@
         push.wait()
 
 
-def rand_body(table, x, y, dk_out, dv_out, z, dk, dv, buf, sem, acc_sem, scores, probs, lows):
-    dk[...] = jnp.zeros_like(dk)
-    dv[...] = jnp.zeros_like(dv)
+def rand_tiles(table, x, y, use):
     sub = lax.broadcasted_iota(jnp.int32, (HD, HD), 0)
     lane = lax.broadcasted_iota(jnp.int32, (HD, HD), 1)
     keep = (sub >> 6) == (lane >> 6)
@@ -305,18 +310,6 @@
 
             sides = [two(y[t, 384:392].astype(F32), 2 * r) for t, r in pair]
             js = [table[NB + t, r] for t, r in pair]
-
-            def use(pq, pk, pv):
-                low = (pq * FACTOR).astype(BF16)
-                for m, (t, r) in enumerate(pair):
-                    rows = slice(m * 64, m * 64 + 64)
-                    buf[t, r * 64 : r * 64 + 64] = low[rows]
-                    span = pl.ds(pl.multiple_of(js[m] * 64, 64), 64)
-                    dk[span] = dk[span] + pk[rows]
-                    dv[span] = dv[span] + pv[rows]
-                    if r == RAND - 1:
-                        pltpu.make_async_copy(buf.at[t], z.at[t], sem.at[t]).start()
-
             return dict(
                 q=both(0),
                 g=both(192),
@@ -325,27 +318,68 @@
                 norm=high_pair(*sides),
                 delta=low_pair(*sides),
                 keep=keep,
-                use=use,
+                use=lambda *parts: use(pair, js, *parts),
             )
 
         return make
 
-    staged([tile_of(n) for n in range(len(entries) // 2)], scores, probs, lows)
-    drains = []
-    for n in range(4):
-        span = pl.ds(n * 256, 256)
-        for m, (src, dst) in enumerate(((dk, dk_out), (dv, dv_out))):
-            drain = pltpu.make_async_copy(src.at[span], dst.at[span], acc_sem.at[2 * n + m])
-            drain.start()
-            drains.append(drain)
-    for drain in drains:
-        drain.wait()
+    return [tile_of(n) for n in range(len(entries) // 2)]
+
+
+def rand_query_body(table, x, y, z, y_out, buf, sem, y_sem, scores, probs, lows):
+    saves = [
+        pltpu.make_async_copy(y.at[pl.ds(2 * n, 2)], y_out.at[pl.ds(2 * n, 2)], y_sem.at[n])
+        for n in range(NB // 2)
+    ]
+    for save in saves:
+        save.start()
+
+    def use(pair, js, pq):
+        low = (pq * FACTOR).astype(BF16)
+        for m, (t, r) in enumerate(pair):
+            buf[t, r * 64 : r * 64 + 64] = low[m * 64 : m * 64 + 64]
+            if r == RAND - 1:
+                pltpu.make_async_copy(buf.at[t], z.at[t], sem.at[t]).start()
+
+    staged(rand_tiles(table, x, y, use), scores, probs, lows, "q")
+    for save in saves:
+        save.wait()
 
     def finish(t, carry):
         pltpu.make_async_copy(buf.at[t], z.at[t], sem.at[t]).wait()
         return carry
 
     lax.fori_loop(0, NB, finish, 0)
+
+
+def rand_key_body(table, x, y_far, dk_out, dv_out, y, dk, dv, y_sem, sem, scores, probs, lows):
+    pulls = [
+        pltpu.make_async_copy(y_far.at[pl.ds(2 * n, 2)], y.at[pl.ds(2 * n, 2)], y_sem.at[n])
+        for n in range(NB // 2)
+    ]
+    for pull in pulls:
+        pull.start()
+    dk[...] = jnp.zeros_like(dk)
+    dv[...] = jnp.zeros_like(dv)
+    for pull in pulls:
+        pull.wait()
+
+    def use(pair, js, pk, pv):
+        for m, j in enumerate(js):
+            rows = slice(m * 64, m * 64 + 64)
+            span = pl.ds(pl.multiple_of(j * 64, 64), 64)
+            dk[span] = dk[span] + pk[rows]
+            dv[span] = dv[span] + pv[rows]
+
+    staged(rand_tiles(table, x, y, use), scores, probs, lows, "kv")
+    pushes = [
+        pltpu.make_async_copy(src, dst, sem.at[n])
+        for n, (src, dst) in enumerate(((dk, dk_out), (dv, dv_out)))
+    ]
+    for push in pushes:
+        push.start()
+    for push in pushes:
+        push.wait()
 
 
 def global_body(
@@ -479,15 +513,10 @@
 
 def merge_body(pos, table, dq, edge, z, gtot, w_in, w, acc, out, out_edge, sem):
     acc[...] = dq[...] * FACTOR
-
-    def step(t, carry):
+    for t in range(NB):
         for r in range(RAND):
-            b = table[t, r]
-            span = pl.ds(pl.multiple_of(b * 64, 64), 64)
+            span = pl.ds(pl.multiple_of(table[t, r] * 64, 64), 64)
             acc[span] = acc[span] + z[t, r * 64 : r * 64 + 64].astype(F32)
-        return carry
-
-    lax.fori_loop(0, NB, step, 0)
     home = jnp.where(pos[0] == 0, 1.0, 0.0)
     pushes = []
 
@@ -628,27 +657,35 @@
     before = lax.ppermute(last, "seq", [(s, s + 1) for s in range(groups - 1)])
     after = lax.ppermute(first, "seq", [(s + 1, s) for s in range(groups - 1)])
     y, gpart, before, after = lax.optimization_barrier((y, gpart, before, after))
-    dk_r, dv_r, z = call(
-        rand_body,
-        (far_acc, far_acc, far((NB, RAND * BLK, HD))),
+    stage_space = [
+        pltpu.VMEM((3, HD, HD), F32),
+        pltpu.VMEM((3, HD, HD), F32),
+        pltpu.VMEM((3, 2, HD, HD), BF16),
+    ]
+    z, y = call(
+        rand_query_body,
+        (far((NB, RAND * BLK, HD)), far((NB, PAIR, HD))),
         [SM, VM, VM],
-        (HB,) * 3,
+        (HB,) * 2,
         flops=1 << 29,
         nbytes=4 << 20,
-        scratch=[
-            grid,
-            grid,
-            pltpu.VMEM((NB, RAND * BLK, HD), BF16),
-            dma((NB,)),
-            dma((8,)),
-            pltpu.VMEM((3, HD, HD), F32),
-            pltpu.VMEM((3, HD, HD), F32),
-            pltpu.VMEM((3, 2, HD, HD), BF16),
-        ],
+        scratch=[pltpu.VMEM((NB, RAND * BLK, HD), BF16), dma((NB,)), dma((NB // 2,))]
+        + stage_space,
     )(table, x, y)
-    z, gpart = lax.optimization_barrier((z, gpart))
+    z, gpart, y = lax.optimization_barrier((z, gpart, y))
     z = exchange(z, "seq")
-    gpart = collect(gpart, gpart.astype(BF16), 4, (0,))
+    moved = lax.ppermute(gpart.astype(BF16), "seq", [(4, 0), (12, 8)])
+    gpart = gpart + moved.astype(F32)
+    dk_r, dv_r = call(
+        rand_key_body,
+        (far_acc, far_acc),
+        [SM, VM, HB],
+        (HB,) * 2,
+        flops=1 << 29,
+        nbytes=4 << 20,
+        scratch=[pltpu.VMEM((NB, PAIR, HD), BF16), grid, grid, dma((NB // 2,)), dma((2,))]
+        + stage_space,
+    )(table, x, keep_far(y))
     w, dq, edge = call(
         gather_body,
         (far((NB, 3 * BLK, HD)), acc, struct((len(EDGES) * 2 * BLK, HD), F32)),
@@ -665,6 +702,9 @@
         after,
         *map(keep_far, (dq_w, dk_w, dv_w, dq_g, dk_g, dv_g, dk_r, dv_r)),
     )
+    gpart, w, dq, edge = lax.optimization_barrier((gpart, w, dq, edge))
+    moved = lax.ppermute(gpart.astype(BF16), "seq", [(8, 0)])
+    gpart = gpart + moved.astype(F32)
     w = call(
         merge_body,
         far((NB, 3 * BLK, HD)),

time: 164 us -> 162 us (0.988)
  Pallas kernels: 21.7 us -> 26.5 us
  waiting for transfers between devices: 60.6 us -> 57.1 us
  starting transfers between devices: 48 us -> 46.1 us
    pallas_call x1 -> x2, Pallas kernels: 4.62 us -> 9.57 us  [the longest x1 5.46 us: per_device(): call(rand_key_body, (far_acc, far_acc), [SM, VM, HB], (HB,) * 2, flops=1...]
    ppermute x6 -> x3, starting transfers between devices: 8.47 us -> 3.88 us  [collect(): moved = lax.ppermute(glow, 'seq', [(s + n * reach, s) for s in starts])]
    ppermute x6 -> x3, waiting for transfers between devices: 4.44 us -> 0.01 us  [collect(): moved = lax.ppermute(glow, 'seq', [(s + n * reach, s) for s in starts])]
    ppermute x0 -> x2, starting transfers between devices: none -> 2.68 us  [the longest x1 2.01 us: per_device(): moved = lax.ppermute(gpart.astype(BF16), 'seq', [(4, 0), (12, 8)])]
  transfers between devices with their start and end apart: 17 -> 16, of which waited for: 9 -> 9; matrix products, arithmetic and copies ran while one was open for 0% -> 0% of each run, Pallas kernels for 6% -> 9%
where the time goes in v6:
time: 162 us; the launch traced here: 161 us
  waiting for transfers between devices  57.1 us (35%)
  starting transfers between devices  46.1 us (28%)
  blocking collectives  29.5 us (18%)
  Pallas kernels  26.5 us (16%)
    all_to_all x3, waiting for transfers between devices, exchange(): return lax.all_to_all(x, axis, split_axis=0, concat_axis=0, tiled=True)  40.3 us
    all_to_all x1, blocking collectives, exchange(): return lax.all_to_all(x, axis, split_axis=0, concat_axis=0, tiled=True)  29.5 us
    all_to_all x3, starting transfers between devices, exchange(): return lax.all_to_all(x, axis, split_axis=0, concat_axis=0, tiled=True)  19.5 us
    ppermute x6, waiting for transfers between devices, spread(): lax.ppermute(source, 'seq', [(s, s + n * reach) for s in starts])  13.8 us
    ppermute x6, starting transfers between devices, spread(): lax.ppermute(source, 'seq', [(s, s + n * reach) for s in starts])  9.5 us
    ppermute x1, starting transfers between devices, per_device(): after = lax.ppermute(first, 'seq', [(s + 1, s) for s in range(groups - 1)])  5.93 us
    pallas_call x1, Pallas kernels, per_device(): call(rand_key_body, (far_acc, far_acc), [SM, VM, HB], (HB,) * 2, flops=1...  5.46 us
    ppermute x1, starting transfers between devices, per_device(): before = lax.ppermute(last, 'seq', [(s, s + 1) for s in range(groups - 1)])  4.55 us
  transfers between devices with their start and end apart: 16, of which 9 were waited for; matrix products, arithmetic and copies ran while one was open for 0% of the time, Pallas kernels for 9%

profile of v6, /device:TPU:32, one launch (start us, length us, event | category | flops | bytes accessed | tf_op | source)
XLA Modules:
  0.0 160.6 jit_solution(13244400324416017139)
XLA Ops:
  0.6 2.5 %shard_map.95 = bf16[16,264,128]{2,1,0:T(8,128)(2,1)} custom-call(bf16[64,2048]{1,0:T(8,128)(2,1)} %q.1, bf16[64,2048]{1,0:T(8,128)(2,1)} %k.1, bf16[64,2048]{1,0:T(8,128)(2,1)} %v.1, bf16[64,2048]{1,0:T(8,128)(2,1)} %o.1, bf16[64,2048]{1,0:T(8,128)(2,1)} %g.1), custom_call_target="tpu_custom_call" | custom-call | bytes 1310720 | tf_op jit(solution)/shard_map/pallas_call | solution.py:585
  3.2 0.0 copy-start.1
  3.2 0.0 copy-start
  3.2 10.1 %all-to-all-start = ((bf16[16,264,128]{2,1,0:T(8,128)(2,1)}), bf16[16,264,128]{2,1,0:T(8,128)(2,1)S(1)}, u32[]{:S(2)}, u32[]{:S(2)}) async-start(bf16[16,264,128]{2,1,0:T(8,128)(2,1)} %shard_map.95), calls=%async_computation | async-start | bytes 2162688 | tf_op jit(solution)/shard_map/all_to_all | solution.py:575
  13.4 0.1 copy.12
  13.5 0.1 reshape.13.entries
  13.6 0.2 shard_map.94.table
  13.9 31.8 %all-to-all-done.x = bf16[16,264,128]{2,1,0:T(8,128)(2,1)S(1)} async-done(((bf16[16,264,128]{2,1,0:T(8,128)(2,1)}), bf16[16,264,128]{2,1,0:T(8,128)(2,1)S(1)}, u32[]{:S(2)}, u32[]{:S(2)}) %all-to-all-start) | async-done | bytes 1081376 | tf_op jit(solution)/shard_map/all_to_all | solution.py:575
  45.7 0.0 copy-done
  45.7 2.3 %shard_map.96 = (bf16[16,392,128]{2,1,0:T(8,128)(2,1)}, bf16[264,128]{1,0:T(8,128)(2,1)S(1)}, bf16[264,128]{1,0:T(8,128)(2,1)S(1)}, bf16[2,264,128]{2,1,0:T(8,128)(2,1)S(1)}) custom-call(s32[1]{0:T(128)} %bitcast.pos, s32[32,128]{1,0:T(8,128)S(1)} %shard_map.94.table, bf16[16,264,128]{2,1,0:T(8,128)(2,1)S(1)} %all-to-all-done.x, f32[1,1024]{1,0:T(1,128)S(1)} %copy-done), custom_call_target="tpu_custom_call" | custom-call | bytes 3145728 | tf_op jit(solution)/shard_map/pallas_call | solution.py:597
  47.9 0.7 collective-permute-start.2
  48.6 0.7 collective-permute-start.1
  49.3 1.3 collective-permute-start
  50.6 0.0 collective-permute-done.2
  50.6 0.0 collective-permute-done.1
  50.6 8.4 %collective-permute-done = bf16[2,264,128]{2,1,0:T(8,128)(2,1)S(1)} collective-permute-done((bf16[2,264,128]{2,1,0:T(8,128)(2,1)S(1)}, bf16[2,264,128]{2,1,0:T(8,128)(2,1)S(1)}, u32[]{:S(2)}, u32[]{:S(2)}) %collective-permute-start) | collective-permute-done | bytes 135200 | tf_op jit(solution)/shard_map/ppermute | solution.py:612
  59.1 3.6 %all-to-all-start.1 = ((bf16[16,392,128]{2,1,0:T(8,128)(2,1)}), bf16[16,392,128]{2,1,0:T(8,128)(2,1)S(1)}, u32[]{:S(2)}, u32[]{:S(2)}) async-start(bf16[16,392,128]{2,1,0:T(8,128)(2,1)} %get-tuple-element.42), calls=%async_computation.1 | async-start | bytes 3211264 | tf_op jit(solution)/shard_map/all_to_all | solution.py:575
  62.7 4.3 %collective-permute-start.5 = (bf16[2,264,128]{2,1,0:T(8,128)(2,1)S(1)}, bf16[2,264,128]{2,1,0:T(8,128)(2,1)S(1)}, u32[]{:S(2)}, u32[]{:S(2)}) collective-permute-start(bf16[2,264,128]{2,1,0:T(8,128)(2,1)S(1)} %add_add_fusion.1), channel_id=1, source_target_pairs={{0,48},{64,112},{128,176},{192,240},{1,49},{65,113},{129,177},{193... | collective-permute-start | bytes 405512 | tf_op jit(solution)/shard_map/ppermute | solution.py:612
  67.0 1.3 collective-permute-start.4
  68.3 1.3 collective-permute-start.3
  69.6 2.9 %shard_map.97 = (f32[1024,128]{1,0:T(8,128)}, f32[1024,128]{1,0:T(8,128)}, f32[1024,128]{1,0:T(8,128)}) custom-call(s32[1]{0:T(128)} %bitcast.pos, bf16[16,264,128]{2,1,0:T(8,128)(2,1)S(1)} %all-to-all-done.x, f32[1,1024]{1,0:T(1,128)S(1)} %copy-done), custom_call_target="tpu_custom_call" | custom-call | flops 536870912 | bytes 2097152 | tf_op jit(solution)/shard_map/pallas_call | solution.py:629
  72.5 0.0 collective-permute-done.5
  72.5 2.6 %collective-permute-done.4 = bf16[2,264,128]{2,1,0:T(8,128)(2,1)S(1)} collective-permute-done((bf16[2,264,128]{2,1,0:T(8,128)(2,1)S(1)}, bf16[2,264,128]{2,1,0:T(8,128)(2,1)S(1)}, u32[]{:S(2)}, u32[]{:S(2)}) %collective-permute-start.4) | collective-permute-done | bytes 135200 | tf_op jit(solution)/shard_map/ppermute | solution.py:612
  75.2 2.7 %collective-permute-done.3 = bf16[2,264,128]{2,1,0:T(8,128)(2,1)S(1)} collective-permute-done((bf16[2,264,128]{2,1,0:T(8,128)(2,1)S(1)}, bf16[2,264,128]{2,1,0:T(8,128)(2,1)S(1)}, u32[]{:S(2)}, u32[]{:S(2)}) %collective-permute-start.3) | collective-permute-done | bytes 135200 | tf_op jit(solution)/shard_map/ppermute | solution.py:612
  77.9 2.3 %shard_map.98 = (f32[1024,128]{1,0:T(8,128)}, f32[1024,128]{1,0:T(8,128)}, f32[1024,128]{1,0:T(8,128)}, f32[3,128,128]{2,1,0:T(8,128)S(1)}, bf16[3,128,128]{2,1,0:T(8,128)(2,1)S(1)}) custom-call(s32[1]{0:T(128)} %bitcast.pos, bf16[16,264,128]{2,1,0:T(8,128)(2,1)S(1)} %all-to-all-done.x, f32[1,1024]{1,0:T(1,128)S(1)} %copy-done, ...), custom_call_target="tpu_custom_call" | custom-call | flops 536870912 | bytes 4194304 | tf_op jit(solution)/shard_map/pallas_call | solution.py:639
  80.2 1.3 collective-permute-start.8
  81.5 1.3 collective-permute-start.7
  82.8 1.3 collective-permute-start.6
  84.1 4.6 %collective-permute-start.9 = (bf16[264,128]{1,0:T(8,128)(2,1)S(1)}, bf16[264,128]{1,0:T(8,128)(2,1)S(1)}, u32[]{:S(2)}, u32[]{:S(2)}) collective-permute-start(bf16[264,128]{1,0:T(8,128)(2,1)S(1)} %get-tuple-element.51), channel_id=1, source_target_pairs={{0,16},{16,32},{32,48},{48,64},{64,80},{80,96},{96,112},{112,128},... | collective-permute-start | bytes 202760 | tf_op jit(solution)/shard_map/ppermute | solution.py:657
  88.7 5.9 %collective-permute-start.10 = (bf16[264,128]{1,0:T(8,128)(2,1)S(1)}, bf16[264,128]{1,0:T(8,128)(2,1)S(1)}, u32[]{:S(2)}, u32[]{:S(2)}) collective-permute-start(bf16[264,128]{1,0:T(8,128)(2,1)S(1)} %get-tuple-element.52), channel_id=1, source_target_pairs={{16,0},{32,16},{48,32},{64,48},{80,64},{96,80},{112,96},{128,112},... | collective-permute-start | bytes 202760 | tf_op jit(solution)/shard_map/ppermute | solution.py:658
  94.6 0.0 collective-permute-done.8
  94.6 0.0 collective-permute-done.7
  94.6 0.0 collective-permute-done.6
  94.7 0.5 collective-permute-done.9.before
  95.2 1.3 collective-permute-done.10.after
  96.5 2.1 %all-to-all-done.1.y = bf16[16,392,128]{2,1,0:T(8,128)(2,1)S(1)} async-done(((bf16[16,392,128]{2,1,0:T(8,128)(2,1)}), bf16[16,392,128]{2,1,0:T(8,128)(2,1)S(1)}, u32[]{:S(2)}, u32[]{:S(2)}) %all-to-all-start.1) | async-done | bytes 1605664 | tf_op jit(solution)/shard_map/all_to_all | solution.py:575
  98.7 4.1 %shard_map.99 = (bf16[16,192,128]{2,1,0:T(8,128)(2,1)}, bf16[16,392,128]{2,1,0:T(8,128)(2,1)}) custom-call(s32[32,128]{1,0:T(8,128)S(1)} %shard_map.94.table, bf16[16,264,128]{2,1,0:T(8,128)(2,1)S(1)} %all-to-all-done.x, bf16[16,392,128]{2,1,0:T(8,128)(2,1)S(1)} %all-to-all-done.1.y), custom_call_target="tpu_custom_call" | custom-call | flops 536870912 | bytes 4194304 | tf_op jit(solution)/shard_map/pallas_call | solution.py:665
  102.8 5.8 %all-to-all-start.2 = ((bf16[16,192,128]{2,1,0:T(8,128)(2,1)}), bf16[16,192,128]{2,1,0:T(8,128)(2,1)S(1)}, u32[]{:S(2)}, u32[]{:S(2)}) async-start(bf16[16,192,128]{2,1,0:T(8,128)(2,1)} %get-tuple-element.74), calls=%async_computation.2 | async-start | bytes 1572864 | tf_op jit(solution)/shard_map/all_to_all | solution.py:575
  108.6 2.0 %collective-permute-start.11 = (bf16[3,128,128]{2,1,0:T(8,128)(2,1)S(1)}, bf16[3,128,128]{2,1,0:T(8,128)(2,1)S(1)}, u32[]{:S(2)}, u32[]{:S(2)}) collective-permute-start(bf16[3,128,128]{2,1,0:T(8,128)(2,1)S(1)} %convert_element_type.24), channel_id=1, source_target_pairs={{64,0},{192,128},{65,1},{193,129},{66,2},{194,130},{67,3},{195,131... | collective-permute-start | bytes 294920 | tf_op jit(solution)/shard_map/ppermute | solution.py:677
  110.6 5.5 %shard_map.100 = (f32[1024,128]{1,0:T(8,128)}, f32[1024,128]{1,0:T(8,128)}) custom-call(s32[32,128]{1,0:T(8,128)S(1)} %shard_map.94.table, bf16[16,264,128]{2,1,0:T(8,128)(2,1)S(1)} %all-to-all-done.x, bf16[16,392,128]{2,1,0:T(8,128)(2,1)} %get-tuple-element.66.y_far), custom_call_target="tpu_custom_call" | custom-call | flops 536870912 | bytes 4194304 | tf_op jit(solution)/shard_map/pallas_call | solution.py:679
  116.1 3.7 %shard_map.101 = (bf16[16,192,128]{2,1,0:T(8,128)(2,1)}, f32[1024,128]{1,0:T(8,128)S(1)}, f32[256,128]{1,0:T(8,128)S(1)}) custom-call(s32[1]{0:T(128)} %bitcast.pos, bf16[16,264,128]{2,1,0:T(8,128)(2,1)S(1)} %all-to-all-done.x, f32[1,1024]{1,0:T(1,128)S(1)} %copy-done, bf16[264,128]{1,0:T(8,128)(2,1)S(1)} %collective-permute-done.9.before, ...), custom_call_target="tpu_custom_call" | custom-call | flops 16777216 | bytes 4194304 | tf_op jit(solution)/shard_map/pallas_call | solution.py:689
  119.8 1.2 collective-permute-done.11
  121.0 0.7 collective-permute-start.12
  121.7 0.0 collective-permute-done.12
  121.8 6.3 %all-to-all-done.2.z = bf16[16,192,128]{2,1,0:T(8,128)(2,1)S(1)} async-done(((bf16[16,192,128]{2,1,0:T(8,128)(2,1)}), bf16[16,192,128]{2,1,0:T(8,128)(2,1)S(1)}, u32[]{:S(2)}, u32[]{:S(2)}) %all-to-all-start.2) | async-done | bytes 786464 | tf_op jit(solution)/shard_map/all_to_all | solution.py:575
  128.1 2.0 %shard_map.102 = bf16[16,192,128]{2,1,0:T(8,128)(2,1)} custom-call(s32[1]{0:T(128)} %bitcast.pos, s32[32,128]{1,0:T(8,128)S(1)} %shard_map.94.table, f32[1024,128]{1,0:T(8,128)S(1)} %get-tuple-element.72.dq, f32[256,128]{1,0:T(8,128)S(1)} %get-tuple-element.73.edge, bf16[16,192,128]{2,1,0:T(8,128)(2,1)S(1)} %all-to-all-done.2.z, ...), custom_call_target="tpu_custom_call", output_to_operand_aliasing={{}: (6, {})} | custom-call | bytes 4194304 | tf_op jit(solution)/shard_map/pallas_call | solution.py:708
  130.0 29.5 %all_to_all.20.w = bf16[16,192,128]{2,1,0:T(8,128)(2,1)S(1)} all-to-all(bf16[16,192,128]{2,1,0:T(8,128)(2,1)} %shard_map.102), channel_id=1, replica_groups=mesh['seq'=16,'head'=16] {'head'}, dimensions={0} | all-to-all | bytes 1572864 | tf_op jit(solution)/shard_map/all_to_all | solution.py:575
  159.6 1.1 shard_map.103
  (8 shorter events, 0.2 us)
Async XLA Ops:
  3.2 10.2 %copy-start.1 = (s32[256,3]{0,1:T(4,128)S(1)}, s32[256,3]{0,1:T(4,128)}, u32[]{:S(2)}) copy-start(s32[256,3]{0,1:T(4,128)} %param.13) | copy-start | bytes 9220
  3.2 42.5 %copy-start = (f32[1,1024]{1,0:T(1,128)S(1)}, f32[1,1024]{1,0:T(1,128)}, u32[]{:S(2)}) copy-start(f32[1,1024]{1,0:T(1,128)} %lse.7) | copy-start | bytes 12292
  3.2 42.5 %all-to-all-start = ((bf16[16,264,128]{2,1,0:T(8,128)(2,1)}), bf16[16,264,128]{2,1,0:T(8,128)(2,1)S(1)}, u32[]{:S(2)}, u32[]{:S(2)}) async-start(bf16[16,264,128]{2,1,0:T(8,128)(2,1)} %shard_map.95), calls=%async_computation | async-start | bytes 2162688 | tf_op jit(solution)/shard_map/all_to_all | solution.py:575
  47.9 2.7 %collective-permute-start.2 = (bf16[2,264,128]{2,1,0:T(8,128)(2,1)S(1)}, bf16[2,264,128]{2,1,0:T(8,128)(2,1)S(1)}, u32[]{:S(2)}, u32[]{:S(2)}) collective-permute-start(bf16[2,264,128]{2,1,0:T(8,128)(2,1)S(1)} %get-tuple-element.40), channel_id=1, source_target_pairs={{0,192},{1,193},{2,194},{3,195},{4,196},{5,197},{6,198},{7,199},{8... | collective-permute-start | bytes 405512 | tf_op jit(solution)/shard_map/ppermute | solution.py:612
  48.6 2.0 %collective-permute-start.1 = (bf16[2,264,128]{2,1,0:T(8,128)(2,1)S(1)}, bf16[2,264,128]{2,1,0:T(8,128)(2,1)S(1)}, u32[]{:S(2)}, u32[]{:S(2)}) collective-permute-start(bf16[2,264,128]{2,1,0:T(8,128)(2,1)S(1)} %get-tuple-element.40), channel_id=1, source_target_pairs={{0,128},{1,129},{2,130},{3,131},{4,132},{5,133},{6,134},{7,135},{8... | collective-permute-start | bytes 405512 | tf_op jit(solution)/shard_map/ppermute | solution.py:612
  49.3 9.8 %collective-permute-start = (bf16[2,264,128]{2,1,0:T(8,128)(2,1)S(1)}, bf16[2,264,128]{2,1,0:T(8,128)(2,1)S(1)}, u32[]{:S(2)}, u32[]{:S(2)}) collective-permute-start(bf16[2,264,128]{2,1,0:T(8,128)(2,1)S(1)} %get-tuple-element.40), channel_id=1, source_target_pairs={{0,64},{1,65},{2,66},{3,67},{4,68},{5,69},{6,70},{7,71},{8,72},{9,... | collective-permute-start | bytes 405512 | tf_op jit(solution)/shard_map/ppermute | solution.py:612
  59.1 39.6 %all-to-all-start.1 = ((bf16[16,392,128]{2,1,0:T(8,128)(2,1)}), bf16[16,392,128]{2,1,0:T(8,128)(2,1)S(1)}, u32[]{:S(2)}, u32[]{:S(2)}) async-start(bf16[16,392,128]{2,1,0:T(8,128)(2,1)} %get-tuple-element.42), calls=%async_computation.1 | async-start | bytes 3211264 | tf_op jit(solution)/shard_map/all_to_all | solution.py:575
  62.7 9.8 %collective-permute-start.5 = (bf16[2,264,128]{2,1,0:T(8,128)(2,1)S(1)}, bf16[2,264,128]{2,1,0:T(8,128)(2,1)S(1)}, u32[]{:S(2)}, u32[]{:S(2)}) collective-permute-start(bf16[2,264,128]{2,1,0:T(8,128)(2,1)S(1)} %add_add_fusion.1), channel_id=1, source_target_pairs={{0,48},{64,112},{128,176},{192,240},{1,49},{65,113},{129,177},{193... | collective-permute-start | bytes 405512 | tf_op jit(solution)/shard_map/ppermute | solution.py:612
  67.0 8.2 %collective-permute-start.4 = (bf16[2,264,128]{2,1,0:T(8,128)(2,1)S(1)}, bf16[2,264,128]{2,1,0:T(8,128)(2,1)S(1)}, u32[]{:S(2)}, u32[]{:S(2)}) collective-permute-start(bf16[2,264,128]{2,1,0:T(8,128)(2,1)S(1)} %add_add_fusion.1), channel_id=1, source_target_pairs={{0,32},{64,96},{128,160},{192,224},{1,33},{65,97},{129,161},{193,2... | collective-permute-start | bytes 405512 | tf_op jit(solution)/shard_map/ppermute | solution.py:612
  68.3 9.6 %collective-permute-start.3 = (bf16[2,264,128]{2,1,0:T(8,128)(2,1)S(1)}, bf16[2,264,128]{2,1,0:T(8,128)(2,1)S(1)}, u32[]{:S(2)}, u32[]{:S(2)}) collective-permute-start(bf16[2,264,128]{2,1,0:T(8,128)(2,1)S(1)} %add_add_fusion.1), channel_id=1, source_target_pairs={{0,16},{64,80},{128,144},{192,208},{1,17},{65,81},{129,145},{193,2... | collective-permute-start | bytes 405512 | tf_op jit(solution)/shard_map/ppermute | solution.py:612
  80.2 14.4 %collective-permute-start.8 = (bf16[3,128,128]{2,1,0:T(8,128)(2,1)S(1)}, bf16[3,128,128]{2,1,0:T(8,128)(2,1)S(1)}, u32[]{:S(2)}, u32[]{:S(2)}) collective-permute-start(bf16[3,128,128]{2,1,0:T(8,128)(2,1)S(1)} %get-tuple-element.50), channel_id=1, source_target_pairs={{48,0},{112,64},{176,128},{240,192},{49,1},{113,65},{177,129},{241... | collective-permute-start | bytes 294920 | tf_op jit(solution)/shard_map/ppermute | solution.py:617
  81.5 13.1 %collective-permute-start.7 = (bf16[3,128,128]{2,1,0:T(8,128)(2,1)S(1)}, bf16[3,128,128]{2,1,0:T(8,128)(2,1)S(1)}, u32[]{:S(2)}, u32[]{:S(2)}) collective-permute-start(bf16[3,128,128]{2,1,0:T(8,128)(2,1)S(1)} %get-tuple-element.50), channel_id=1, source_target_pairs={{32,0},{96,64},{160,128},{224,192},{33,1},{97,65},{161,129},{225,1... | collective-permute-start | bytes 294920 | tf_op jit(solution)/shard_map/ppermute | solution.py:617
  82.8 11.8 %collective-permute-start.6 = (bf16[3,128,128]{2,1,0:T(8,128)(2,1)S(1)}, bf16[3,128,128]{2,1,0:T(8,128)(2,1)S(1)}, u32[]{:S(2)}, u32[]{:S(2)}) collective-permute-start(bf16[3,128,128]{2,1,0:T(8,128)(2,1)S(1)} %get-tuple-element.50), channel_id=1, source_target_pairs={{16,0},{80,64},{144,128},{208,192},{17,1},{81,65},{145,129},{209,1... | collective-permute-start | bytes 294920 | tf_op jit(solution)/shard_map/ppermute | solution.py:617
  84.1 11.1 %collective-permute-start.9 = (bf16[264,128]{1,0:T(8,128)(2,1)S(1)}, bf16[264,128]{1,0:T(8,128)(2,1)S(1)}, u32[]{:S(2)}, u32[]{:S(2)}) collective-permute-start(bf16[264,128]{1,0:T(8,128)(2,1)S(1)} %get-tuple-element.51), channel_id=1, source_target_pairs={{0,16},{16,32},{32,48},{48,64},{64,80},{80,96},{96,112},{112,128},... | collective-permute-start | bytes 202760 | tf_op jit(solution)/shard_map/ppermute | solution.py:657
  88.7 7.8 %collective-permute-start.10 = (bf16[264,128]{1,0:T(8,128)(2,1)S(1)}, bf16[264,128]{1,0:T(8,128)(2,1)S(1)}, u32[]{:S(2)}, u32[]{:S(2)}) collective-permute-start(bf16[264,128]{1,0:T(8,128)(2,1)S(1)} %get-tuple-element.52), channel_id=1, source_target_pairs={{16,0},{32,16},{48,32},{64,48},{80,64},{96,80},{112,96},{128,112},... | collective-permute-start | bytes 202760 | tf_op jit(solution)/shard_map/ppermute | solution.py:658
  102.8 25.3 %all-to-all-start.2 = ((bf16[16,192,128]{2,1,0:T(8,128)(2,1)}), bf16[16,192,128]{2,1,0:T(8,128)(2,1)S(1)}, u32[]{:S(2)}, u32[]{:S(2)}) async-start(bf16[16,192,128]{2,1,0:T(8,128)(2,1)} %get-tuple-element.74), calls=%async_computation.2 | async-start | bytes 1572864 | tf_op jit(solution)/shard_map/all_to_all | solution.py:575
  108.6 12.4 %collective-permute-start.11 = (bf16[3,128,128]{2,1,0:T(8,128)(2,1)S(1)}, bf16[3,128,128]{2,1,0:T(8,128)(2,1)S(1)}, u32[]{:S(2)}, u32[]{:S(2)}) collective-permute-start(bf16[3,128,128]{2,1,0:T(8,128)(2,1)S(1)} %convert_element_type.24), channel_id=1, source_target_pairs={{64,0},{192,128},{65,1},{193,129},{66,2},{194,130},{67,3},{195,131... | collective-permute-start | bytes 294920 | tf_op jit(solution)/shard_map/ppermute | solution.py:677
  121.0 0.7 collective-permute-start.12

commit v7 on v6

--- a/solution.py
+++ b/solution.py
@@ -133,32 +133,34 @@
     return pair if b % 2 else pltpu.roll(pair, BLK, 1)
 
 
-def select_body(pos, table, x, lse, dest, last, first, glob, ext, out, sem):
+def block_ext(x, b, norm):
     row = lax.broadcasted_iota(jnp.int32, (8, HD), 0)
+    high, low = pieces(norm)
+    tile = jnp.where(row == 0, high, jnp.where(row == 1, low, 0.0))
+    return jnp.where(left_half(), x[b, 256:264].astype(F32), tile)
+
+
+def slab_body(pos, x, lse, last, first, glob):
     lse_all = lse[...]
-
-    def ext_of(b, norm):
-        high, low = pieces(norm)
-        tile = jnp.where(row == 0, high, jnp.where(row == 1, low, 0.0))
-        return jnp.where(left_half(), x[b, 256:264].astype(F32), tile)
-
+    keep = pos[0] == 0
+    for b in (0, 1, NB - 1):
+        full = block_ext(x, b, norm_rows(lse_all, b)).astype(BF16)
+        if b < GLOB:
+            glob[b, 0:256] = jnp.where(keep, x[b, 0:256], jnp.zeros((256, HD), BF16))
+            glob[b, 256:264] = jnp.where(keep, full, jnp.zeros((8, HD), BF16))
+        for slab, owner in ((first, 0), (last, NB - 1)):
+            if b == owner:
+                slab[0:256] = x[b, 0:256]
+                slab[256:264] = full
+
+
+def select_body(pos, table, x, lse, dest, ext, out, sem):
+    lse_all = lse[...]
     for b in range(NB):
         norm = norm_rows(lse_all, b)
         if b < GLOB:
-            plain = ext_of(b, norm)
-            full = plain.astype(BF16)
-            if b == 0:
-                first[0:256] = x[b, 0:256]
-                first[256:264] = full
-            keep = pos[0] == 0
-            glob[b, 0:256] = jnp.where(keep, x[b, 0:256], jnp.zeros((256, HD), BF16))
-            glob[b, 256:264] = jnp.where(keep, full, jnp.zeros((8, HD), BF16))
             norm = jnp.where(pos[0] == 0, OFF, norm)
-        ext[b] = ext_of(b, norm)
-        if b == NB - 1:
-            last[0:256] = x[b, 0:256]
-            last[256:264] = ext[b].astype(BF16)
-
+        ext[b] = block_ext(x, b, norm)
 
     def step(i, carry):
         for c in range(4):
@@ -594,11 +596,18 @@
     table = call(table_body, struct((2 * NB, HD), jnp.int32), [SM, VM], VM, nbytes=1 << 14)(
         pos, rand_blocks.reshape(NB, NB * RAND)
     )
-    y, last, first, glob = call(
+    last, first, glob = call(
+        slab_body,
+        (struct((SLAB, HD)), struct((SLAB, HD)), struct((GLOB, SLAB, HD))),
+        [SM, VM, VM],
+        (VM,) * 3,
+        nbytes=1 << 18,
+    )(pos, x, logsumexp)
+    y = call(
         select_body,
-        (far((NB, PAIR, HD)), struct((SLAB, HD)), struct((SLAB, HD)), struct((GLOB, SLAB, HD))),
+        far((NB, PAIR, HD)),
         [SM, SM, VM, VM],
-        (HB, VM, VM, VM),
+        HB,
         nbytes=3 << 20,
         scratch=[
             pltpu.VMEM((NB, 8, HD), F32),
@@ -606,6 +615,7 @@
             dma((NB,)),
         ],
     )(pos, table, x, logsumexp)
+
     def spread(glob, reach, starts):
         source = glob
         for n in (1, 2, 3):
@@ -656,7 +666,7 @@
     gpart = collect(gpart, glow, 1, corners)
     before = lax.ppermute(last, "seq", [(s, s + 1) for s in range(groups - 1)])
     after = lax.ppermute(first, "seq", [(s + 1, s) for s in range(groups - 1)])
-    y, gpart, before, after = lax.optimization_barrier((y, gpart, before, after))
+    y, gpart = lax.optimization_barrier((y, gpart))
     stage_space = [
         pltpu.VMEM((3, HD, HD), F32),
         pltpu.VMEM((3, HD, HD), F32),
@@ -672,7 +682,7 @@
         scratch=[pltpu.VMEM((NB, RAND * BLK, HD), BF16), dma((NB,)), dma((NB // 2,))]
         + stage_space,
     )(table, x, y)
-    z, gpart, y = lax.optimization_barrier((z, gpart, y))
+    z, gpart, y, before, after = lax.optimization_barrier((z, gpart, y, before, after))
     z = exchange(z, "seq")
     moved = lax.ppermute(gpart.astype(BF16), "seq", [(4, 0), (12, 8)])
     gpart = gpart + moved.astype(F32)

time: 162 us -> 160 us (0.988)
  waiting for transfers between devices: 57.1 us -> 54.6 us
    ppermute x6, waiting for transfers between devices: 13.8 us -> 11.1 us  [spread(): lax.ppermute(source, 'seq', [(s, s + n * reach) for s in starts])]
    all_to_all x3, waiting for transfers between devices: 40.3 us -> 42.5 us  [exchange(): return lax.all_to_all(x, axis, split_axis=0, concat_axis=0, tiled=True)]
  transfers between devices with their start and end apart: 16 -> 16, of which waited for: 9 -> 7; matrix products, arithmetic and copies ran while one was open for 0% -> 0% of each run, Pallas kernels for 9% -> 13%
where the time goes in v7:
time: 160 us; the launch traced here: 158 us
  waiting for transfers between devices  54.6 us (34%)
  starting transfers between devices  45.8 us (29%)
  blocking collectives  29.6 us (18%)
  Pallas kernels  26.5 us (17%)
    all_to_all x3, waiting for transfers between devices, exchange(): return lax.all_to_all(x, axis, split_axis=0, concat_axis=0, tiled=True)  42.5 us
    all_to_all x1, blocking collectives, exchange(): return lax.all_to_all(x, axis, split_axis=0, concat_axis=0, tiled=True)  29.6 us
    all_to_all x3, starting transfers between devices, exchange(): return lax.all_to_all(x, axis, split_axis=0, concat_axis=0, tiled=True)  19.3 us
    ppermute x6, waiting for transfers between devices, spread(): lax.ppermute(source, 'seq', [(s, s + n * reach) for s in starts])  11.1 us
    ppermute x6, starting transfers between devices, spread(): lax.ppermute(source, 'seq', [(s, s + n * reach) for s in starts])  9.49 us
    ppermute x1, starting transfers between devices, per_device(): after = lax.ppermute(first, 'seq', [(s + 1, s) for s in range(groups - 1)])  5.93 us
    pallas_call x1, Pallas kernels, per_device(): call(rand_key_body, (far_acc, far_acc), [SM, VM, HB], (HB,) * 2, flops=1...  5.45 us
    ppermute x1, starting transfers between devices, per_device(): before = lax.ppermute(last, 'seq', [(s, s + 1) for s in range(groups - 1)])  4.55 us
  transfers between devices with their start and end apart: 16, of which 7 were waited for; matrix products, arithmetic and copies ran while one was open for 0% of the time, Pallas kernels for 13%

profile of v7, /device:TPU:32, one launch (start us, length us, event | category | flops | bytes accessed | tf_op | source)
XLA Modules:
  0.0 158.0 jit_solution(7781113489154464156)
XLA Ops:
  0.6 2.5 %shard_map.95 = bf16[16,264,128]{2,1,0:T(8,128)(2,1)} custom-call(bf16[64,2048]{1,0:T(8,128)(2,1)} %q.1, bf16[64,2048]{1,0:T(8,128)(2,1)} %k.1, bf16[64,2048]{1,0:T(8,128)(2,1)} %v.1, bf16[64,2048]{1,0:T(8,128)(2,1)} %o.1, bf16[64,2048]{1,0:T(8,128)(2,1)} %g.1), custom_call_target="tpu_custom_call" | custom-call | bytes 1310720 | tf_op jit(solution)/shard_map/pallas_call | solution.py:587
  3.2 0.0 copy-start
  3.2 0.0 copy-start.1
  3.2 10.1 %all-to-all-start = ((bf16[16,264,128]{2,1,0:T(8,128)(2,1)}), bf16[16,264,128]{2,1,0:T(8,128)(2,1)S(1)}, u32[]{:S(2)}, u32[]{:S(2)}) async-start(bf16[16,264,128]{2,1,0:T(8,128)(2,1)} %shard_map.95), calls=%async_computation | async-start | bytes 2162688 | tf_op jit(solution)/shard_map/all_to_all | solution.py:577
  13.3 32.3 %all-to-all-done.x = bf16[16,264,128]{2,1,0:T(8,128)(2,1)S(1)} async-done(((bf16[16,264,128]{2,1,0:T(8,128)(2,1)}), bf16[16,264,128]{2,1,0:T(8,128)(2,1)S(1)}, u32[]{:S(2)}, u32[]{:S(2)}) %all-to-all-start) | async-done | bytes 1081376 | tf_op jit(solution)/shard_map/all_to_all | solution.py:577
  45.7 0.1 shard_map.96
  45.7 0.7 collective-permute-start.2
  46.4 0.7 collective-permute-start.1
  47.1 1.3 collective-permute-start
  48.4 0.1 copy.12
  48.5 0.1 reshape.13.entries
  48.7 0.2 shard_map.94.table
  48.9 2.2 %shard_map.97 = bf16[16,392,128]{2,1,0:T(8,128)(2,1)} custom-call(s32[1]{0:T(128)} %bitcast.pos, s32[32,128]{1,0:T(8,128)S(1)} %shard_map.94.table, bf16[16,264,128]{2,1,0:T(8,128)(2,1)S(1)} %all-to-all-done.x, f32[1,1024]{1,0:T(1,128)S(1)} %copy-done), custom_call_target="tpu_custom_call" | custom-call | bytes 3145728 | tf_op jit(solution)/shard_map/pallas_call | solution.py:606
  51.1 0.0 collective-permute-done.2
  51.1 0.0 collective-permute-done.1
  51.2 5.7 %collective-permute-done = bf16[2,264,128]{2,1,0:T(8,128)(2,1)S(1)} collective-permute-done((bf16[2,264,128]{2,1,0:T(8,128)(2,1)S(1)}, bf16[2,264,128]{2,1,0:T(8,128)(2,1)S(1)}, u32[]{:S(2)}, u32[]{:S(2)}) %collective-permute-start) | collective-permute-done | bytes 135200 | tf_op jit(solution)/shard_map/ppermute | solution.py:622
  56.9 3.6 %all-to-all-start.1 = ((bf16[16,392,128]{2,1,0:T(8,128)(2,1)}), bf16[16,392,128]{2,1,0:T(8,128)(2,1)S(1)}, u32[]{:S(2)}, u32[]{:S(2)}) async-start(bf16[16,392,128]{2,1,0:T(8,128)(2,1)} %shard_map.97), calls=%async_computation.1 | async-start | bytes 3211264 | tf_op jit(solution)/shard_map/all_to_all | solution.py:577
  60.5 4.3 %collective-permute-start.5 = (bf16[2,264,128]{2,1,0:T(8,128)(2,1)S(1)}, bf16[2,264,128]{2,1,0:T(8,128)(2,1)S(1)}, u32[]{:S(2)}, u32[]{:S(2)}) collective-permute-start(bf16[2,264,128]{2,1,0:T(8,128)(2,1)S(1)} %add_add_fusion.1), channel_id=1, source_target_pairs={{0,48},{64,112},{128,176},{192,240},{1,49},{65,113},{129,177},{193... | collective-permute-start | bytes 405512 | tf_op jit(solution)/shard_map/ppermute | solution.py:622
  64.8 1.3 collective-permute-start.4
  66.1 1.3 collective-permute-start.3
  67.4 2.9 %shard_map.98 = (f32[1024,128]{1,0:T(8,128)}, f32[1024,128]{1,0:T(8,128)}, f32[1024,128]{1,0:T(8,128)}) custom-call(s32[1]{0:T(128)} %bitcast.pos, bf16[16,264,128]{2,1,0:T(8,128)(2,1)S(1)} %all-to-all-done.x, f32[1,1024]{1,0:T(1,128)S(1)} %copy-done), custom_call_target="tpu_custom_call" | custom-call | flops 536870912 | bytes 2097152 | tf_op jit(solution)/shard_map/pallas_call | solution.py:639
  70.3 0.0 collective-permute-done.5
  70.3 2.6 %collective-permute-done.4 = bf16[2,264,128]{2,1,0:T(8,128)(2,1)S(1)} collective-permute-done((bf16[2,264,128]{2,1,0:T(8,128)(2,1)S(1)}, bf16[2,264,128]{2,1,0:T(8,128)(2,1)S(1)}, u32[]{:S(2)}, u32[]{:S(2)}) %collective-permute-start.4) | collective-permute-done | bytes 135200 | tf_op jit(solution)/shard_map/ppermute | solution.py:622
  73.0 2.7 %collective-permute-done.3 = bf16[2,264,128]{2,1,0:T(8,128)(2,1)S(1)} collective-permute-done((bf16[2,264,128]{2,1,0:T(8,128)(2,1)S(1)}, bf16[2,264,128]{2,1,0:T(8,128)(2,1)S(1)}, u32[]{:S(2)}, u32[]{:S(2)}) %collective-permute-start.3) | collective-permute-done | bytes 135200 | tf_op jit(solution)/shard_map/ppermute | solution.py:622
  75.7 2.3 %shard_map.99 = (f32[1024,128]{1,0:T(8,128)}, f32[1024,128]{1,0:T(8,128)}, f32[1024,128]{1,0:T(8,128)}, f32[3,128,128]{2,1,0:T(8,128)S(1)}, bf16[3,128,128]{2,1,0:T(8,128)(2,1)S(1)}) custom-call(s32[1]{0:T(128)} %bitcast.pos, bf16[16,264,128]{2,1,0:T(8,128)(2,1)S(1)} %all-to-all-done.x, f32[1,1024]{1,0:T(1,128)S(1)} %copy-done, ...), custom_call_target="tpu_custom_call" | custom-call | flops 536870912 | bytes 4194304 | tf_op jit(solution)/shard_map/pallas_call | solution.py:649
  78.0 1.3 collective-permute-start.8
  79.3 1.3 collective-permute-start.7
  80.6 1.3 collective-permute-start.6
  81.9 4.6 %collective-permute-start.9 = (bf16[264,128]{1,0:T(8,128)(2,1)S(1)}, bf16[264,128]{1,0:T(8,128)(2,1)S(1)}, u32[]{:S(2)}, u32[]{:S(2)}) collective-permute-start(bf16[264,128]{1,0:T(8,128)(2,1)S(1)} %get-tuple-element.53), channel_id=1, source_target_pairs={{0,16},{16,32},{32,48},{48,64},{64,80},{80,96},{96,112},{112,128},... | collective-permute-start | bytes 202760 | tf_op jit(solution)/shard_map/ppermute | solution.py:667
  86.5 5.9 %collective-permute-start.10 = (bf16[264,128]{1,0:T(8,128)(2,1)S(1)}, bf16[264,128]{1,0:T(8,128)(2,1)S(1)}, u32[]{:S(2)}, u32[]{:S(2)}) collective-permute-start(bf16[264,128]{1,0:T(8,128)(2,1)S(1)} %get-tuple-element.54), channel_id=1, source_target_pairs={{16,0},{32,16},{48,32},{64,48},{80,64},{96,80},{112,96},{128,112},... | collective-permute-start | bytes 202760 | tf_op jit(solution)/shard_map/ppermute | solution.py:668
  92.4 0.0 collective-permute-done.8
  92.4 0.0 collective-permute-done.7
  92.5 0.0 collective-permute-done.6
  92.5 4.0 %all-to-all-done.1.y = bf16[16,392,128]{2,1,0:T(8,128)(2,1)S(1)} async-done(((bf16[16,392,128]{2,1,0:T(8,128)(2,1)}), bf16[16,392,128]{2,1,0:T(8,128)(2,1)S(1)}, u32[]{:S(2)}, u32[]{:S(2)}) %all-to-all-start.1) | async-done | bytes 1605664 | tf_op jit(solution)/shard_map/all_to_all | solution.py:577
  96.5 4.1 %shard_map.100 = (bf16[16,192,128]{2,1,0:T(8,128)(2,1)}, bf16[16,392,128]{2,1,0:T(8,128)(2,1)}) custom-call(s32[32,128]{1,0:T(8,128)S(1)} %shard_map.94.table, bf16[16,264,128]{2,1,0:T(8,128)(2,1)S(1)} %all-to-all-done.x, bf16[16,392,128]{2,1,0:T(8,128)(2,1)S(1)} %all-to-all-done.1.y), custom_call_target="tpu_custom_call" | custom-call | flops 536870912 | bytes 4194304 | tf_op jit(solution)/shard_map/pallas_call | solution.py:675
  100.6 0.0 collective-permute-done.9.before
  100.6 0.0 collective-permute-done.10.after
  100.6 5.5 %all-to-all-start.2 = ((bf16[16,192,128]{2,1,0:T(8,128)(2,1)}), bf16[16,192,128]{2,1,0:T(8,128)(2,1)S(1)}, u32[]{:S(2)}, u32[]{:S(2)}) async-start(bf16[16,192,128]{2,1,0:T(8,128)(2,1)} %get-tuple-element.72), calls=%async_computation.2 | async-start | bytes 1572864 | tf_op jit(solution)/shard_map/all_to_all | solution.py:577
  106.2 2.0 %collective-permute-start.11 = (bf16[3,128,128]{2,1,0:T(8,128)(2,1)S(1)}, bf16[3,128,128]{2,1,0:T(8,128)(2,1)S(1)}, u32[]{:S(2)}, u32[]{:S(2)}) collective-permute-start(bf16[3,128,128]{2,1,0:T(8,128)(2,1)S(1)} %convert_element_type.24), channel_id=1, source_target_pairs={{64,0},{192,128},{65,1},{193,129},{66,2},{194,130},{67,3},{195,131... | collective-permute-start | bytes 294920 | tf_op jit(solution)/shard_map/ppermute | solution.py:687
  108.2 5.4 %shard_map.101 = (f32[1024,128]{1,0:T(8,128)}, f32[1024,128]{1,0:T(8,128)}) custom-call(s32[32,128]{1,0:T(8,128)S(1)} %shard_map.94.table, bf16[16,264,128]{2,1,0:T(8,128)(2,1)S(1)} %all-to-all-done.x, bf16[16,392,128]{2,1,0:T(8,128)(2,1)} %get-tuple-element.64.y_far), custom_call_target="tpu_custom_call" | custom-call | flops 536870912 | bytes 4194304 | tf_op jit(solution)/shard_map/pallas_call | solution.py:689
  113.7 3.7 %shard_map.102 = (bf16[16,192,128]{2,1,0:T(8,128)(2,1)}, f32[1024,128]{1,0:T(8,128)S(1)}, f32[256,128]{1,0:T(8,128)S(1)}) custom-call(s32[1]{0:T(128)} %bitcast.pos, bf16[16,264,128]{2,1,0:T(8,128)(2,1)S(1)} %all-to-all-done.x, f32[1,1024]{1,0:T(1,128)S(1)} %copy-done, bf16[264,128]{1,0:T(8,128)(2,1)S(1)} %collective-permute-done.9.before, ...), custom_call_target="tpu_custom_call" | custom-call | flops 16777216 | bytes 4194304 | tf_op jit(solution)/shard_map/pallas_call | solution.py:699
  117.4 1.0 collective-permute-done.11
  118.5 0.7 collective-permute-start.12
  119.1 0.0 collective-permute-done.12
  119.2 6.2 %all-to-all-done.2.z = bf16[16,192,128]{2,1,0:T(8,128)(2,1)S(1)} async-done(((bf16[16,192,128]{2,1,0:T(8,128)(2,1)}), bf16[16,192,128]{2,1,0:T(8,128)(2,1)S(1)}, u32[]{:S(2)}, u32[]{:S(2)}) %all-to-all-start.2) | async-done | bytes 786464 | tf_op jit(solution)/shard_map/all_to_all | solution.py:577
  125.4 2.0 %shard_map.103 = bf16[16,192,128]{2,1,0:T(8,128)(2,1)} custom-call(s32[1]{0:T(128)} %bitcast.pos, s32[32,128]{1,0:T(8,128)S(1)} %shard_map.94.table, f32[1024,128]{1,0:T(8,128)S(1)} %get-tuple-element.70.dq, f32[256,128]{1,0:T(8,128)S(1)} %get-tuple-element.71.edge, bf16[16,192,128]{2,1,0:T(8,128)(2,1)S(1)} %all-to-all-done.2.z, ...), custom_call_target="tpu_custom_call", output_to_operand_aliasing={{}: (6, {})} | custom-call | bytes 4194304 | tf_op jit(solution)/shard_map/pallas_call | solution.py:718
  127.4 29.6 %all_to_all.20.w = bf16[16,192,128]{2,1,0:T(8,128)(2,1)S(1)} all-to-all(bf16[16,192,128]{2,1,0:T(8,128)(2,1)} %shard_map.103), channel_id=1, replica_groups=mesh['seq'=16,'head'=16] {'head'}, dimensions={0} | all-to-all | bytes 1572864 | tf_op jit(solution)/shard_map/all_to_all | solution.py:577
  156.9 1.1 shard_map.104
  (9 shorter events, 0.2 us)
Async XLA Ops:
  3.2 42.5 %copy-start = (f32[1,1024]{1,0:T(1,128)S(1)}, f32[1,1024]{1,0:T(1,128)}, u32[]{:S(2)}) copy-start(f32[1,1024]{1,0:T(1,128)} %lse.9) | copy-start | bytes 12292
  3.2 45.2 %copy-start.1 = (s32[256,3]{0,1:T(4,128)S(1)}, s32[256,3]{0,1:T(4,128)}, u32[]{:S(2)}) copy-start(s32[256,3]{0,1:T(4,128)} %param.13) | copy-start | bytes 9220
  3.2 42.5 %all-to-all-start = ((bf16[16,264,128]{2,1,0:T(8,128)(2,1)}), bf16[16,264,128]{2,1,0:T(8,128)(2,1)S(1)}, u32[]{:S(2)}, u32[]{:S(2)}) async-start(bf16[16,264,128]{2,1,0:T(8,128)(2,1)} %shard_map.95), calls=%async_computation | async-start | bytes 2162688 | tf_op jit(solution)/shard_map/all_to_all | solution.py:577
  45.7 5.4 %collective-permute-start.2 = (bf16[2,264,128]{2,1,0:T(8,128)(2,1)S(1)}, bf16[2,264,128]{2,1,0:T(8,128)(2,1)S(1)}, u32[]{:S(2)}, u32[]{:S(2)}) collective-permute-start(bf16[2,264,128]{2,1,0:T(8,128)(2,1)S(1)} %get-tuple-element.39), channel_id=1, source_target_pairs={{0,192},{1,193},{2,194},{3,195},{4,196},{5,197},{6,198},{7,199},{8... | collective-permute-start | bytes 405512 | tf_op jit(solution)/shard_map/ppermute | solution.py:622
  46.4 4.7 %collective-permute-start.1 = (bf16[2,264,128]{2,1,0:T(8,128)(2,1)S(1)}, bf16[2,264,128]{2,1,0:T(8,128)(2,1)S(1)}, u32[]{:S(2)}, u32[]{:S(2)}) collective-permute-start(bf16[2,264,128]{2,1,0:T(8,128)(2,1)S(1)} %get-tuple-element.39), channel_id=1, source_target_pairs={{0,128},{1,129},{2,130},{3,131},{4,132},{5,133},{6,134},{7,135},{8... | collective-permute-start | bytes 405512 | tf_op jit(solution)/shard_map/ppermute | solution.py:622
  47.1 9.8 %collective-permute-start = (bf16[2,264,128]{2,1,0:T(8,128)(2,1)S(1)}, bf16[2,264,128]{2,1,0:T(8,128)(2,1)S(1)}, u32[]{:S(2)}, u32[]{:S(2)}) collective-permute-start(bf16[2,264,128]{2,1,0:T(8,128)(2,1)S(1)} %get-tuple-element.39), channel_id=1, source_target_pairs={{0,64},{1,65},{2,66},{3,67},{4,68},{5,69},{6,70},{7,71},{8,72},{9,... | collective-permute-start | bytes 405512 | tf_op jit(solution)/shard_map/ppermute | solution.py:622
  56.9 39.6 %all-to-all-start.1 = ((bf16[16,392,128]{2,1,0:T(8,128)(2,1)}), bf16[16,392,128]{2,1,0:T(8,128)(2,1)S(1)}, u32[]{:S(2)}, u32[]{:S(2)}) async-start(bf16[16,392,128]{2,1,0:T(8,128)(2,1)} %shard_map.97), calls=%async_computation.1 | async-start | bytes 3211264 | tf_op jit(solution)/shard_map/all_to_all | solution.py:577
  60.5 9.8 %collective-permute-start.5 = (bf16[2,264,128]{2,1,0:T(8,128)(2,1)S(1)}, bf16[2,264,128]{2,1,0:T(8,128)(2,1)S(1)}, u32[]{:S(2)}, u32[]{:S(2)}) collective-permute-start(bf16[2,264,128]{2,1,0:T(8,128)(2,1)S(1)} %add_add_fusion.1), channel_id=1, source_target_pairs={{0,48},{64,112},{128,176},{192,240},{1,49},{65,113},{129,177},{193... | collective-permute-start | bytes 405512 | tf_op jit(solution)/shard_map/ppermute | solution.py:622
  64.8 8.2 %collective-permute-start.4 = (bf16[2,264,128]{2,1,0:T(8,128)(2,1)S(1)}, bf16[2,264,128]{2,1,0:T(8,128)(2,1)S(1)}, u32[]{:S(2)}, u32[]{:S(2)}) collective-permute-start(bf16[2,264,128]{2,1,0:T(8,128)(2,1)S(1)} %add_add_fusion.1), channel_id=1, source_target_pairs={{0,32},{64,96},{128,160},{192,224},{1,33},{65,97},{129,161},{193,2... | collective-permute-start | bytes 405512 | tf_op jit(solution)/shard_map/ppermute | solution.py:622
  66.1 9.6 %collective-permute-start.3 = (bf16[2,264,128]{2,1,0:T(8,128)(2,1)S(1)}, bf16[2,264,128]{2,1,0:T(8,128)(2,1)S(1)}, u32[]{:S(2)}, u32[]{:S(2)}) collective-permute-start(bf16[2,264,128]{2,1,0:T(8,128)(2,1)S(1)} %add_add_fusion.1), channel_id=1, source_target_pairs={{0,16},{64,80},{128,144},{192,208},{1,17},{65,81},{129,145},{193,2... | collective-permute-start | bytes 405512 | tf_op jit(solution)/shard_map/ppermute | solution.py:622
  78.0 14.4 %collective-permute-start.8 = (bf16[3,128,128]{2,1,0:T(8,128)(2,1)S(1)}, bf16[3,128,128]{2,1,0:T(8,128)(2,1)S(1)}, u32[]{:S(2)}, u32[]{:S(2)}) collective-permute-start(bf16[3,128,128]{2,1,0:T(8,128)(2,1)S(1)} %get-tuple-element.48), channel_id=1, source_target_pairs={{48,0},{112,64},{176,128},{240,192},{49,1},{113,65},{177,129},{241... | collective-permute-start | bytes 294920 | tf_op jit(solution)/shard_map/ppermute | solution.py:627
  79.3 13.1 %collective-permute-start.7 = (bf16[3,128,128]{2,1,0:T(8,128)(2,1)S(1)}, bf16[3,128,128]{2,1,0:T(8,128)(2,1)S(1)}, u32[]{:S(2)}, u32[]{:S(2)}) collective-permute-start(bf16[3,128,128]{2,1,0:T(8,128)(2,1)S(1)} %get-tuple-element.48), channel_id=1, source_target_pairs={{32,0},{96,64},{160,128},{224,192},{33,1},{97,65},{161,129},{225,1... | collective-permute-start | bytes 294920 | tf_op jit(solution)/shard_map/ppermute | solution.py:627
  80.6 11.8 %collective-permute-start.6 = (bf16[3,128,128]{2,1,0:T(8,128)(2,1)S(1)}, bf16[3,128,128]{2,1,0:T(8,128)(2,1)S(1)}, u32[]{:S(2)}, u32[]{:S(2)}) collective-permute-start(bf16[3,128,128]{2,1,0:T(8,128)(2,1)S(1)} %get-tuple-element.48), channel_id=1, source_target_pairs={{16,0},{80,64},{144,128},{208,192},{17,1},{81,65},{145,129},{209,1... | collective-permute-start | bytes 294920 | tf_op jit(solution)/shard_map/ppermute | solution.py:627
  81.9 18.7 %collective-permute-start.9 = (bf16[264,128]{1,0:T(8,128)(2,1)S(1)}, bf16[264,128]{1,0:T(8,128)(2,1)S(1)}, u32[]{:S(2)}, u32[]{:S(2)}) collective-permute-start(bf16[264,128]{1,0:T(8,128)(2,1)S(1)} %get-tuple-element.53), channel_id=1, source_target_pairs={{0,16},{16,32},{32,48},{48,64},{64,80},{80,96},{96,112},{112,128},... | collective-permute-start | bytes 202760 | tf_op jit(solution)/shard_map/ppermute | solution.py:667
  86.5 14.1 %collective-permute-start.10 = (bf16[264,128]{1,0:T(8,128)(2,1)S(1)}, bf16[264,128]{1,0:T(8,128)(2,1)S(1)}, u32[]{:S(2)}, u32[]{:S(2)}) collective-permute-start(bf16[264,128]{1,0:T(8,128)(2,1)S(1)} %get-tuple-element.54), channel_id=1, source_target_pairs={{16,0},{32,16},{48,32},{64,48},{80,64},{96,80},{112,96},{128,112},... | collective-permute-start | bytes 202760 | tf_op jit(solution)/shard_map/ppermute | solution.py:668
  100.6 24.8 %all-to-all-start.2 = ((bf16[16,192,128]{2,1,0:T(8,128)(2,1)}), bf16[16,192,128]{2,1,0:T(8,128)(2,1)S(1)}, u32[]{:S(2)}, u32[]{:S(2)}) async-start(bf16[16,192,128]{2,1,0:T(8,128)(2,1)} %get-tuple-element.72), calls=%async_computation.2 | async-start | bytes 1572864 | tf_op jit(solution)/shard_map/all_to_all | solution.py:577
  106.2 12.2 %collective-permute-start.11 = (bf16[3,128,128]{2,1,0:T(8,128)(2,1)S(1)}, bf16[3,128,128]{2,1,0:T(8,128)(2,1)S(1)}, u32[]{:S(2)}, u32[]{:S(2)}) collective-permute-start(bf16[3,128,128]{2,1,0:T(8,128)(2,1)S(1)} %convert_element_type.24), channel_id=1, source_target_pairs={{64,0},{192,128},{65,1},{193,129},{66,2},{194,130},{67,3},{195,131... | collective-permute-start | bytes 294920 | tf_op jit(solution)/shard_map/ppermute | solution.py:687
  118.5 0.7 collective-permute-start.12

commit v8 on v7

--- a/solution.py
+++ b/solution.py
@@ -197,9 +197,9 @@
 
 
 def staged(tiles, scores, probs, lows, want="qkv"):
-    depth = 3
+    depth = 4
     held = {}
-    for step in range(len(tiles) + 2):
+    for step in range(len(tiles) + 3):
         if step < len(tiles):
             tile = tiles[step]()
             held[step] = tile
@@ -221,7 +221,7 @@
                 lows[low_view] = pt.astype(BF16)
             low_view = (n % depth, 1) + view[1:]
             lows[low_view] = (pt * (probs[view] - tile["delta"])).astype(BF16)
-        n = step - 2
+        n = step - 3
         if 0 <= n < len(tiles):
             tile = held.pop(n)
             shape = (tile["k"].shape[0], tile["q"].shape[0])
@@ -657,9 +657,9 @@
         + [
             dma((3,)),
             pltpu.VMEM((3, HD, HD), F32),
-            pltpu.VMEM((3, 256, 256), F32),
-            pltpu.VMEM((3, 256, 256), F32),
-            pltpu.VMEM((3, 2, 256, 256), BF16),
+            pltpu.VMEM((4, 256, 256), F32),
+            pltpu.VMEM((4, 256, 256), F32),
+            pltpu.VMEM((4, 2, 256, 256), BF16),
         ],
     )(pos, x, logsumexp, glob)
     glow, last, first = lax.optimization_barrier((glow, last, first))
@@ -668,9 +668,9 @@
     after = lax.ppermute(first, "seq", [(s + 1, s) for s in range(groups - 1)])
     y, gpart = lax.optimization_barrier((y, gpart))
     stage_space = [
-        pltpu.VMEM((3, HD, HD), F32),
-        pltpu.VMEM((3, HD, HD), F32),
-        pltpu.VMEM((3, 2, HD, HD), BF16),
+        pltpu.VMEM((4, HD, HD), F32),
+        pltpu.VMEM((4, HD, HD), F32),
+        pltpu.VMEM((4, 2, HD, HD), BF16),
     ]
     z, y = call(
         rand_query_body,

time: 160 us -> 159 us (level)
  no operation moved by 1% of the time
where the time goes in v8:
time: 159 us; the launch traced here: 158 us
  waiting for transfers between devices  54.9 us (35%)
  starting transfers between devices  45.8 us (29%)
  blocking collectives  29.6 us (19%)
  Pallas kernels  26 us (16%)
    all_to_all x3, waiting for transfers between devices, exchange(): return lax.all_to_all(x, axis, split_axis=0, concat_axis=0, tiled=True)  42.6 us
    all_to_all x1, blocking collectives, exchange(): return lax.all_to_all(x, axis, split_axis=0, concat_axis=0, tiled=True)  29.6 us
    all_to_all x3, starting transfers between devices, exchange(): return lax.all_to_all(x, axis, split_axis=0, concat_axis=0, tiled=True)  19.3 us
    ppermute x6, waiting for transfers between devices, spread(): lax.ppermute(source, 'seq', [(s, s + n * reach) for s in starts])  11.1 us
    ppermute x6, starting transfers between devices, spread(): lax.ppermute(source, 'seq', [(s, s + n * reach) for s in starts])  9.49 us
    ppermute x1, starting transfers between devices, per_device(): after = lax.ppermute(first, 'seq', [(s + 1, s) for s in range(groups - 1)])  5.93 us
    pallas_call x1, Pallas kernels, per_device(): call(rand_key_body, (far_acc, far_acc), [SM, VM, HB], (HB,) * 2, flops=1...  5.32 us
    ppermute x1, starting transfers between devices, per_device(): before = lax.ppermute(last, 'seq', [(s, s + 1) for s in range(groups - 1)])  4.55 us
  transfers between devices with their start and end apart: 16, of which 7 were waited for; matrix products, arithmetic and copies ran while one was open for 0% of the time, Pallas kernels for 13%

profile of v8, /device:TPU:32, one launch (start us, length us, event | category | flops | bytes accessed | tf_op | source)
XLA Modules:
  0.0 157.7 jit_solution(2916567355160711764)
XLA Ops:
  0.6 2.5 %shard_map.95 = bf16[16,264,128]{2,1,0:T(8,128)(2,1)} custom-call(bf16[64,2048]{1,0:T(8,128)(2,1)} %q.1, bf16[64,2048]{1,0:T(8,128)(2,1)} %k.1, bf16[64,2048]{1,0:T(8,128)(2,1)} %v.1, bf16[64,2048]{1,0:T(8,128)(2,1)} %o.1, bf16[64,2048]{1,0:T(8,128)(2,1)} %g.1), custom_call_target="tpu_custom_call" | custom-call | bytes 1310720 | tf_op jit(solution)/shard_map/pallas_call | solution.py:587
  3.2 0.0 copy-start
  3.2 0.0 copy-start.1
  3.2 10.1 %all-to-all-start = ((bf16[16,264,128]{2,1,0:T(8,128)(2,1)}), bf16[16,264,128]{2,1,0:T(8,128)(2,1)S(1)}, u32[]{:S(2)}, u32[]{:S(2)}) async-start(bf16[16,264,128]{2,1,0:T(8,128)(2,1)} %shard_map.95), calls=%async_computation | async-start | bytes 2162688 | tf_op jit(solution)/shard_map/all_to_all | solution.py:577
  13.3 32.3 %all-to-all-done.x = bf16[16,264,128]{2,1,0:T(8,128)(2,1)S(1)} async-done(((bf16[16,264,128]{2,1,0:T(8,128)(2,1)}), bf16[16,264,128]{2,1,0:T(8,128)(2,1)S(1)}, u32[]{:S(2)}, u32[]{:S(2)}) %all-to-all-start) | async-done | bytes 1081376 | tf_op jit(solution)/shard_map/all_to_all | solution.py:577
  45.7 0.1 shard_map.96
  45.7 0.7 collective-permute-start.2
  46.4 0.7 collective-permute-start.1
  47.1 1.3 collective-permute-start
  48.4 0.1 copy.12
  48.5 0.1 reshape.13.entries
  48.7 0.2 shard_map.94.table
  48.9 2.2 %shard_map.97 = bf16[16,392,128]{2,1,0:T(8,128)(2,1)} custom-call(s32[1]{0:T(128)} %bitcast.pos, s32[32,128]{1,0:T(8,128)S(1)} %shard_map.94.table, bf16[16,264,128]{2,1,0:T(8,128)(2,1)S(1)} %all-to-all-done.x, f32[1,1024]{1,0:T(1,128)S(1)} %copy-done), custom_call_target="tpu_custom_call" | custom-call | bytes 3145728 | tf_op jit(solution)/shard_map/pallas_call | solution.py:606
  51.1 0.0 collective-permute-done.2
  51.1 0.0 collective-permute-done.1
  51.2 5.7 %collective-permute-done = bf16[2,264,128]{2,1,0:T(8,128)(2,1)S(1)} collective-permute-done((bf16[2,264,128]{2,1,0:T(8,128)(2,1)S(1)}, bf16[2,264,128]{2,1,0:T(8,128)(2,1)S(1)}, u32[]{:S(2)}, u32[]{:S(2)}) %collective-permute-start) | collective-permute-done | bytes 135200 | tf_op jit(solution)/shard_map/ppermute | solution.py:622
  56.9 3.6 %all-to-all-start.1 = ((bf16[16,392,128]{2,1,0:T(8,128)(2,1)}), bf16[16,392,128]{2,1,0:T(8,128)(2,1)S(1)}, u32[]{:S(2)}, u32[]{:S(2)}) async-start(bf16[16,392,128]{2,1,0:T(8,128)(2,1)} %shard_map.97), calls=%async_computation.1 | async-start | bytes 3211264 | tf_op jit(solution)/shard_map/all_to_all | solution.py:577
  60.5 4.3 %collective-permute-start.5 = (bf16[2,264,128]{2,1,0:T(8,128)(2,1)S(1)}, bf16[2,264,128]{2,1,0:T(8,128)(2,1)S(1)}, u32[]{:S(2)}, u32[]{:S(2)}) collective-permute-start(bf16[2,264,128]{2,1,0:T(8,128)(2,1)S(1)} %add_add_fusion.1), channel_id=1, source_target_pairs={{0,48},{64,112},{128,176},{192,240},{1,49},{65,113},{129,177},{193... | collective-permute-start | bytes 405512 | tf_op jit(solution)/shard_map/ppermute | solution.py:622
  64.8 1.3 collective-permute-start.4
  66.1 1.3 collective-permute-start.3
  67.4 2.9 %shard_map.98 = (f32[1024,128]{1,0:T(8,128)}, f32[1024,128]{1,0:T(8,128)}, f32[1024,128]{1,0:T(8,128)}) custom-call(s32[1]{0:T(128)} %bitcast.pos, bf16[16,264,128]{2,1,0:T(8,128)(2,1)S(1)} %all-to-all-done.x, f32[1,1024]{1,0:T(1,128)S(1)} %copy-done), custom_call_target="tpu_custom_call" | custom-call | flops 536870912 | bytes 2097152 | tf_op jit(solution)/shard_map/pallas_call | solution.py:639
  70.3 0.0 collective-permute-done.5
  70.3 2.6 %collective-permute-done.4 = bf16[2,264,128]{2,1,0:T(8,128)(2,1)S(1)} collective-permute-done((bf16[2,264,128]{2,1,0:T(8,128)(2,1)S(1)}, bf16[2,264,128]{2,1,0:T(8,128)(2,1)S(1)}, u32[]{:S(2)}, u32[]{:S(2)}) %collective-permute-start.4) | collective-permute-done | bytes 135200 | tf_op jit(solution)/shard_map/ppermute | solution.py:622
  73.0 2.7 %collective-permute-done.3 = bf16[2,264,128]{2,1,0:T(8,128)(2,1)S(1)} collective-permute-done((bf16[2,264,128]{2,1,0:T(8,128)(2,1)S(1)}, bf16[2,264,128]{2,1,0:T(8,128)(2,1)S(1)}, u32[]{:S(2)}, u32[]{:S(2)}) %collective-permute-start.3) | collective-permute-done | bytes 135200 | tf_op jit(solution)/shard_map/ppermute | solution.py:622
  75.7 2.2 %shard_map.99 = (f32[1024,128]{1,0:T(8,128)}, f32[1024,128]{1,0:T(8,128)}, f32[1024,128]{1,0:T(8,128)}, f32[3,128,128]{2,1,0:T(8,128)S(1)}, bf16[3,128,128]{2,1,0:T(8,128)(2,1)S(1)}) custom-call(s32[1]{0:T(128)} %bitcast.pos, bf16[16,264,128]{2,1,0:T(8,128)(2,1)S(1)} %all-to-all-done.x, f32[1,1024]{1,0:T(1,128)S(1)} %copy-done, ...), custom_call_target="tpu_custom_call" | custom-call | flops 536870912 | bytes 4194304 | tf_op jit(solution)/shard_map/pallas_call | solution.py:649
  77.9 1.3 collective-permute-start.8
  79.2 1.3 collective-permute-start.7
  80.5 1.3 collective-permute-start.6
  81.8 4.6 %collective-permute-start.9 = (bf16[264,128]{1,0:T(8,128)(2,1)S(1)}, bf16[264,128]{1,0:T(8,128)(2,1)S(1)}, u32[]{:S(2)}, u32[]{:S(2)}) collective-permute-start(bf16[264,128]{1,0:T(8,128)(2,1)S(1)} %get-tuple-element.53), channel_id=1, source_target_pairs={{0,16},{16,32},{32,48},{48,64},{64,80},{80,96},{96,112},{112,128},... | collective-permute-start | bytes 202760 | tf_op jit(solution)/shard_map/ppermute | solution.py:667
  86.4 5.9 %collective-permute-start.10 = (bf16[264,128]{1,0:T(8,128)(2,1)S(1)}, bf16[264,128]{1,0:T(8,128)(2,1)S(1)}, u32[]{:S(2)}, u32[]{:S(2)}) collective-permute-start(bf16[264,128]{1,0:T(8,128)(2,1)S(1)} %get-tuple-element.54), channel_id=1, source_target_pairs={{16,0},{32,16},{48,32},{64,48},{80,64},{96,80},{112,96},{128,112},... | collective-permute-start | bytes 202760 | tf_op jit(solution)/shard_map/ppermute | solution.py:668
  92.3 0.0 collective-permute-done.8
  92.3 0.0 collective-permute-done.7
  92.3 0.0 collective-permute-done.6
  92.4 4.1 %all-to-all-done.1.y = bf16[16,392,128]{2,1,0:T(8,128)(2,1)S(1)} async-done(((bf16[16,392,128]{2,1,0:T(8,128)(2,1)}), bf16[16,392,128]{2,1,0:T(8,128)(2,1)S(1)}, u32[]{:S(2)}, u32[]{:S(2)}) %all-to-all-start.1) | async-done | bytes 1605664 | tf_op jit(solution)/shard_map/all_to_all | solution.py:577
  96.5 3.8 %shard_map.100 = (bf16[16,192,128]{2,1,0:T(8,128)(2,1)}, bf16[16,392,128]{2,1,0:T(8,128)(2,1)}) custom-call(s32[32,128]{1,0:T(8,128)S(1)} %shard_map.94.table, bf16[16,264,128]{2,1,0:T(8,128)(2,1)S(1)} %all-to-all-done.x, bf16[16,392,128]{2,1,0:T(8,128)(2,1)S(1)} %all-to-all-done.1.y), custom_call_target="tpu_custom_call" | custom-call | flops 536870912 | bytes 4194304 | tf_op jit(solution)/shard_map/pallas_call | solution.py:675
  100.3 0.0 collective-permute-done.9.before
  100.4 0.0 collective-permute-done.10.after
  100.4 5.5 %all-to-all-start.2 = ((bf16[16,192,128]{2,1,0:T(8,128)(2,1)}), bf16[16,192,128]{2,1,0:T(8,128)(2,1)S(1)}, u32[]{:S(2)}, u32[]{:S(2)}) async-start(bf16[16,192,128]{2,1,0:T(8,128)(2,1)} %get-tuple-element.72), calls=%async_computation.2 | async-start | bytes 1572864 | tf_op jit(solution)/shard_map/all_to_all | solution.py:577
  105.9 2.0 %collective-permute-start.11 = (bf16[3,128,128]{2,1,0:T(8,128)(2,1)S(1)}, bf16[3,128,128]{2,1,0:T(8,128)(2,1)S(1)}, u32[]{:S(2)}, u32[]{:S(2)}) collective-permute-start(bf16[3,128,128]{2,1,0:T(8,128)(2,1)S(1)} %convert_element_type.24), channel_id=1, source_target_pairs={{64,0},{192,128},{65,1},{193,129},{66,2},{194,130},{67,3},{195,131... | collective-permute-start | bytes 294920 | tf_op jit(solution)/shard_map/ppermute | solution.py:687
  107.9 5.3 %shard_map.101 = (f32[1024,128]{1,0:T(8,128)}, f32[1024,128]{1,0:T(8,128)}) custom-call(s32[32,128]{1,0:T(8,128)S(1)} %shard_map.94.table, bf16[16,264,128]{2,1,0:T(8,128)(2,1)S(1)} %all-to-all-done.x, bf16[16,392,128]{2,1,0:T(8,128)(2,1)} %get-tuple-element.64.y_far), custom_call_target="tpu_custom_call" | custom-call | flops 536870912 | bytes 4194304 | tf_op jit(solution)/shard_map/pallas_call | solution.py:689
  113.3 3.7 %shard_map.102 = (bf16[16,192,128]{2,1,0:T(8,128)(2,1)}, f32[1024,128]{1,0:T(8,128)S(1)}, f32[256,128]{1,0:T(8,128)S(1)}) custom-call(s32[1]{0:T(128)} %bitcast.pos, bf16[16,264,128]{2,1,0:T(8,128)(2,1)S(1)} %all-to-all-done.x, f32[1,1024]{1,0:T(1,128)S(1)} %copy-done, bf16[264,128]{1,0:T(8,128)(2,1)S(1)} %collective-permute-done.9.before, ...), custom_call_target="tpu_custom_call" | custom-call | flops 16777216 | bytes 4194304 | tf_op jit(solution)/shard_map/pallas_call | solution.py:699
  117.0 1.2 collective-permute-done.11
  118.2 0.7 collective-permute-start.12
  118.9 0.0 collective-permute-done.12
  118.9 6.2 %all-to-all-done.2.z = bf16[16,192,128]{2,1,0:T(8,128)(2,1)S(1)} async-done(((bf16[16,192,128]{2,1,0:T(8,128)(2,1)}), bf16[16,192,128]{2,1,0:T(8,128)(2,1)S(1)}, u32[]{:S(2)}, u32[]{:S(2)}) %all-to-all-start.2) | async-done | bytes 786464 | tf_op jit(solution)/shard_map/all_to_all | solution.py:577
  125.1 2.0 %shard_map.103 = bf16[16,192,128]{2,1,0:T(8,128)(2,1)} custom-call(s32[1]{0:T(128)} %bitcast.pos, s32[32,128]{1,0:T(8,128)S(1)} %shard_map.94.table, f32[1024,128]{1,0:T(8,128)S(1)} %get-tuple-element.70.dq, f32[256,128]{1,0:T(8,128)S(1)} %get-tuple-element.71.edge, bf16[16,192,128]{2,1,0:T(8,128)(2,1)S(1)} %all-to-all-done.2.z, ...), custom_call_target="tpu_custom_call", output_to_operand_aliasing={{}: (6, {})} | custom-call | bytes 4194304 | tf_op jit(solution)/shard_map/pallas_call | solution.py:718
  127.1 29.6 %all_to_all.20.w = bf16[16,192,128]{2,1,0:T(8,128)(2,1)S(1)} all-to-all(bf16[16,192,128]{2,1,0:T(8,128)(2,1)} %shard_map.103), channel_id=1, replica_groups=mesh['seq'=16,'head'=16] {'head'}, dimensions={0} | all-to-all | bytes 1572864 | tf_op jit(solution)/shard_map/all_to_all | solution.py:577
  156.7 1.1 shard_map.104
  (9 shorter events, 0.2 us)
Async XLA Ops:
  3.2 42.5 %copy-start = (f32[1,1024]{1,0:T(1,128)S(1)}, f32[1,1024]{1,0:T(1,128)}, u32[]{:S(2)}) copy-start(f32[1,1024]{1,0:T(1,128)} %lse.9) | copy-start | bytes 12292
  3.2 45.2 %copy-start.1 = (s32[256,3]{0,1:T(4,128)S(1)}, s32[256,3]{0,1:T(4,128)}, u32[]{:S(2)}) copy-start(s32[256,3]{0,1:T(4,128)} %param.13) | copy-start | bytes 9220
  3.2 42.5 %all-to-all-start = ((bf16[16,264,128]{2,1,0:T(8,128)(2,1)}), bf16[16,264,128]{2,1,0:T(8,128)(2,1)S(1)}, u32[]{:S(2)}, u32[]{:S(2)}) async-start(bf16[16,264,128]{2,1,0:T(8,128)(2,1)} %shard_map.95), calls=%async_computation | async-start | bytes 2162688 | tf_op jit(solution)/shard_map/all_to_all | solution.py:577
  45.7 5.4 %collective-permute-start.2 = (bf16[2,264,128]{2,1,0:T(8,128)(2,1)S(1)}, bf16[2,264,128]{2,1,0:T(8,128)(2,1)S(1)}, u32[]{:S(2)}, u32[]{:S(2)}) collective-permute-start(bf16[2,264,128]{2,1,0:T(8,128)(2,1)S(1)} %get-tuple-element.39), channel_id=1, source_target_pairs={{0,192},{1,193},{2,194},{3,195},{4,196},{5,197},{6,198},{7,199},{8... | collective-permute-start | bytes 405512 | tf_op jit(solution)/shard_map/ppermute | solution.py:622
  46.4 4.7 %collective-permute-start.1 = (bf16[2,264,128]{2,1,0:T(8,128)(2,1)S(1)}, bf16[2,264,128]{2,1,0:T(8,128)(2,1)S(1)}, u32[]{:S(2)}, u32[]{:S(2)}) collective-permute-start(bf16[2,264,128]{2,1,0:T(8,128)(2,1)S(1)} %get-tuple-element.39), channel_id=1, source_target_pairs={{0,128},{1,129},{2,130},{3,131},{4,132},{5,133},{6,134},{7,135},{8... | collective-permute-start | bytes 405512 | tf_op jit(solution)/shard_map/ppermute | solution.py:622
  47.1 9.8 %collective-permute-start = (bf16[2,264,128]{2,1,0:T(8,128)(2,1)S(1)}, bf16[2,264,128]{2,1,0:T(8,128)(2,1)S(1)}, u32[]{:S(2)}, u32[]{:S(2)}) collective-permute-start(bf16[2,264,128]{2,1,0:T(8,128)(2,1)S(1)} %get-tuple-element.39), channel_id=1, source_target_pairs={{0,64},{1,65},{2,66},{3,67},{4,68},{5,69},{6,70},{7,71},{8,72},{9,... | collective-permute-start | bytes 405512 | tf_op jit(solution)/shard_map/ppermute | solution.py:622
  56.9 39.6 %all-to-all-start.1 = ((bf16[16,392,128]{2,1,0:T(8,128)(2,1)}), bf16[16,392,128]{2,1,0:T(8,128)(2,1)S(1)}, u32[]{:S(2)}, u32[]{:S(2)}) async-start(bf16[16,392,128]{2,1,0:T(8,128)(2,1)} %shard_map.97), calls=%async_computation.1 | async-start | bytes 3211264 | tf_op jit(solution)/shard_map/all_to_all | solution.py:577
  60.5 9.8 %collective-permute-start.5 = (bf16[2,264,128]{2,1,0:T(8,128)(2,1)S(1)}, bf16[2,264,128]{2,1,0:T(8,128)(2,1)S(1)}, u32[]{:S(2)}, u32[]{:S(2)}) collective-permute-start(bf16[2,264,128]{2,1,0:T(8,128)(2,1)S(1)} %add_add_fusion.1), channel_id=1, source_target_pairs={{0,48},{64,112},{128,176},{192,240},{1,49},{65,113},{129,177},{193... | collective-permute-start | bytes 405512 | tf_op jit(solution)/shard_map/ppermute | solution.py:622
  64.8 8.2 %collective-permute-start.4 = (bf16[2,264,128]{2,1,0:T(8,128)(2,1)S(1)}, bf16[2,264,128]{2,1,0:T(8,128)(2,1)S(1)}, u32[]{:S(2)}, u32[]{:S(2)}) collective-permute-start(bf16[2,264,128]{2,1,0:T(8,128)(2,1)S(1)} %add_add_fusion.1), channel_id=1, source_target_pairs={{0,32},{64,96},{128,160},{192,224},{1,33},{65,97},{129,161},{193,2... | collective-permute-start | bytes 405512 | tf_op jit(solution)/shard_map/ppermute | solution.py:622
  66.1 9.6 %collective-permute-start.3 = (bf16[2,264,128]{2,1,0:T(8,128)(2,1)S(1)}, bf16[2,264,128]{2,1,0:T(8,128)(2,1)S(1)}, u32[]{:S(2)}, u32[]{:S(2)}) collective-permute-start(bf16[2,264,128]{2,1,0:T(8,128)(2,1)S(1)} %add_add_fusion.1), channel_id=1, source_target_pairs={{0,16},{64,80},{128,144},{192,208},{1,17},{65,81},{129,145},{193,2... | collective-permute-start | bytes 405512 | tf_op jit(solution)/shard_map/ppermute | solution.py:622
  77.9 14.4 %collective-permute-start.8 = (bf16[3,128,128]{2,1,0:T(8,128)(2,1)S(1)}, bf16[3,128,128]{2,1,0:T(8,128)(2,1)S(1)}, u32[]{:S(2)}, u32[]{:S(2)}) collective-permute-start(bf16[3,128,128]{2,1,0:T(8,128)(2,1)S(1)} %get-tuple-element.48), channel_id=1, source_target_pairs={{48,0},{112,64},{176,128},{240,192},{49,1},{113,65},{177,129},{241... | collective-permute-start | bytes 294920 | tf_op jit(solution)/shard_map/ppermute | solution.py:627
  79.2 13.1 %collective-permute-start.7 = (bf16[3,128,128]{2,1,0:T(8,128)(2,1)S(1)}, bf16[3,128,128]{2,1,0:T(8,128)(2,1)S(1)}, u32[]{:S(2)}, u32[]{:S(2)}) collective-permute-start(bf16[3,128,128]{2,1,0:T(8,128)(2,1)S(1)} %get-tuple-element.48), channel_id=1, source_target_pairs={{32,0},{96,64},{160,128},{224,192},{33,1},{97,65},{161,129},{225,1... | collective-permute-start | bytes 294920 | tf_op jit(solution)/shard_map/ppermute | solution.py:627
  80.5 11.8 %collective-permute-start.6 = (bf16[3,128,128]{2,1,0:T(8,128)(2,1)S(1)}, bf16[3,128,128]{2,1,0:T(8,128)(2,1)S(1)}, u32[]{:S(2)}, u32[]{:S(2)}) collective-permute-start(bf16[3,128,128]{2,1,0:T(8,128)(2,1)S(1)} %get-tuple-element.48), channel_id=1, source_target_pairs={{16,0},{80,64},{144,128},{208,192},{17,1},{81,65},{145,129},{209,1... | collective-permute-start | bytes 294920 | tf_op jit(solution)/shard_map/ppermute | solution.py:627
  81.8 18.5 %collective-permute-start.9 = (bf16[264,128]{1,0:T(8,128)(2,1)S(1)}, bf16[264,128]{1,0:T(8,128)(2,1)S(1)}, u32[]{:S(2)}, u32[]{:S(2)}) collective-permute-start(bf16[264,128]{1,0:T(8,128)(2,1)S(1)} %get-tuple-element.53), channel_id=1, source_target_pairs={{0,16},{16,32},{32,48},{48,64},{64,80},{80,96},{96,112},{112,128},... | collective-permute-start | bytes 202760 | tf_op jit(solution)/shard_map/ppermute | solution.py:667
  86.4 14.0 %collective-permute-start.10 = (bf16[264,128]{1,0:T(8,128)(2,1)S(1)}, bf16[264,128]{1,0:T(8,128)(2,1)S(1)}, u32[]{:S(2)}, u32[]{:S(2)}) collective-permute-start(bf16[264,128]{1,0:T(8,128)(2,1)S(1)} %get-tuple-element.54), channel_id=1, source_target_pairs={{16,0},{32,16},{48,32},{64,48},{80,64},{96,80},{112,96},{128,112},... | collective-permute-start | bytes 202760 | tf_op jit(solution)/shard_map/ppermute | solution.py:668
  100.4 24.8 %all-to-all-start.2 = ((bf16[16,192,128]{2,1,0:T(8,128)(2,1)}), bf16[16,192,128]{2,1,0:T(8,128)(2,1)S(1)}, u32[]{:S(2)}, u32[]{:S(2)}) async-start(bf16[16,192,128]{2,1,0:T(8,128)(2,1)} %get-tuple-element.72), calls=%async_computation.2 | async-start | bytes 1572864 | tf_op jit(solution)/shard_map/all_to_all | solution.py:577
  105.9 12.2 %collective-permute-start.11 = (bf16[3,128,128]{2,1,0:T(8,128)(2,1)S(1)}, bf16[3,128,128]{2,1,0:T(8,128)(2,1)S(1)}, u32[]{:S(2)}, u32[]{:S(2)}) collective-permute-start(bf16[3,128,128]{2,1,0:T(8,128)(2,1)S(1)} %convert_element_type.24), channel_id=1, source_target_pairs={{64,0},{192,128},{65,1},{193,129},{66,2},{194,130},{67,3},{195,131... | collective-permute-start | bytes 294920 | tf_op jit(solution)/shard_map/ppermute | solution.py:687
  118.2 0.7 collective-permute-start.12
